TPU v7x, 32 devices: a whole 2x2x4 slice. The times are simulated.
32 devices in a mesh: ctx: 16 (over z, y, x), wsh: 2 (over core).
Axes of the slice: x: 2, y: 2, z: 4, core: 2. Of those that a mesh axis runs over, the one named last changes fastest.
Arguments:
- tokens: bfloat16 [4, 4096, 768], P('wsh', 'ctx'), may hold values from -6 to 6
- cont_lengths: int32 [4, 8], P('wsh'), may hold values from 1 to 512, 2048 in all within a row
- grad_out: bfloat16 [4, 4096, 768], P('wsh', 'ctx'), may hold values from -6 to 6
- ln_gain_one: bfloat16 [768], P('wsh'), may hold values from 0.099609375 to 1.8984375
- ln_bias_one: bfloat16 [768], P('wsh'), may hold values from -1.25 to 1.25
- w_query: bfloat16 [768, 768], P('wsh'), may hold values from -0.21875 to 0.21875
- b_query: bfloat16 [768], P('wsh'), may hold values from -3 to 3
- w_key: bfloat16 [768, 768], P('wsh'), may hold values from -0.21875 to 0.21875
- w_value: bfloat16 [768, 768], P('wsh'), may hold values from -0.21875 to 0.21875
- b_value: bfloat16 [768], P('wsh'), may hold values from -0.625 to 0.625
- w_out: bfloat16 [768, 768], P('wsh'), may hold values from -1.25 to 1.25
- b_out: bfloat16 [768], P('wsh'), may hold values from -0.625 to 0.625
- ln_gain_two: bfloat16 [768], P('wsh'), may hold values from 0.099609375 to 1.8984375
- ln_bias_two: bfloat16 [768], P('wsh'), may hold values from -1.25 to 1.25
- w_in: bfloat16 [768, 3072], P('wsh'), may hold values from -0.21875 to 0.21875
- b_in: bfloat16 [3072], P('wsh'), may hold values from -3 to 3
- w_back: bfloat16 [3072, 768], P('wsh'), may hold values from -0.109375 to 0.109375
- b_back: bfloat16 [768], P('wsh'), may hold values from -0.625 to 0.625
Outputs:
- out_tokens: bfloat16 [4, 4096, 768], P('wsh', 'ctx')
- grad_tokens: float32 [4, 4096, 768], P('wsh', 'ctx')
- grad_ln_gain_one: float32 [768], P('wsh')
- grad_ln_bias_one: float32 [768], P('wsh')
- grad_w_query: float32 [768, 768], P('wsh')
- grad_b_query: float32 [768], P('wsh')
- grad_w_key: float32 [768, 768], P('wsh')
- grad_w_value: float32 [768, 768], P('wsh')
- grad_b_value: float32 [768], P('wsh')
- grad_w_out: float32 [768, 768], P('wsh')
- grad_b_out: float32 [768], P('wsh')
- grad_ln_gain_two: float32 [768], P('wsh')
- grad_ln_bias_two: float32 [768], P('wsh')
- grad_w_in: float32 [768, 3072], P('wsh')
- grad_b_in: float32 [3072], P('wsh')
- grad_w_back: float32 [3072, 768], P('wsh')
- grad_b_back: float32 [768], P('wsh')
Inputs may be any that keep to these rules, and one draw needn't show every extreme that they name: `cont_lengths`: each row holds 8 continuation lengths that sum to 2048; the largest of each row is 512.
All inputs are finite; a program needn't handle non-finite values.
Results may differ from a plain program's by a relative error of at most 0.02.
Values may be sent and summed in bfloat16 or wider, within the bound.
No kernel may reach another device: no remote copies, remote signals or barrier semaphores. Data moves between devices by JAX's collectives and lax.ppermute only.
A program may use at most 256 MiB of HBM per device.

v0:
```python
import jax
import jax.numpy as jnp
from jax import lax
from jax.sharding import PartitionSpec as P

HEADS = 12
HEAD = 64
PROMPT = 2048
MICRO = 2


EPSILON = 1e-12
NEGATIVE = -1e30


def shortened(x):

    def short(part):
        return part.astype(jnp.bfloat16) if part.dtype == jnp.float32 else part

    return jax.tree.map(short, x)


def dot_plain(left_side, right_side):
    return jnp.dot(left_side, right_side, preferred_element_type=jnp.float32)


def dot_inner(left_side, right_side):
    return lax.dot_general(
        left_side, right_side, (((0,), (0,)), ((), ())), preferred_element_type=jnp.float32
    )


def dot_transposed(left_side, right_side):
    return lax.dot_general(
        left_side, right_side, (((1,), (1,)), ((), ())), preferred_element_type=jnp.float32
    )


def exact_gelu(values):
    return jax.nn.gelu(values, approximate=False)


def dealt_position(stored, stripe, n_ctx):
    block = stored // stripe
    within = stored % stripe
    device = block // 2
    return jnp.where(block % 2 == 0, device, 2 * n_ctx - 1 - device) * stripe + within


def norm_forward(values, gain_vec, bias_vec):
    center = values - jnp.mean(values, axis=-1, keepdims=True)
    scaled = lax.rsqrt(jnp.mean(center * center, axis=-1, keepdims=True) + EPSILON)
    normed = center * scaled
    return (normed * gain_vec + bias_vec, normed, scaled)


def norm_backward(upstream, normed, scaled, gain_vec):
    inner_grad = upstream * gain_vec
    result = scaled * (
        inner_grad
        - jnp.mean(inner_grad, axis=-1, keepdims=True)
        - normed * jnp.mean(inner_grad * normed, axis=-1, keepdims=True)
    )
    return (result, jnp.sum(upstream * normed, axis=0), jnp.sum(upstream, axis=0))


def segment_of(positions, seg_ends):
    beyond = (positions - PROMPT)[None, :, None] >= seg_ends[:, None, :]
    count_past = jnp.sum(beyond.astype(jnp.int32), axis=2, dtype=jnp.int32)
    return jnp.where(positions[None, :] >= PROMPT, count_past, -1)


def visible(query_pos, query_seg, key_pos, key_seg):
    causal = key_pos[None, None, :] <= query_pos[None, :, None]
    shared = (key_pos < PROMPT)[None, None, :] | (key_seg[:, None, :] == query_seg[:, :, None])
    return causal & shared


def attend_block(carried, pieces, context_info):
    queries, query_pos, query_seg, seg_ends, layout = context_info
    key_part, value_part = pieces
    groups, amount = (key_part.shape[0], key_part.shape[1])
    key_pos = dealt_position(jnp.arange(amount, dtype=jnp.int32), layout[0], layout[1])
    allowed = visible(query_pos, query_seg, key_pos, segment_of(key_pos, seg_ends))

    def attend_compute(current):
        running, totals, weighted = current
        keys_heads = key_part.reshape(groups, amount, HEADS, HEAD)
        values_heads = value_part.reshape(groups, amount, HEADS, HEAD)
        scores = jnp.einsum(
            "grhe,gnhe->ghrn", queries, keys_heads, preferred_element_type=jnp.float32
        ) * HEAD ** (-0.5)
        scores = jnp.where(allowed[:, None], scores, NEGATIVE)
        highest = jnp.maximum(running, jnp.max(scores, axis=-1))
        soft = jnp.where(allowed[:, None], jnp.exp(scores - highest[..., None]), 0.0)
        totals = jnp.sum(soft, axis=-1)
        weighted = jnp.einsum(
            "ghrn,gnhe->ghre",
            soft.astype(jnp.bfloat16),
            values_heads,
            preferred_element_type=jnp.float32,
        )
        return (highest, totals, weighted)

    def attend_skipped(current):
        return current

    return lax.cond(jnp.any(allowed), attend_compute, attend_skipped, carried)


def back_block(pieces, context_info, grad_info):
    queries, query_pos, query_seg, seg_ends, layout = context_info
    grad_heads, logsum, row_delta = grad_info
    key_part, value_part = pieces
    groups, amount = (key_part.shape[0], key_part.shape[1])
    row_count = queries.shape[1]
    key_pos = dealt_position(jnp.arange(amount, dtype=jnp.int32), layout[0], layout[1])
    allowed = visible(query_pos, query_seg, key_pos, segment_of(key_pos, seg_ends))
    score_scale = HEAD ** (-0.5)

    def back_compute(unused):
        keys_heads = key_part.reshape(groups, amount, HEADS, HEAD)
        values_heads = value_part.reshape(groups, amount, HEADS, HEAD)
        scores = (
            jnp.einsum("grhe,gnhe->ghrn", queries, keys_heads, preferred_element_type=jnp.float32)
            * score_scale
        )
        soft = jnp.where(allowed[:, None], jnp.exp(scores - logsum[..., None]), 0.0)
        grad_soft = jnp.einsum(
            "grhe,gnhe->ghrn", grad_heads, values_heads, preferred_element_type=jnp.float32
        )
        grad_scores = (soft * (grad_soft - row_delta[..., None])).astype(jnp.bfloat16)
        query_grad = None
        pair_grad = None
        query_grad = (
            jnp.einsum(
                "ghrn,gnhe->ghre", grad_scores, keys_heads, preferred_element_type=jnp.float32
            )
            * score_scale
        )
        key_grad = (
            jnp.einsum("ghrn,grhe->gnhe", grad_scores, queries, preferred_element_type=jnp.float32)
            * score_scale
        )
        value_grad = jnp.einsum(
            "ghrn,grhe->gnhe",
            soft.astype(jnp.bfloat16),
            grad_heads,
            preferred_element_type=jnp.float32,
        )
        pair_grad = jnp.concatenate(
            [
                key_grad.reshape(groups, amount, HEADS * HEAD),
                value_grad.reshape(groups, amount, HEADS * HEAD),
            ],
            axis=-1,
        )
        return (query_grad, pair_grad)

    def back_skipped(unused):
        query_grad = jnp.zeros((groups, HEADS, row_count, HEAD), jnp.float32)
        pair_grad = jnp.zeros((groups, amount, 2 * HEADS * HEAD), jnp.float32)
        return (query_grad, pair_grad)

    return lax.cond(jnp.any(allowed), back_compute, back_skipped, 0)


def back_fold(pieces, context_info, grad_info):
    query_add, pair_grad = back_block(pieces, context_info, grad_info)
    return (query_add, pair_grad)


def add_tuples(first_terms, second_terms):
    if first_terms is None:
        return second_terms
    return tuple(
        (first_term + second_term for first_term, second_term in zip(first_terms, second_terms))
    )


def body(
    tokens,
    cont_lengths,
    grad_out,
    ln_gain_one,
    ln_bias_one,
    w_query,
    b_query,
    w_key,
    w_value,
    b_value,
    w_out,
    b_out,
    ln_gain_two,
    ln_bias_two,
    w_in,
    b_in,
    w_back,
    b_back,
):
    shards = (
        ln_gain_one,
        ln_bias_one,
        w_query,
        b_query,
        w_key,
        w_value,
        b_value,
        w_out,
        b_out,
        ln_gain_two,
        ln_bias_two,
        w_in,
        b_in,
        w_back,
        b_back,
    )
    params = (
        lax.all_gather(shards[0], "wsh", axis=0, tiled=True),
        lax.all_gather(shards[1], "wsh", axis=0, tiled=True),
        lax.all_gather(shards[2], "wsh", axis=0, tiled=True),
        lax.all_gather(shards[3], "wsh", axis=0, tiled=True),
        lax.all_gather(shards[4], "wsh", axis=0, tiled=True),
        lax.all_gather(shards[5], "wsh", axis=0, tiled=True),
        lax.all_gather(shards[6], "wsh", axis=0, tiled=True),
        lax.all_gather(shards[7], "wsh", axis=0, tiled=True),
        lax.all_gather(shards[8], "wsh", axis=0, tiled=True),
        lax.all_gather(shards[9], "wsh", axis=0, tiled=True),
        lax.all_gather(shards[10], "wsh", axis=0, tiled=True),
        lax.all_gather(shards[11], "wsh", axis=0, tiled=True),
        lax.all_gather(shards[12], "wsh", axis=0, tiled=True),
        lax.all_gather(shards[13], "wsh", axis=0, tiled=True),
        lax.all_gather(shards[14], "wsh", axis=0, tiled=True),
    )
    (
        gain_one,
        bias_one,
        query_w,
        query_b,
        key_w,
        value_w,
        value_b,
        out_w,
        out_b,
        gain_two,
        bias_two,
        in_w,
        in_b,
        back_w,
        back_b,
    ) = params
    gain_one = gain_one.astype(jnp.float32)
    bias_one = bias_one.astype(jnp.float32)
    query_b = query_b.astype(jnp.float32)
    value_b = value_b.astype(jnp.float32)
    out_b = out_b.astype(jnp.float32)
    gain_two = gain_two.astype(jnp.float32)
    bias_two = bias_two.astype(jnp.float32)
    in_b = in_b.astype(jnp.float32)
    back_b = back_b.astype(jnp.float32)
    local_groups, row_count, model_width = tokens.shape
    groups = local_groups // MICRO
    n_ctx = lax.axis_size("ctx")
    layout = (row_count // 2, n_ctx)
    own_start = lax.axis_index("ctx") * row_count
    query_pos = dealt_position(
        own_start + jnp.arange(row_count, dtype=jnp.int32), layout[0], layout[1]
    )
    outputs = []
    grad_outputs = []
    pending = None
    reduced = None
    for micro_index in range(MICRO):
        first_group = micro_index * groups
        inputs = (
            tokens[first_group : first_group + groups]
            .reshape(groups * row_count, model_width)
            .astype(jnp.float32)
        )
        seg_ends = jnp.cumsum(
            cont_lengths[first_group : first_group + groups], axis=1, dtype=jnp.int32
        )
        query_seg = segment_of(query_pos, seg_ends)
        normed_one, hat_one, scale_one = norm_forward(inputs, gain_one, bias_one)
        low_one = normed_one.astype(jnp.bfloat16)
        queries = (dot_plain(low_one, query_w) + query_b).astype(jnp.bfloat16)
        key_local = (
            dot_plain(low_one, key_w).astype(jnp.bfloat16).reshape(groups, row_count, model_width)
        )
        value_local = (
            (dot_plain(low_one, value_w) + value_b)
            .astype(jnp.bfloat16)
            .reshape(groups, row_count, model_width)
        )
        query_heads = queries.reshape(groups, row_count, HEADS, HEAD)
        context_info = (query_heads, query_pos, query_seg, seg_ends, layout)
        start_state = (
            jnp.full((groups, HEADS, row_count), NEGATIVE, jnp.float32),
            jnp.zeros((groups, HEADS, row_count), jnp.float32),
            jnp.zeros((groups, HEADS, row_count, HEAD), jnp.float32),
        )
        final_state = attend_block(
            start_state,
            (
                lax.all_gather(key_local, "ctx", axis=1, tiled=True),
                lax.all_gather(value_local, "ctx", axis=1, tiled=True),
            ),
            context_info=context_info,
        )
        running, totals, weighted = final_state
        logsum = running + jnp.log(totals)
        attended = weighted / totals[..., None]
        attended_rows = jnp.transpose(attended, (0, 2, 1, 3)).reshape(
            groups * row_count, model_width
        )
        low_attended = attended_rows.astype(jnp.bfloat16)
        middle = inputs + dot_plain(low_attended, out_w) + out_b
        normed_two, hat_two, scale_two = norm_forward(middle, gain_two, bias_two)
        low_two = normed_two.astype(jnp.bfloat16)
        hidden_pre = dot_plain(low_two, in_w) + in_b
        hidden, gelu_back = jax.vjp(exact_gelu, hidden_pre)
        low_hidden = hidden.astype(jnp.bfloat16)
        result = middle + dot_plain(low_hidden, back_w) + back_b
        outputs.append(result.astype(jnp.bfloat16).reshape(groups, row_count, model_width))
        upstream_low = grad_out[first_group : first_group + groups].reshape(
            groups * row_count, model_width
        )
        upstream = upstream_low.astype(jnp.float32)
        grad_back_w = dot_inner(low_hidden, upstream_low)
        grad_back_b = jnp.sum(upstream, axis=0)
        grad_hidden = dot_transposed(upstream_low, back_w)
        grad_pre = gelu_back(grad_hidden)[0].astype(jnp.bfloat16)
        grad_in_w = dot_inner(low_two, grad_pre)
        grad_in_b = jnp.sum(grad_pre.astype(jnp.float32), axis=0)
        grad_normed_two = dot_transposed(grad_pre, in_w)
        grad_mid_norm, grad_gain_two, grad_bias_two = norm_backward(
            grad_normed_two, hat_two, scale_two, gain_two
        )
        grad_middle = upstream + grad_mid_norm
        grad_branch = grad_middle.astype(jnp.bfloat16)
        grad_out_w = dot_inner(low_attended, grad_branch)
        grad_out_b = jnp.sum(grad_branch.astype(jnp.float32), axis=0)
        grad_attended = dot_transposed(grad_branch, out_w).astype(jnp.bfloat16)
        grad_heads = grad_attended.reshape(groups, row_count, HEADS, HEAD)
        row_delta = jnp.einsum("grhe,ghre->ghr", grad_heads.astype(jnp.float32), attended)
        grad_info = (grad_heads, logsum, row_delta)
        query_grad, term = back_fold(
            (
                lax.all_gather(key_local, "ctx", axis=1, tiled=True),
                lax.all_gather(value_local, "ctx", axis=1, tiled=True),
            ),
            context_info=context_info,
            grad_info=grad_info,
        )
        own_grads = lax.psum_scatter(
            term.astype(jnp.bfloat16), "ctx", scatter_dimension=1, tiled=True
        ).astype(jnp.float32)
        grad_queries = (
            jnp.transpose(query_grad, (0, 2, 1, 3))
            .reshape(groups * row_count, model_width)
            .astype(jnp.bfloat16)
        )
        grad_keys = (
            own_grads[..., :model_width]
            .reshape(groups * row_count, model_width)
            .astype(jnp.bfloat16)
        )
        grad_values = (
            own_grads[..., model_width:]
            .reshape(groups * row_count, model_width)
            .astype(jnp.bfloat16)
        )
        grad_query_w = dot_inner(low_one, grad_queries)
        grad_query_b = jnp.sum(grad_queries.astype(jnp.float32), axis=0)
        grad_key_w = dot_inner(low_one, grad_keys)
        grad_value_w = dot_inner(low_one, grad_values)
        grad_value_b = jnp.sum(grad_values.astype(jnp.float32), axis=0)
        grad_normed_one = (
            dot_transposed(grad_queries, query_w)
            + dot_transposed(grad_keys, key_w)
            + dot_transposed(grad_values, value_w)
        )
        grad_in_norm, grad_gain_one, grad_bias_one = norm_backward(
            grad_normed_one, hat_one, scale_one, gain_one
        )
        grad_outputs.append((grad_middle + grad_in_norm).reshape(groups, row_count, model_width))
        micro_grads = (
            grad_gain_one,
            grad_bias_one,
            grad_query_w,
            grad_query_b,
            grad_key_w,
            grad_value_w,
            grad_value_b,
            grad_out_w,
            grad_out_b,
            grad_gain_two,
            grad_bias_two,
            grad_in_w,
            grad_in_b,
            grad_back_w,
            grad_back_b,
        )
        pending = add_tuples(pending, micro_grads)
    shares = jax.tree.map(
        lambda part: part.astype(jnp.float32),
        lax.psum_scatter(shortened(pending), "wsh", scatter_dimension=0, tiled=True),
    )
    reduced = jax.tree.map(
        lambda part: part.astype(jnp.float32), lax.psum(shortened(shares), "ctx")
    )
    out_tokens = jnp.concatenate(outputs, axis=0)
    grad_tokens = jnp.concatenate(grad_outputs, axis=0)
    return (
        out_tokens,
        grad_tokens,
        reduced[0],
        reduced[1],
        reduced[2],
        reduced[3],
        reduced[4],
        reduced[5],
        reduced[6],
        reduced[7],
        reduced[8],
        reduced[9],
        reduced[10],
        reduced[11],
        reduced[12],
        reduced[13],
        reduced[14],
    )


def solution(mesh):
    placed = (
        P("wsh", "ctx", None),
        P("wsh", None),
        P("wsh", "ctx", None),
        P("wsh"),
        P("wsh"),
        P("wsh", None),
        P("wsh"),
        P("wsh", None),
        P("wsh", None),
        P("wsh"),
        P("wsh", None),
        P("wsh"),
        P("wsh"),
        P("wsh"),
        P("wsh", None),
        P("wsh"),
        P("wsh", None),
        P("wsh"),
    )
    return jax.shard_map(
        body,
        mesh=mesh,
        in_specs=placed,
        out_specs=(
            P("wsh", "ctx", None),
            P("wsh", "ctx", None),
            P("wsh"),
            P("wsh"),
            P("wsh", None),
            P("wsh"),
            P("wsh", None),
            P("wsh", None),
            P("wsh"),
            P("wsh", None),
            P("wsh"),
            P("wsh"),
            P("wsh"),
            P("wsh", None),
            P("wsh"),
            P("wsh", None),
            P("wsh"),
        ),
        check_vma=False,
    )
```

profile of v0, /device:TPU:0, one launch (start us, length us, event | category | flops | bytes accessed | tf_op | source)
XLA Modules:
  0.0 1466.5 jit_solution(10385209844396533104)
XLA Ops:
  63.8 79.6 %all-gather.42.cloned.1.call-done = bf16[4096,768]{1,0:T(8,128)(2,1)} async-done(((bf16[256,768]{1,0:T(8,128)(2,1)}), bf16[4096,768]{1,0:T(8,128)(2,1)}) %all-gather.42.cloned.1.call-update) | async-done | bytes 6291472 | tf_op jit(solution)/shard_map/all_gather | solution.py:307
  143.4 95.2 %all-gather.40.cloned.1.call-done = bf16[4096,768]{1,0:T(8,128)(2,1)} async-done(((bf16[256,768]{1,0:T(8,128)(2,1)}), bf16[4096,768]{1,0:T(8,128)(2,1)}) %all-gather.40.cloned.1.call-update) | async-done | bytes 6291472 | tf_op jit(solution)/shard_map/all_gather | solution.py:306
  238.5 87.0 %conditional.5 = (f32[1,12,256]{2,1,0:T(8,128)S(1)}, f32[1,12,256]{2,1,0:T(8,128)S(1)}, f32[1,12,256,64]{2,3,1,0:T(8,128)}) conditional(s32[]{:T(128)} %convert_element_type.464, () %tuple.42, (pred[1,256,4096]{2,1,0:T(8,128)(4,1)S(1)}, bf16[1,256,12,64]{1,3,2,0:T(8,128)(2,1)}, bf16[1,4096,768]{2,1,0:T(8,128)(2,1)}, ...), branch_computations={%region_18.19_spmd, %region_19.22_spmd} | conditional | flops 3384800256 | bytes 193155104 | solution.py:109
  256.2 22.4 %fusion.15 = (f32[12,256]{1,0:T(8,128)S(1)}, f32[12,256,4096]{2,1,0:T(8,128)}) fusion(pred[256,4096]{1,0:T(8,128)(4,1)S(1)} %bitcast.344, bf16[4096,12,64]{0,2,1:T(8,128)(2,1)} %bitcast.332, bf16[1,256,12,64]{1,3,2,0:T(8,128)(2,1)} %get-tuple-element.61), kind=kOutput, calls=%fused_computation.17 | convolution fusion | flops 1648358400 | bytes 58077184 | tf_op jit(solution)/shard_map/cond/branch_1_fun/grhe,gnhe->ghrn/dot_general | solution.py:91
  278.5 22.9 %fusion.21 = f32[1,12,256,64]{2,3,1,0:T(8,128)} fusion(bf16[4096,12,64]{0,2,1:T(8,128)(2,1)} %bitcast.356, f32[12,256,4096]{2,1,0:T(8,128)} %get-tuple-element.294, f32[12,256]{1,0:T(8,128)S(1)} %get-tuple-element.291, pred[256,4096]{1,0:T(8,128)(4,1)S(1)} %bitcast.345), kind=kOutput, calls=%fused_computation.22 | convolution fusion | flops 1673527296 | bytes 58470400 | tf_op jit(solution)/shard_map/cond/branch_1_fun/ghrn,gnhe->ghre/dot_general | solution.py:98
  301.4 24.1 %fusion.17 = f32[12,256]{1,0:T(8,128)S(1)} fusion(f32[12,256,4096]{2,1,0:T(8,128)} %get-tuple-element.294, f32[12,256]{1,0:T(8,128)S(1)} %get-tuple-element.291, pred[256,4096]{1,0:T(8,128)(4,1)S(1)} %bitcast.346), kind=kLoop, calls=%fused_computation.19 | loop fusion | flops 62911488 | bytes 51404800 | tf_op jit(solution)/shard_map/cond/branch_1_fun/reduce_sum | solution.py:97
  330.1 15.6 %all-gather.38.cloned.1.call-done = bf16[4096,768]{1,0:T(8,128)(2,1)} async-done(((bf16[256,768]{1,0:T(8,128)(2,1)}), bf16[4096,768]{1,0:T(8,128)(2,1)}) %all-gather.38.cloned.1.call-update) | async-done | bytes 6291472 | tf_op jit(solution)/shard_map/all_gather | solution.py:307
  345.7 95.3 %all-gather.36.cloned.1.call-done = bf16[4096,768]{1,0:T(8,128)(2,1)} async-done(((bf16[256,768]{1,0:T(8,128)(2,1)}), bf16[4096,768]{1,0:T(8,128)(2,1)}) %all-gather.36.cloned.1.call-update) | async-done | bytes 6291472 | tf_op jit(solution)/shard_map/all_gather | solution.py:306
  441.0 88.6 %conditional.4 = (f32[1,12,256]{2,1,0:T(8,128)S(1)}, f32[1,12,256]{2,1,0:T(8,128)S(1)}, f32[1,12,256,64]{2,3,1,0:T(8,128)}) conditional(s32[]{:T(128)} %convert_element_type.440, () %tuple.40, (pred[1,256,4096]{2,1,0:T(8,128)(4,1)S(1)}, bf16[1,256,12,64]{1,3,2,0:T(8,128)(2,1)S(1)}, bf16[1,4096,768]{2,1,0:T(8,128)(2,1)}, ...), branch_computations={%region_6.7_spmd, %region_7.10_spmd} | conditional | flops 3384800256 | bytes 193155104 | solution.py:109
  459.0 24.4 %fusion = (f32[12,256]{1,0:T(8,128)S(1)}, f32[12,256,4096]{2,1,0:T(8,128)}) fusion(pred[256,4096]{1,0:T(8,128)(4,1)S(1)} %bitcast.349, bf16[4096,12,64]{0,2,1:T(8,128)(2,1)} %bitcast.333, bf16[1,256,12,64]{1,3,2,0:T(8,128)(2,1)S(1)} %get-tuple-element.57), kind=kOutput, calls=%fused_computation.2 | convolution fusion | flops 1648358400 | bytes 58077184 | tf_op jit(solution)/shard_map/cond/branch_1_fun/grhe,gnhe->ghrn/dot_general | solution.py:91
  483.5 22.4 %fusion.6 = f32[1,12,256,64]{2,3,1,0:T(8,128)} fusion(bf16[4096,12,64]{0,2,1:T(8,128)(2,1)} %bitcast.357, f32[12,256,4096]{2,1,0:T(8,128)} %get-tuple-element.290, f32[12,256]{1,0:T(8,128)S(1)} %get-tuple-element.287, pred[256,4096]{1,0:T(8,128)(4,1)S(1)} %bitcast.350), kind=kOutput, calls=%fused_computation.7 | convolution fusion | flops 1673527296 | bytes 58470400 | tf_op jit(solution)/shard_map/cond/branch_1_fun/ghrn,gnhe->ghre/dot_general | solution.py:98
  505.9 23.3 %fusion.2 = f32[12,256]{1,0:T(8,128)S(1)} fusion(f32[12,256,4096]{2,1,0:T(8,128)} %get-tuple-element.290, f32[12,256]{1,0:T(8,128)S(1)} %get-tuple-element.287, pred[256,4096]{1,0:T(8,128)(4,1)S(1)} %bitcast.351), kind=kLoop, calls=%fused_computation.4 | loop fusion | flops 62911488 | bytes 51404800 | tf_op jit(solution)/shard_map/cond/branch_1_fun/reduce_sum | solution.py:97
  578.7 139.7 %conditional.6 = (bf16[1,4096,1536]{1,2,0:T(8,128)(2,1)}, bf16[1,12,256,64]{2,3,1,0:T(8,128)(2,1)S(1)}) conditional(s32[]{:T(128)} %convert_element_type.440, () %tuple.44, (pred[1,256,4096]{2,1,0:T(8,128)(4,1)S(1)}, bf16[1,256,12,64]{1,3,2,0:T(8,128)(2,1)S(1)}, bf16[1,4096,768]{2,1,0:T(8,128)(2,1)}, f32[1,12,256]{2,1,0:T(8,128)S(1)}, ...), branch_computations={%region_26.27_spmd, %region_27.28_spmd} | conditional | flops 8211136512 | bytes 314789888 | solution.py:166
  597.8 22.1 %fusion.37 = f32[12,256,4096]{2,1,0:T(8,128)} fusion(bf16[4096,12,64]{0,2,1:T(8,128)(2,1)} %bitcast.328, bf16[1,256,12,64]{1,3,2,0:T(8,128)(2,1)S(1)} %get-tuple-element.65), kind=kOutput, calls=%fused_computation.42 | convolution fusion | flops 1610612736 | bytes 57016320 | tf_op jit(solution)/shard_map/cond/branch_1_fun/grhe,gnhe->ghrn/dot_general | solution.py:126
  619.9 22.0 %fusion.31 = bf16[12,4096,64]{1,2,0:T(8,128)(2,1)} fusion(bf16[256,12,64]{0,2,1:T(8,128)(2,1)S(1)} %bitcast.372, f32[12,256,4096]{2,1,0:T(8,128)} %fusion.37, f32[12,256]{1,0:T(8,128)S(1)} %add_bitcast_fusion, pred[256,4096]{1,0:T(8,128)(4,1)S(1)} %bitcast.352), kind=kOutput, calls=%fused_computation.34 | convolution fusion | flops 1660944384 | bytes 58077184 | tf_op jit(solution)/shard_map/cond/branch_1_fun/ghrn,grhe->gnhe/dot_general | solution.py:146
  642.0 32.3 %multiply_convert_fusion = bf16[12,256,4096]{2,1,0:T(8,128)(2,1)} fusion(f32[12,256,4096]{2,1,0:T(8,128)} %fusion.37, f32[12,256]{1,0:T(8,128)S(1)} %multiply_reduce_fusion, f32[12,256]{1,0:T(8,128)S(1)} %add_bitcast_fusion, pred[256,4096]{1,0:T(8,128)(4,1)S(1)} %bitcast.353, bf16[256,12,64]{0,2,1:T(8,128)(2,1)S(1)} %bitcast.373, ...), kind=kOutput, calls=%fused_computation.30 | convolution fusion | flops 1686110208 | bytes 83255296 | tf_op jit(solution)/shard_map/cond/branch_1_fun/grhe,gnhe->ghrn/dot_general | solution.py:130
  674.3 14.3 fusion.35
  688.7 15.3 %convolution_multiply_fusion = bf16[12,4096,64]{1,2,0:T(8,128)(2,1)} fusion(bf16[12,256,4096]{2,1,0:T(8,128)(2,1)} %multiply_convert_fusion, bf16[1,256,12,64]{1,3,2,0:T(8,128)(2,1)S(1)} %get-tuple-element.65), kind=kOutput, calls=%fused_computation.36 | convolution fusion | flops 1616904192 | bytes 31850496 | tf_op jit(solution)/shard_map/cond/branch_1_fun/ghrn,grhe->gnhe/dot_general | solution.py:143
  703.9 14.3 pad_maximum_fusion
  720.6 142.7 %conditional.7 = (bf16[1,4096,1536]{1,2,0:T(8,128)(2,1)}, bf16[1,12,256,64]{2,3,1,0:T(8,128)(2,1)S(1)}) conditional(s32[]{:T(128)} %convert_element_type.464, () %tuple.46, (pred[1,256,4096]{2,1,0:T(8,128)(4,1)S(1)}, bf16[1,256,12,64]{1,3,2,0:T(8,128)(2,1)}, bf16[1,4096,768]{2,1,0:T(8,128)(2,1)}, f32[1,12,256]{2,1,0:T(8,128)S(1)}, ...), branch_computations={%region_33.34_spmd, %region_34.35_spmd} | conditional | flops 8211136512 | bytes 314789888 | solution.py:166
  739.7 22.5 %fusion.48 = f32[12,256,4096]{2,1,0:T(8,128)} fusion(bf16[4096,12,64]{0,2,1:T(8,128)(2,1)} %bitcast.330, bf16[1,256,12,64]{1,3,2,0:T(8,128)(2,1)} %get-tuple-element.73), kind=kOutput, calls=%fused_computation.59 | convolution fusion | flops 1610612736 | bytes 57016320 | tf_op jit(solution)/shard_map/cond/branch_1_fun/grhe,gnhe->ghrn/dot_general | solution.py:126
  762.2 23.0 %fusion.42 = bf16[12,4096,64]{1,2,0:T(8,128)(2,1)} fusion(bf16[256,12,64]{0,2,1:T(8,128)(2,1)S(1)} %bitcast.374, f32[12,256,4096]{2,1,0:T(8,128)} %fusion.48, f32[12,256]{1,0:T(8,128)S(1)} %add_bitcast_fusion.1, pred[256,4096]{1,0:T(8,128)(4,1)S(1)} %bitcast.347), kind=kOutput, calls=%fused_computation.51 | convolution fusion | flops 1660944384 | bytes 58077184 | tf_op jit(solution)/shard_map/cond/branch_1_fun/ghrn,grhe->gnhe/dot_general | solution.py:146
  785.2 32.7 %multiply_convert_fusion.1 = bf16[12,256,4096]{2,1,0:T(8,128)(2,1)} fusion(f32[12,256,4096]{2,1,0:T(8,128)} %fusion.48, f32[12,256]{1,0:T(8,128)S(1)} %multiply_reduce_fusion.1, f32[12,256]{1,0:T(8,128)S(1)} %add_bitcast_fusion.1, pred[256,4096]{1,0:T(8,128)(4,1)S(1)} %bitcast.348, bf16[256,12,64]{0,2,1:T(8,128)(2,1)S(1)} %bitcast.375, ...), kind=kOutput, calls=%fused_computation.47 | convolution fusion | flops 1686110208 | bytes 83255296 | tf_op jit(solution)/shard_map/cond/branch_1_fun/grhe,gnhe->ghrn/dot_general | solution.py:130
  817.9 14.6 fusion.46
  832.5 16.1 %convolution_multiply_fusion.2 = bf16[12,4096,64]{1,2,0:T(8,128)(2,1)} fusion(bf16[12,256,4096]{2,1,0:T(8,128)(2,1)} %multiply_convert_fusion.1, bf16[1,256,12,64]{1,3,2,0:T(8,128)(2,1)} %get-tuple-element.73), kind=kOutput, calls=%fused_computation.53 | convolution fusion | flops 1616904192 | bytes 31850496 | tf_op jit(solution)/shard_map/cond/branch_1_fun/ghrn,grhe->gnhe/dot_general | solution.py:143
  848.6 14.3 pad_maximum_fusion.1
  884.1 37.3 %reduce-scatter.9.cloned.1.call-done = bf16[1,256,1536]{1,2,0:T(8,128)(2,1)} async-done(((bf16[1,4096,1536]{1,2,0:T(8,128)(2,1)}), bf16[1,256,1536]{1,2,0:T(8,128)(2,1)}) %reduce-scatter.9.cloned.1.call-update) | async-done | bytes 786448 | tf_op jit(solution)/shard_map/reduce_scatter | solution.py:356
  924.5 205.4 %reduce-scatter.11.cloned.1.call-done = bf16[1,256,1536]{1,2,0:T(8,128)(2,1)} async-done(((bf16[1,4096,1536]{1,2,0:T(8,128)(2,1)}), bf16[1,256,1536]{1,2,0:T(8,128)(2,1)}) %reduce-scatter.11.cloned.1.call-update) | async-done | bytes 786448 | tf_op jit(solution)/shard_map/reduce_scatter | solution.py:356
  1153.2 16.6 %reduce-scatter.21.cloned.1.call-done = bf16[384,3072]{1,0:T(8,128)(2,1)} async-done(((bf16[768,3072]{1,0:T(8,128)(2,1)}), bf16[384,3072]{1,0:T(8,128)(2,1)}) %reduce-scatter.21.cloned.1.call-update) | async-done | bytes 2359312 | tf_op jit(solution)/shard_map/reduce_scatter | solution.py:408
  1169.8 16.6 %reduce-scatter.23.cloned.1.call-done = bf16[1536,768]{1,0:T(8,128)(2,1)} async-done(((bf16[3072,768]{1,0:T(8,128)(2,1)}), bf16[1536,768]{1,0:T(8,128)(2,1)}) %reduce-scatter.23.cloned.1.call-update) | async-done | bytes 2359312 | tf_op jit(solution)/shard_map/reduce_scatter | solution.py:408
  1233.1 80.4 %all-reduce.9 = (bf16[384]{0:T(512)(128)(2,1)S(1)}, bf16[384]{0:T(512)(128)(2,1)S(1)}, bf16[384]{0:T(512)(128)(2,1)S(1)}, bf16[384]{0:T(512)(128)(2,1)S(1)}, bf1...) all-reduce(bf16[384]{0:T(512)(128)(2,1)S(1)} %dynamic-slice.1, ...), channel_id=1, replica_groups=mesh['ctx'=16,'wsh'=2] {'ctx'}, use_global_device_ids=true, to_apply=%region_41.42 | all-reduce | flops 4608 | bytes 18432 | tf_op jit(solution)/shard_map/psum | solution.py:411
  1321.7 126.1 %all-reduce.14.cloned.1.call-done = (bf16[384,768]{1,0:T(8,128)(2,1)}, bf16[384,768]{1,0:T(8,128)(2,1)}, bf16[384,768]{1,0:T(8,128)(2,1)}, bf16[384,768]{1,0:T(8...) async-done(((bf16[384,768]{1,0:T(8,128)(2,1)}, bf16[384,768]{1,0:T(8,128)(2,1)}, bf16[384,768]{1,0:T(8,128)(2,1)}, bf16[384,768]{1,0:T(8,128)(2,1)}, ...) | async-done | bytes 7077904 | tf_op jit(solution)/shard_map/psum | solution.py:411
  (401 shorter events, 295.6 us)
Async XLA Ops:
  7.2 14.3 all-gather.28.cloned.1.call-start
  7.9 25.6 %all-gather.26.cloned.1.call-start = ((), (), s32[]{:S(2)}) async-start(), calls=%async_computation.9 | async-start | bytes 1769472 | tf_op jit(solution)/shard_map/all_gather | solution.py:224
  8.7 48.5 %all-gather.24.cloned.1.call-start = ((), (), s32[]{:S(2)}) async-start(), calls=%async_computation.8 | async-start | bytes 1769472 | tf_op jit(solution)/shard_map/all_gather | solution.py:222
  9.4 134.0 %all-gather.42.cloned.1.call-start = ((), (), s32[]{:S(2)}) async-start(), calls=%async_computation.25 | async-start | bytes 6684672 | tf_op jit(solution)/shard_map/all_gather | solution.py:307
  14.7 45.4 %copy-start.39 = (f32[768]{0:T(1024)}, f32[768]{0:T(1024)S(1)}, u32[]{:S(2)}) copy-start(f32[768]{0:T(1024)S(1)} %reshape.1323) | copy-start | bytes 9220
  14.7 45.4 %copy-start.41 = (f32[768]{0:T(1024)}, f32[768]{0:T(1024)S(1)}, u32[]{:S(2)}) copy-start(f32[768]{0:T(1024)S(1)} %reshape.1324) | copy-start | bytes 9220
  18.6 38.6 %copy-start.53 = (f32[256]{0:T(256)}, f32[256]{0:T(256)S(1)}, u32[]{:S(2)}) copy-start(f32[256]{0:T(256)S(1)} %get-tuple-element.331) | copy-start | bytes 3076
  18.6 41.5 %copy-start.51 = (f32[256]{0:T(256)}, f32[256]{0:T(256)S(1)}, u32[]{:S(2)}) copy-start(f32[256]{0:T(256)S(1)} %get-tuple-element.332) | copy-start | bytes 3076
  19.0 38.2 %copy-start.59 = (f32[256]{0:T(256)}, f32[256]{0:T(256)S(1)}, u32[]{:S(2)}) copy-start(f32[256]{0:T(256)S(1)} %add_rsqrt_fusion.1) | copy-start | bytes 3076
  24.2 214.3 %all-gather.40.cloned.1.call-start = ((), (), s32[]{:S(2)}) async-start(), calls=%async_computation.24 | async-start | bytes 6684672 | tf_op jit(solution)/shard_map/all_gather | solution.py:306
  36.2 291.6 %all-gather.30.cloned.1.call-start = ((), (), s32[]{:S(2)}) async-start(), calls=%async_computation.11 | async-start | bytes 1769472 | tf_op jit(solution)/shard_map/all_gather | solution.py:227
  36.8 308.9 %all-gather.38.cloned.1.call-start = ((), (), s32[]{:S(2)}) async-start(), calls=%async_computation.23 | async-start | bytes 6684672 | tf_op jit(solution)/shard_map/all_gather | solution.py:307
  38.2 402.8 %all-gather.36.cloned.1.call-start = ((), (), s32[]{:S(2)}) async-start(), calls=%async_computation.22 | async-start | bytes 6684672 | tf_op jit(solution)/shard_map/all_gather | solution.py:306
  39.6 495.4 %all-gather.32.cloned.1.call-start = ((), (), s32[]{:S(2)}) async-start(), calls=%async_computation.12 | async-start | bytes 7077888 | tf_op jit(solution)/shard_map/all_gather | solution.py:231
  40.3 518.0 %all-gather.34.cloned.1.call-start = ((), (), s32[]{:S(2)}) async-start(), calls=%async_computation.13 | async-start | bytes 7077888 | tf_op jit(solution)/shard_map/all_gather | solution.py:233
  40.9 880.5 %reduce-scatter.9.cloned.1.call-start = ((), (), s32[]{:S(2)}) async-start(), calls=%async_computation.14 | async-start | bytes 13369344 | tf_op jit(solution)/shard_map/reduce_scatter | solution.py:356
  55.9 182.6 %copy-start.2 = (pred[1,256,4096]{2,1,0:T(8,128)(4,1)}, pred[1,256,4096]{2,1,0:T(8,128)(4,1)S(1)}, u32[]{:S(2)}) copy-start(pred[1,256,4096]{2,1,0:T(8,128)(4,1)S(1)} %get-tuple-element.308) | copy-start | bytes 3145732
  325.5 115.5 %copy-start.45 = (f32[1,12,256]{2,1,0:T(8,128)}, f32[1,12,256]{2,1,0:T(8,128)S(1)}, u32[]{:S(2)}) copy-start(f32[1,12,256]{2,1,0:T(8,128)S(1)} %get-tuple-element.110) | copy-start | bytes 36868
  325.5 115.5 %copy-start.49 = (f32[1,12,256]{2,1,0:T(8,128)}, f32[1,12,256]{2,1,0:T(8,128)S(1)}, u32[]{:S(2)}) copy-start(f32[1,12,256]{2,1,0:T(8,128)S(1)} %get-tuple-element.114) | copy-start | bytes 36868
  329.8 242.2 %copy-start.6 = (f32[256,768]{1,0:T(8,128)}, f32[256,768]{1,0:T(8,128)S(1)}, u32[]{:S(2)}) copy-start(f32[256,768]{1,0:T(8,128)S(1)} %get-tuple-element.316) | copy-start | bytes 2359300
  329.8 244.6 %copy-start.61 = (f32[256]{0:T(256)}, f32[256]{0:T(256)S(1)}, u32[]{:S(2)}) copy-start(f32[256]{0:T(256)S(1)} %broadcast_multiply_fusion.8) | copy-start | bytes 3076
  330.1 244.4 %copy-start.72 = (f32[256]{0:T(256)}, f32[256]{0:T(256)S(1)}, u32[]{:S(2)}) copy-start(f32[256]{0:T(256)S(1)} %add_rsqrt_fusion) | copy-start | bytes 3076
  533.8 40.6 %copy-start.57 = (f32[256]{0:T(256)}, f32[256]{0:T(256)S(1)}, u32[]{:S(2)}) copy-start(f32[256]{0:T(256)S(1)} %broadcast_multiply_fusion.10) | copy-start | bytes 3076
  534.9 39.5 %copy-start.67 = (f32[256]{0:T(256)}, f32[256]{0:T(256)S(1)}, u32[]{:S(2)}) copy-start(f32[256]{0:T(256)S(1)} %add_rsqrt_fusion.2) | copy-start | bytes 3076
  719.2 410.6 %reduce-scatter.11.cloned.1.call-start = ((), (), s32[]{:S(2)}) async-start(), calls=%async_computation.15 | async-start | bytes 13369344 | tf_op jit(solution)/shard_map/reduce_scatter | solution.py:356
  863.4 277.5 %reduce-scatter.19.cloned.1.call-start = ((), (), s32[]{:S(2)}) async-start(), calls=%async_computation.19 | async-start | bytes 1769472 | tf_op jit(solution)/shard_map/reduce_scatter | solution.py:408
  867.3 285.9 %reduce-scatter.13.cloned.1.call-start = ((), (), s32[]{:S(2)}) async-start(), calls=%async_computation.16 | async-start | bytes 1769472 | tf_op jit(solution)/shard_map/reduce_scatter | solution.py:408
  869.9 299.9 %reduce-scatter.21.cloned.1.call-start = ((), (), s32[]{:S(2)}) async-start(), calls=%async_computation.20 | async-start | bytes 7077888 | tf_op jit(solution)/shard_map/reduce_scatter | solution.py:408
  877.2 309.2 %reduce-scatter.23.cloned.1.call-start = ((), (), s32[]{:S(2)}) async-start(), calls=%async_computation.21 | async-start | bytes 7077888 | tf_op jit(solution)/shard_map/reduce_scatter | solution.py:408
  884.1 314.8 %reduce-scatter.15.cloned.1.call-start = ((), (), s32[]{:S(2)}) async-start(), calls=%async_computation.17 | async-start | bytes 1769472 | tf_op jit(solution)/shard_map/reduce_scatter | solution.py:408
  1133.4 78.0 %reduce-scatter.17.cloned.1.call-start = ((), (), s32[]{:S(2)}) async-start(), calls=%async_computation.18 | async-start | bytes 1769472 | tf_op jit(solution)/shard_map/reduce_scatter | solution.py:408
  1136.9 310.9 %all-reduce.14.cloned.1.call-start = ((), (), s32[]{:S(2)}) async-start(), calls=%async_computation.26 | async-start | bytes 14155776 | tf_op jit(solution)/shard_map/psum | solution.py:411
  (78 other events, 317.6 us)
Sparse Core Ops, SparseCore 0:
  9.5 11.9 all-gather.27
  23.1 10.3 all-gather.25
  35.0 10.3 all-gather.23
  48.7 94.6 all-gather.41
  146.6 91.9 all-gather.39
  239.9 7.7 all-gather.29
  251.1 94.5 all-gather.37
  349.0 91.9 all-gather.35
  442.5 12.9 all-gather.31
  456.9 15.6 all-gather.33
  719.3 202.0 reduce-scatter.8
  926.9 202.8 reduce-scatter.10
  1132.7 7.9 reduce-scatter.18
  1143.4 9.7 reduce-scatter.12
  1155.9 13.8 reduce-scatter.20
  1172.5 13.8 reduce-scatter.22
  1189.0 9.7 reduce-scatter.14
  1201.6 9.7 reduce-scatter.16
  1217.8 229.9 all-reduce.13
where the time goes:
time: 1480 us; the launch traced here: 1470 us
  waiting for transfers between devices  741 us (50%)
  matrix products  402 us (27%)
  other arithmetic  116 us (8%)
  blocking collectives  101 us (7%)
  local copies, waits for them, and re-layouts  86 us (6%)
  between operations  18.3 us (1%)
    reduce_scatter x2, waiting for transfers between devices, body(): lax.psum_scatter(term.astype(jnp.bfloat16), 'ctx', scatter_dimension=1, t...  243 us
    all_gather x2, waiting for transfers between devices, body(): lax.all_gather(key_local, 'ctx', axis=1, tiled=True)  190 us
    psum x1, waiting for transfers between devices, body(): lax.psum(shortened(shares), 'ctx')  126 us
    all_gather x2, waiting for transfers between devices, body(): lax.all_gather(value_local, 'ctx', axis=1, tiled=True)  95.2 us
    psum x1, blocking collectives, body(): lax.psum(shortened(shares), 'ctx')  80.4 us
    another operation x11, local copies, waits for them, and re-layouts  70.9 us
    reduce_scatter x6, waiting for transfers between devices, body(): lax.psum_scatter(shortened(pending), 'wsh', scatter_dimension=0, tiled=True)  70.5 us
    dot_general x2, matrix products, back_compute(): jnp.einsum('grhe,gnhe->ghrn', grad_heads, values_heads, preferred_element...  65 us
  transfers between devices with their start and end apart: 19, of which 14 were waited for; matrix products, arithmetic and copies ran while one was open for 29% of the time, Pallas kernels for 0%

commit v1 on v0

v1 whole, which is shorter than its diff:
```python
import jax
import jax.numpy as jnp
from jax import lax
from jax.experimental import pallas as pl
from jax.experimental.pallas import tpu as pltpu
from jax.sharding import PartitionSpec as P

HEADS = 12
HEAD = 64
PROMPT = 2048
MOSTLEN = 512
HP = 8
TILE = 256

EPSILON = 1e-12
NEGATIVE = -1e30
F32 = jnp.float32
BF16 = jnp.bfloat16


def dot_plain(left_side, right_side):
    return jnp.dot(left_side, right_side, preferred_element_type=F32)


def dot_inner(left_side, right_side):
    return lax.dot_general(
        left_side, right_side, (((0,), (0,)), ((), ())), preferred_element_type=F32
    )


def dot_transposed(left_side, right_side):
    return lax.dot_general(
        left_side, right_side, (((1,), (1,)), ((), ())), preferred_element_type=F32
    )


def exact_gelu(values):
    return jax.nn.gelu(values, approximate=False)


def norm_forward(values, gain_vec, bias_vec):
    center = values - jnp.mean(values, axis=-1, keepdims=True)
    scaled = lax.rsqrt(jnp.mean(center * center, axis=-1, keepdims=True) + EPSILON)
    normed = center * scaled
    return (normed * gain_vec + bias_vec, normed, scaled)


def norm_backward(upstream, normed, scaled, gain_vec):
    inner_grad = upstream * gain_vec
    result = scaled * (
        inner_grad
        - jnp.mean(inner_grad, axis=-1, keepdims=True)
        - normed * jnp.mean(inner_grad * normed, axis=-1, keepdims=True)
    )
    return (
        result,
        jnp.sum(upstream * normed, axis=0, keepdims=True),
        jnp.sum(upstream, axis=0, keepdims=True),
    )


def vmem_specs(count):
    return [pl.BlockSpec(memory_space=pltpu.VMEM) for unused in range(count)]


SMEM_SPEC = pl.BlockSpec(memory_space=pltpu.SMEM)
PARAMS = pltpu.CompilerParams(vmem_limit_bytes=56 << 20)


def project_kernel(
    wsh_ref, x_ref, gain_ref, bias_ref, mine_ref, other_ref, add_ref, out_ref, low_ref
):
    half = mine_ref.shape[1]
    mine_at = wsh_ref[0]

    @pl.when(pl.program_id(0) == 0)
    def _():
        normed, unused, unused_two = norm_forward(
            x_ref[...].astype(F32), gain_ref[...], bias_ref[...]
        )
        low_ref[0] = normed[:, :half].astype(BF16)
        low_ref[1] = normed[:, half:].astype(BF16)

    total = dot_plain(low_ref[mine_at], mine_ref[0]) + dot_plain(low_ref[1 - mine_at], other_ref[0])
    out_ref[0] = (total + add_ref[0]).astype(BF16)


def project(mine_at, rows_in, gain, bias, mine, other, add):
    parts, half, width = mine.shape
    count, model = rows_in.shape
    whole = lambda i, *unused: (0, 0)
    return pl.pallas_call(
        project_kernel,
        grid_spec=pltpu.PrefetchScalarGridSpec(
            num_scalar_prefetch=1,
            grid=(parts,),
            in_specs=[
                pl.BlockSpec((count, model), whole),
                pl.BlockSpec((1, model), whole),
                pl.BlockSpec((1, model), whole),
                pl.BlockSpec((1, half, width), lambda i, *unused: (i, 0, 0)),
                pl.BlockSpec((1, half, width), lambda i, *unused: (i, 0, 0)),
                pl.BlockSpec((1, 1, width), lambda i, *unused: (i, 0, 0)),
            ],
            out_specs=[
                pl.BlockSpec((1, count, width), lambda i, *unused: (i, 0, 0)),
                pl.BlockSpec((2, count, half), lambda i, *unused: (0, 0, 0)),
            ],
        ),
        out_shape=[
            jax.ShapeDtypeStruct((parts, count, width), BF16),
            jax.ShapeDtypeStruct((2, count, half), BF16),
        ],
        compiler_params=PARAMS,
        name="project",
    )(mine_at, rows_in, gain, bias, mine, other, add)


def finish_kernel(
    wsh_ref,
    x_ref,
    gain_ref,
    dmid_ref,
    low_ref,
    grads_ref,
    mine_ref,
    other_ref,
    keep_ref,
    send_ref,
    cols_ref,
    out_ref,
    dgain_ref,
    dbias_ref,
    acc_ref,
):
    step = pl.program_id(0)
    mine_at = wsh_ref[0]
    grads = grads_ref[0]
    keep_ref[0] = dot_inner(low_ref[mine_at], grads).astype(BF16)
    send_ref[0] = dot_inner(low_ref[1 - mine_at], grads).astype(BF16)
    cols_ref[0] = jnp.sum(grads.astype(F32), axis=0, keepdims=True)

    @pl.when(step == 0)
    def _():
        acc_ref[...] = jnp.zeros_like(acc_ref)

    acc_ref[mine_at] += dot_transposed(grads, mine_ref[0])
    acc_ref[1 - mine_at] += dot_transposed(grads, other_ref[0])

    @pl.when(step == pl.num_programs(0) - 1)
    def _():
        unused, normed, scaled = norm_forward(x_ref[...].astype(F32), 1.0, 0.0)
        upstream = jnp.concatenate([acc_ref[0], acc_ref[1]], axis=1)
        result, dgain, dbias = norm_backward(upstream, normed, scaled, gain_ref[...])
        out_ref[...] = dmid_ref[...] + result
        dgain_ref[...] = dgain
        dbias_ref[...] = dbias


def finish(mine_at, rows_in, gain, dmid, low, grads, mine, other):
    parts, half, width = mine.shape
    count, model = rows_in.shape
    whole = lambda i, *unused: (0, 0)
    each = lambda i, *unused: (i, 0, 0)
    return pl.pallas_call(
        finish_kernel,
        grid_spec=pltpu.PrefetchScalarGridSpec(
            num_scalar_prefetch=1,
            grid=(parts,),
            in_specs=[
                pl.BlockSpec((count, model), whole),
                pl.BlockSpec((1, model), whole),
                pl.BlockSpec((count, model), whole),
                pl.BlockSpec((2, count, half), lambda i, *unused: (0, 0, 0)),
                pl.BlockSpec((1, count, width), each),
                pl.BlockSpec((1, half, width), each),
                pl.BlockSpec((1, half, width), each),
            ],
            out_specs=[
                pl.BlockSpec((1, half, width), each),
                pl.BlockSpec((1, half, width), each),
                pl.BlockSpec((1, 1, width), each),
                pl.BlockSpec((count, model), whole),
                pl.BlockSpec((1, model), whole),
                pl.BlockSpec((1, model), whole),
            ],
            scratch_shapes=[pltpu.VMEM((2, count, half), F32)],
        ),
        out_shape=[
            jax.ShapeDtypeStruct((parts, half, width), BF16),
            jax.ShapeDtypeStruct((parts, half, width), BF16),
            jax.ShapeDtypeStruct((parts, 1, width), F32),
            jax.ShapeDtypeStruct((count, model), F32),
            jax.ShapeDtypeStruct((1, model), F32),
            jax.ShapeDtypeStruct((1, model), F32),
        ],
        compiler_params=PARAMS,
        name="finish",
    )(mine_at, rows_in, gain, dmid, low, grads, mine, other)


def head_columns(block, kind, head, heads):
    at = (kind * heads + head) * HEAD
    return block[:, at : at + HEAD]


def sorted_rows(stripe, source, half, span):
    return source * stripe if half == 0 else span + (HP - 1 - source) * stripe


def load_queries(packed_ref, target_ref, heads, kind, scaled):
    stripe = packed_ref.shape[2]
    span = HP * stripe
    for source in range(HP):
        for half in range(2):
            at = sorted_rows(stripe, source, half, span)
            block = packed_ref[source, half]
            for head in range(heads):
                part = head_columns(block, kind, head, heads)
                if scaled:
                    part = part * jnp.asarray(HEAD**-0.5, BF16)
                target_ref[head, at : at + stripe, :] = part


def load_keys(rows_of, total, stripe, heads, keys_ref, values_ref, turned_ref, turned_kind):
    for block_at in range(total // stripe):
        block = rows_of(block_at)
        at = block_at * stripe
        for head in range(heads):
            keys_ref[head, at : at + stripe, :] = head_columns(block, 0, head, heads)
            values_ref[head, at : at + stripe, :] = head_columns(block, 1, head, heads)
    source_ref = keys_ref if turned_kind == 0 else values_ref
    for chunk in range(total // TILE):
        for head in range(heads):
            turned_ref[head, chunk] = source_ref[
                head, chunk * TILE : (chunk + 1) * TILE, :
            ].T


def local_rows(packed_ref):
    stripe = packed_ref.shape[2]

    def rows_of(block_at):
        if block_at < HP:
            return packed_ref[block_at, 0]
        return packed_ref[2 * HP - 1 - block_at, 1]

    return rows_of


def remote_rows(prompts_ref, halo_ref):
    parts = prompts_ref.shape[0]
    halo_blocks = halo_ref.shape[0]

    def rows_of(block_at):
        if block_at < parts * HP:
            return prompts_ref[block_at // HP, block_at % HP]
        return halo_ref[halo_blocks - 1 - (block_at - parts * HP)]

    return rows_of


def row_slice(index, size=TILE):
    return pl.ds(pl.multiple_of(index * size, size), size)


def tile_iotas():
    return (
        lax.broadcasted_iota(jnp.int32, (TILE, TILE), 0),
        lax.broadcasted_iota(jnp.int32, (TILE, TILE), 1),
    )


def forward_step(query_tile, chunk, subs, mask, refs, heads):
    queries_ref, keys_ref, turned_ref, top_ref, sum_ref, acc_ref = refs
    for head in range(heads):
        query = queries_ref[head, row_slice(query_tile), :]
        scores = []
        for sub in range(subs):
            part = dot_transposed(keys_ref[head, row_slice(chunk + sub), :], query)
            if mask is not None:
                part = jnp.where(mask, part, NEGATIVE)
            scores.append(part)
        old = top_ref[query_tile, head]
        new = old
        for part in scores:
            new = jnp.maximum(new, jnp.max(part, axis=0, keepdims=True))
        alpha = jnp.exp(old - new)
        total = sum_ref[query_tile, head] * alpha
        acc = acc_ref[query_tile, head] * alpha
        for sub, part in enumerate(scores):
            soft = jnp.exp(part - new)
            total = total + jnp.sum(soft, axis=0, keepdims=True)
            acc = acc + dot_plain(turned_ref[head, chunk + sub], soft.astype(BF16))
        top_ref[query_tile, head] = new
        sum_ref[query_tile, head] = total
        acc_ref[query_tile, head] = acc


def loop(first, last, step):
    def run(index, unused):
        step(index)
        return unused

    lax.fori_loop(first, last, run, 0)


def walk_local(tiles, scalars_ref, starts_ref, step):
    wide = 2 if tiles % 2 == 0 else 1

    def prompt_tile(tile):
        loop(0, tile, lambda chunk: step(tile, chunk, 1, None))
        down, across = tile_iotas()
        step(tile, tile, 1, down <= across)

    def cont_tile(tile):
        query_tile = tiles + tile
        loop(0, tiles // wide, lambda chunk: step(query_tile, chunk * wide, wide, None))

        def band(chunk):
            down, across = tile_iotas()
            shifted = down + (chunk - tile) * TILE
            begin = starts_ref[tile] - tile * TILE
            mask = (shifted <= across) & (shifted >= begin)
            step(query_tile, tiles + chunk, 1, mask)

        loop(scalars_ref[tile], tile + 1, band)

    loop(0, tiles, prompt_tile)
    loop(0, tiles, cont_tile)


def walk_remote(tiles, parts, halo_tiles, scalars_ref, starts_ref, step, done):
    wide = 2 if tiles % 2 == 0 else 1

    def whole(query_tile, part):
        loop(
            0,
            tiles // wide,
            lambda chunk: step(query_tile, part * tiles + chunk * wide, wide, None),
        )

    def prompt_tile(tile):
        for part in range(parts):

            @pl.when(scalars_ref[2 * tiles + part] > 0)
            def _():
                whole(tile, part)

        done(tile, False)

    def cont_tile(tile):
        query_tile = tiles + tile
        for part in range(parts):
            whole(query_tile, part)

        def band(chunk):
            down, unused = tile_iotas()
            shifted = down + (chunk - halo_tiles) * TILE
            step(query_tile, parts * tiles + chunk, 1, shifted >= starts_ref[tile])

        loop(scalars_ref[tiles + tile], halo_tiles, band)
        done(query_tile, True)

    loop(0, tiles, prompt_tile)
    loop(0, tiles, cont_tile)


def forward_local_kernel(
    scalars_ref,
    starts_ref,
    packed_ref,
    top_ref,
    sum_ref,
    acc_ref,
    queries_ref,
    keys_ref,
    values_ref,
    turned_ref,
):
    heads = queries_ref.shape[0]
    stripe = packed_ref.shape[2]
    span = HP * stripe
    load_queries(packed_ref, queries_ref, heads, 2, True)
    load_keys(
        local_rows(packed_ref), 2 * span, stripe, heads, keys_ref, values_ref, turned_ref, 1
    )
    top_ref[...] = jnp.full(top_ref.shape, NEGATIVE, F32)
    sum_ref[...] = jnp.zeros(sum_ref.shape, F32)
    acc_ref[...] = jnp.zeros(acc_ref.shape, F32)
    refs = (queries_ref, keys_ref, turned_ref, top_ref, sum_ref, acc_ref)
    walk_local(
        span // TILE,
        scalars_ref,
        starts_ref,
        lambda tile, chunk, subs, mask: forward_step(tile, chunk, subs, mask, refs, heads),
    )


def store_rows(out_ref, block, query_tile, continued, columns):
    stripe = out_ref.shape[2]
    per = TILE // stripe
    tiles = HP // per
    for piece in range(per):
        rows = block[piece * stripe : (piece + 1) * stripe, :]
        if continued:
            source = HP - 1 - ((query_tile - tiles) * per + piece)
            out_ref[source, 1, :, columns] = rows
        else:
            out_ref[query_tile * per + piece, 0, :, columns] = rows


def forward_remote_kernel(
    scalars_ref,
    starts_ref,
    packed_ref,
    prompts_ref,
    halo_ref,
    top_in_ref,
    sum_in_ref,
    acc_in_ref,
    out_ref,
    log_ref,
    mixed_ref,
    queries_ref,
    keys_ref,
    values_ref,
    turned_ref,
    top_ref,
    sum_ref,
    acc_ref,
):
    heads = queries_ref.shape[0]
    stripe = packed_ref.shape[2]
    span = HP * stripe
    parts = prompts_ref.shape[0]
    halo = halo_ref.shape[0] * stripe
    load_queries(packed_ref, queries_ref, heads, 2, True)
    load_keys(
        remote_rows(prompts_ref, halo_ref),
        parts * span + halo,
        stripe,
        heads,
        keys_ref,
        values_ref,
        turned_ref,
        1,
    )
    top_ref[...] = top_in_ref[...]
    sum_ref[...] = sum_in_ref[...]
    acc_ref[...] = acc_in_ref[...]
    refs = (queries_ref, keys_ref, turned_ref, top_ref, sum_ref, acc_ref)

    def done(query_tile, continued):
        mixed = []
        for head in range(heads):
            total = sum_ref[query_tile, head]
            part = acc_ref[query_tile, head] / total
            log_ref[query_tile, head] = top_ref[query_tile, head] + jnp.log(total)
            mixed_ref[query_tile, head] = part
            mixed.append(part)
        block = jnp.concatenate(mixed, axis=0).T.astype(BF16)
        store_rows(out_ref, block, query_tile, continued, slice(None))

    walk_remote(
        span // TILE,
        parts,
        halo // TILE,
        scalars_ref,
        starts_ref,
        lambda tile, chunk, subs, mask: forward_step(tile, chunk, subs, mask, refs, heads),
        done,
    )


def forward_local(scalars, starts, packed, heads):
    stripe = packed.shape[2]
    span = HP * stripe
    tiles = 2 * span // TILE
    return pl.pallas_call(
        forward_local_kernel,
        in_specs=[SMEM_SPEC] + vmem_specs(2),
        out_specs=vmem_specs(3),
        out_shape=[
            jax.ShapeDtypeStruct((tiles, heads, 1, TILE), F32),
            jax.ShapeDtypeStruct((tiles, heads, 1, TILE), F32),
            jax.ShapeDtypeStruct((tiles, heads, HEAD, TILE), F32),
        ],
        scratch_shapes=[
            pltpu.VMEM((heads, 2 * span, HEAD), BF16),
            pltpu.VMEM((heads, 2 * span, HEAD), BF16),
            pltpu.VMEM((heads, 2 * span, HEAD), BF16),
            pltpu.VMEM((heads, tiles, HEAD, TILE), BF16),
        ],
        compiler_params=PARAMS,
        name="forward_local",
    )(scalars, starts, packed)


def forward_remote(scalars, starts, packed, prompts, halo, state, heads):
    stripe = packed.shape[2]
    span = HP * stripe
    tiles = 2 * span // TILE
    rows = prompts.shape[0] * span + halo.shape[0] * stripe
    return pl.pallas_call(
        forward_remote_kernel,
        in_specs=[SMEM_SPEC] + vmem_specs(7),
        out_specs=vmem_specs(3),
        out_shape=[
            jax.ShapeDtypeStruct((HP, 2, stripe, heads * HEAD), BF16),
            jax.ShapeDtypeStruct((tiles, heads, 1, TILE), F32),
            jax.ShapeDtypeStruct((tiles, heads, HEAD, TILE), F32),
        ],
        scratch_shapes=[
            pltpu.VMEM((heads, 2 * span, HEAD), BF16),
            pltpu.VMEM((heads, rows, HEAD), BF16),
            pltpu.VMEM((heads, rows, HEAD), BF16),
            pltpu.VMEM((heads, rows // TILE, HEAD, TILE), BF16),
            pltpu.VMEM((tiles, heads, 1, TILE), F32),
            pltpu.VMEM((tiles, heads, 1, TILE), F32),
            pltpu.VMEM((tiles, heads, HEAD, TILE), F32),
        ],
        compiler_params=PARAMS,
        name="forward_remote",
    )(scalars, starts, packed, prompts, halo, *state)


def backward_step(query_tile, chunk, subs, mask, refs, heads):
    (
        queries_ref,
        ups_ref,
        keys_ref,
        values_ref,
        turned_ref,
        log_ref,
        delta_ref,
        dquery_ref,
        dkeys_ref,
        dvalues_ref,
    ) = refs
    for head in range(heads):
        query = queries_ref[head, row_slice(query_tile), :]
        ups = ups_ref[head, row_slice(query_tile), :]
        logsum = log_ref[query_tile, head]
        delta = delta_ref[query_tile, head]
        dquery = dquery_ref[query_tile, head]
        for sub in range(subs):
            rows = row_slice(chunk + sub)
            scores = dot_transposed(keys_ref[head, rows, :], query)
            grad_soft = dot_transposed(values_ref[head, rows, :], ups)
            soft = jnp.exp(scores - logsum)
            if mask is not None:
                soft = jnp.where(mask, soft, 0.0)
            grad_scores = (soft * (grad_soft - delta)).astype(BF16)
            dvalues_ref[head, rows, :] += dot_plain(soft.astype(BF16), ups)
            dkeys_ref[head, rows, :] += dot_plain(grad_scores, query)
            dquery = dquery + dot_plain(turned_ref[head, chunk + sub], grad_scores)
        dquery_ref[query_tile, head] = dquery


def key_grad_rows(dkeys_ref, dvalues_ref, at, stripe, heads):
    pieces = [dkeys_ref[head, at : at + stripe, :] for head in range(heads)]
    pieces = pieces + [dvalues_ref[head, at : at + stripe, :] for head in range(heads)]
    return jnp.concatenate(pieces, axis=1).astype(BF16)


def backward_remote_kernel(
    scalars_ref,
    starts_ref,
    packed_ref,
    ups_in_ref,
    prompts_ref,
    halo_ref,
    log_ref,
    mixed_ref,
    dprompts_ref,
    dhalo_ref,
    dquery_ref,
    delta_ref,
    queries_ref,
    ups_ref,
    keys_ref,
    values_ref,
    turned_ref,
    dkeys_ref,
    dvalues_ref,
):
    heads = queries_ref.shape[0]
    stripe = packed_ref.shape[2]
    span = HP * stripe
    parts = prompts_ref.shape[0]
    halo_blocks = halo_ref.shape[0]
    halo = halo_blocks * stripe
    load_queries(packed_ref, queries_ref, heads, 2, True)
    load_queries(ups_in_ref, ups_ref, heads, 0, False)
    load_keys(
        remote_rows(prompts_ref, halo_ref),
        parts * span + halo,
        stripe,
        heads,
        keys_ref,
        values_ref,
        turned_ref,
        0,
    )
    for query_tile in range(2 * span // TILE):
        for head in range(heads):
            ups = ups_ref[head, query_tile * TILE : (query_tile + 1) * TILE, :]
            delta_ref[query_tile, head] = jnp.sum(
                ups.T.astype(F32) * mixed_ref[query_tile, head], axis=0, keepdims=True
            )
    dquery_ref[...] = jnp.zeros(dquery_ref.shape, F32)
    dkeys_ref[...] = jnp.zeros(dkeys_ref.shape, F32)
    dvalues_ref[...] = jnp.zeros(dvalues_ref.shape, F32)
    refs = (
        queries_ref,
        ups_ref,
        keys_ref,
        values_ref,
        turned_ref,
        log_ref,
        delta_ref,
        dquery_ref,
        dkeys_ref,
        dvalues_ref,
    )
    walk_remote(
        span // TILE,
        parts,
        halo // TILE,
        scalars_ref,
        starts_ref,
        lambda tile, chunk, subs, mask: backward_step(tile, chunk, subs, mask, refs, heads),
        lambda tile, continued: None,
    )
    for block_at in range(parts * HP):
        dprompts_ref[block_at // HP, block_at % HP] = key_grad_rows(
            dkeys_ref, dvalues_ref, block_at * stripe, stripe, heads
        )
    for block_at in range(halo_blocks):
        dhalo_ref[halo_blocks - 1 - block_at] = key_grad_rows(
            dkeys_ref, dvalues_ref, parts * span + block_at * stripe, stripe, heads
        )


def backward_local_kernel(
    scalars_ref,
    starts_ref,
    packed_ref,
    ups_in_ref,
    log_ref,
    delta_ref,
    dquery_in_ref,
    out_ref,
    queries_ref,
    ups_ref,
    keys_ref,
    values_ref,
    turned_ref,
    dquery_ref,
    dkeys_ref,
    dvalues_ref,
):
    heads = queries_ref.shape[0]
    stripe = packed_ref.shape[2]
    span = HP * stripe
    width = heads * HEAD
    load_queries(packed_ref, queries_ref, heads, 2, True)
    load_queries(ups_in_ref, ups_ref, heads, 0, False)
    load_keys(
        local_rows(packed_ref), 2 * span, stripe, heads, keys_ref, values_ref, turned_ref, 0
    )
    dquery_ref[...] = dquery_in_ref[...]
    dkeys_ref[...] = jnp.zeros(dkeys_ref.shape, F32)
    dvalues_ref[...] = jnp.zeros(dvalues_ref.shape, F32)
    refs = (
        queries_ref,
        ups_ref,
        keys_ref,
        values_ref,
        turned_ref,
        log_ref,
        delta_ref,
        dquery_ref,
        dkeys_ref,
        dvalues_ref,
    )
    walk_local(
        span // TILE,
        scalars_ref,
        starts_ref,
        lambda tile, chunk, subs, mask: backward_step(tile, chunk, subs, mask, refs, heads),
    )
    for source in range(HP):
        for half in range(2):
            at = sorted_rows(stripe, source, half, span)
            out_ref[source, half, :, : 2 * width] = key_grad_rows(
                dkeys_ref, dvalues_ref, at, stripe, heads
            )
    pad = out_ref.shape[3] - 3 * width
    for query_tile in range(2 * span // TILE):
        turned = jnp.concatenate([dquery_ref[query_tile, head] for head in range(heads)], axis=0)
        block = (turned * HEAD**-0.5).T
        if pad:
            block = jnp.concatenate([block, jnp.zeros((TILE, pad), F32)], axis=1)
        store_rows(
            out_ref,
            block.astype(BF16),
            query_tile,
            query_tile >= span // TILE,
            slice(2 * width, None),
        )


def backward_remote(scalars, starts, packed, ups, prompts, halo, logsum, mixed, heads):
    stripe = packed.shape[2]
    span = HP * stripe
    tiles = 2 * span // TILE
    rows = prompts.shape[0] * span + halo.shape[0] * stripe
    return pl.pallas_call(
        backward_remote_kernel,
        in_specs=[SMEM_SPEC] + vmem_specs(7),
        out_specs=vmem_specs(4),
        out_shape=[
            jax.ShapeDtypeStruct(prompts.shape, BF16),
            jax.ShapeDtypeStruct(halo.shape, BF16),
            jax.ShapeDtypeStruct((tiles, heads, HEAD, TILE), F32),
            jax.ShapeDtypeStruct((tiles, heads, 1, TILE), F32),
        ],
        scratch_shapes=[
            pltpu.VMEM((heads, 2 * span, HEAD), BF16),
            pltpu.VMEM((heads, 2 * span, HEAD), BF16),
            pltpu.VMEM((heads, rows, HEAD), BF16),
            pltpu.VMEM((heads, rows, HEAD), BF16),
            pltpu.VMEM((heads, rows // TILE, HEAD, TILE), BF16),
            pltpu.VMEM((heads, rows, HEAD), F32),
            pltpu.VMEM((heads, rows, HEAD), F32),
        ],
        compiler_params=PARAMS,
        name="backward_remote",
    )(scalars, starts, packed, ups, prompts, halo, logsum, mixed)


def backward_local(scalars, starts, packed, ups, logsum, delta, dquery, heads):
    stripe = packed.shape[2]
    span = HP * stripe
    tiles = 2 * span // TILE
    rows = 2 * span
    return pl.pallas_call(
        backward_local_kernel,
        in_specs=[SMEM_SPEC] + vmem_specs(6),
        out_specs=vmem_specs(1)[0],
        out_shape=jax.ShapeDtypeStruct(packed.shape, BF16),
        scratch_shapes=[
            pltpu.VMEM((heads, rows, HEAD), BF16),
            pltpu.VMEM((heads, rows, HEAD), BF16),
            pltpu.VMEM((heads, rows, HEAD), BF16),
            pltpu.VMEM((heads, rows, HEAD), BF16),
            pltpu.VMEM((heads, tiles, HEAD, TILE), BF16),
            pltpu.VMEM((tiles, heads, HEAD, TILE), F32),
            pltpu.VMEM((heads, rows, HEAD), F32),
            pltpu.VMEM((heads, rows, HEAD), F32),
        ],
        compiler_params=PARAMS,
        name="backward_local",
    )(scalars, starts, packed, ups, logsum, delta, dquery)


def gather_pair(shard, axis):
    ways = lax.axis_size("wsh")
    if ways == 2:
        other = lax.ppermute(shard, "wsh", [(0, 1), (1, 0)])
        return (shard, other, lax.axis_index("wsh"))
    whole = lax.all_gather(shard, "wsh", axis=axis, tiled=True)
    first, second = jnp.split(whole, 2, axis=axis)
    return (first, second, jnp.zeros((), jnp.int32))


def scatter_rows(keep, send):
    ways = lax.axis_size("wsh")
    if ways == 2:
        got = lax.ppermute(send, "wsh", [(0, 1), (1, 0)])
        return (keep.astype(F32) + got.astype(F32)).astype(BF16)
    whole = jnp.concatenate([keep, send], axis=-2)
    return lax.psum_scatter(whole, "wsh", scatter_dimension=whole.ndim - 2, tiled=True)


def reduce_parts(parts, axis="ctx"):
    ways = lax.axis_size(axis)
    bits = ways.bit_length() - 1
    index = lax.axis_index(axis)
    rest = tuple(range(3, bits))
    orders = [(0, 1, 2) + rest, (1, 2, 0) + rest, (2, 0, 1) + rest]
    parts = list(parts)

    def traded(value, bit):
        return lax.ppermute(value, axis, [(i, i ^ (1 << bit)) for i in range(ways)])

    for step in range(bits):
        for at in range(len(parts)):
            bit = orders[at % 3][step]
            flag = (index >> bit) & 1
            count = parts[at].shape[0] // 2
            keep = lax.dynamic_slice_in_dim(parts[at], flag * count, count, 0)
            send = lax.dynamic_slice_in_dim(parts[at], (1 - flag) * count, count, 0)
            got = traded(send, bit)
            parts[at] = (keep.astype(F32) + got.astype(F32)).astype(BF16)
    for step in reversed(range(bits)):
        for at in range(len(parts)):
            bit = orders[at % 3][step]
            flag = (index >> bit) & 1
            mine = parts[at]
            got = traded(mine, bit)
            parts[at] = jnp.where(
                flag == 0,
                jnp.concatenate([mine, got], axis=0),
                jnp.concatenate([got, mine], axis=0),
            )
    return parts


def own_half(value, at, axis=0):
    count = value.shape[axis] // 2
    keep = lax.dynamic_slice_in_dim(value, at * count, count, axis)
    send = lax.dynamic_slice_in_dim(value, (1 - at) * count, count, axis)
    return keep, send


def body(
    tokens,
    cont_lengths,
    grad_out,
    ln_gain_one,
    ln_bias_one,
    w_query,
    b_query,
    w_key,
    w_value,
    b_value,
    w_out,
    b_out,
    ln_gain_two,
    ln_bias_two,
    w_in,
    b_in,
    w_back,
    b_back,
):
    groups, rows, model = tokens.shape
    ways = lax.axis_size("ctx")
    shards = lax.axis_size("wsh")
    wsh_at = lax.axis_index("wsh")
    parts = ways // HP
    stripe = rows // 2
    span = HP * stripe
    tiles = span // TILE
    heads = HEADS * groups // HP
    triples = HEADS // heads
    width = heads * HEAD
    packed_width = -(-3 * width // 128) * 128
    pad = packed_width - 3 * width
    count = groups * rows
    hidden_size = w_in.shape[1]
    my_ctx = lax.axis_index("ctx")
    part_at = my_ctx // HP
    group_at = (my_ctx % HP) % groups

    small_rows = [ln_gain_one, ln_bias_one, b_query, b_value, b_out, ln_gain_two, ln_bias_two]
    small_rows = small_rows + [b_back, b_in]
    shard_width = model // shards
    small = jnp.concatenate([row.reshape(-1, shard_width) for row in small_rows], axis=0)
    small = lax.all_gather(small, "wsh", axis=0, tiled=False) if shards != 2 else None or (
        lambda mine: (
            lambda got: jnp.where(wsh_at == 0, jnp.stack([mine, got]), jnp.stack([got, mine]))
        )(lax.ppermute(mine, "wsh", [(0, 1), (1, 0)]))
    )(small)
    vectors = [small[:, at].reshape(1, model).astype(F32) for at in range(8)]
    gain_one, bias_one, query_b, value_b, out_b, gain_two, bias_two, back_b = vectors
    in_b = small[:, 8:].reshape(1, hidden_size).astype(F32)

    def by_triple(value):
        return value.reshape(value.shape[0], triples, width).transpose(1, 0, 2)

    stacked = [by_triple(w_key), by_triple(w_value), by_triple(w_query)]
    stacked_b = [jnp.zeros((triples, 1, width), F32), by_triple(value_b), by_triple(query_b)]
    if pad:
        stacked.append(jnp.zeros((triples, w_key.shape[0], pad), BF16))
        stacked_b.append(jnp.zeros((triples, 1, pad), F32))
    stacked = jnp.concatenate(stacked, axis=2)
    stacked_b = jnp.concatenate(stacked_b, axis=2)
    first_w, second_w, first_at = gather_pair(stacked, 1)
    at_vector = first_at.reshape(1)
    out_w = lax.all_gather(w_out, "wsh", axis=0, tiled=True)
    in_w = lax.all_gather(w_in, "wsh", axis=0, tiled=True)
    back_w = lax.all_gather(w_back, "wsh", axis=0, tiled=True)

    token_rows = tokens.reshape(count, model)
    packed, low_one = project(
        at_vector, token_rows, gain_one, bias_one, first_w, second_w, stacked_b
    )
    cube = [[part * HP + at for at in range(HP)] for part in range(parts)]

    def exchange(value):
        return lax.all_to_all(value, "ctx", 0, 0, axis_index_groups=cube)

    packed = exchange(packed.reshape(HP, rows, packed_width)).reshape(HP, 2, stripe, packed_width)

    lengths = lax.dynamic_index_in_dim(cont_lengths, group_at, 0, keepdims=False)
    seg_ends = jnp.cumsum(lengths, dtype=jnp.int32)
    chunk_start = (parts - 1 - part_at) * span
    places = chunk_start + jnp.arange(span, dtype=jnp.int32)
    begins = jnp.max(
        jnp.where(seg_ends[None, :] <= places[:, None], seg_ends[None, :], 0), axis=1
    )
    starts = (begins - chunk_start).reshape(tiles, 1, TILE)
    halo_rows = min(MOSTLEN, span)
    halo_tiles = halo_rows // TILE
    halo_blocks = halo_rows // stripe
    first_start = starts[:, 0, 0]
    local_first = jnp.maximum(first_start, 0) // TILE
    has_halo = part_at < parts - 1
    halo_first = jnp.where(
        has_halo, jnp.clip(first_start + halo_rows, 0, halo_rows) // TILE, halo_tiles
    )
    seen = [(part_at >= shift).astype(jnp.int32).reshape(1) for shift in range(1, parts)]
    scalars = jnp.concatenate([local_first, halo_first] + seen).astype(jnp.int32)

    def shifted(value, shift):
        pairs = [
            (part * HP + at, ((part + shift) % parts) * HP + at)
            for part in range(parts)
            for at in range(HP)
        ]
        return lax.ppermute(value, "ctx", pairs)

    def to_former(value):
        pairs = [(i, i - HP) for i in range(HP, ways)]
        return lax.ppermute(value, "ctx", pairs)

    def to_latter(value):
        pairs = [(i, i + HP) for i in range(ways - HP)]
        return lax.ppermute(value, "ctx", pairs)

    own_prompts = packed[:, 0, :, : 2 * width]
    prompts = jnp.stack([shifted(own_prompts, shift) for shift in range(1, parts)])
    halo = to_former(packed[:halo_blocks, 1, :, : 2 * width])
    state = forward_local(scalars, starts, packed, heads)
    mixed_rows, logsum, mixed = forward_remote(
        scalars, starts, packed, prompts, halo, state, heads
    )

    def to_tokens(value):
        back = exchange(value.reshape(HP, rows, width)).reshape(triples, count, width)
        return back.transpose(1, 0, 2).reshape(count, model)

    def to_heads(value):
        split = value.reshape(count, triples, width).transpose(1, 0, 2)
        return exchange(split.reshape(HP, rows, width)).reshape(HP, 2, stripe, width)

    low_attended = to_tokens(mixed_rows)

    inputs = token_rows.astype(F32)
    middle = inputs + dot_plain(low_attended, out_w) + out_b
    normed_two, hat_two, scale_two = norm_forward(middle, gain_two, bias_two)
    low_two = normed_two.astype(BF16)
    hidden_pre = dot_plain(low_two, in_w) + in_b
    hidden, gelu_back = jax.vjp(exact_gelu, hidden_pre)
    low_hidden = hidden.astype(BF16)
    result = middle + dot_plain(low_hidden, back_w) + back_b
    out_tokens = result.astype(BF16).reshape(groups, rows, model)
    upstream_low = grad_out.reshape(count, model)
    upstream = upstream_low.astype(F32)
    grad_back_w = dot_inner(low_hidden, upstream_low).astype(BF16)
    grad_back_b = jnp.sum(upstream, axis=0, keepdims=True)
    grad_hidden = dot_transposed(upstream_low, back_w)
    grad_pre = gelu_back(grad_hidden)[0].astype(BF16)
    grad_in_w = dot_inner(low_two, grad_pre).astype(BF16)
    grad_in_b = jnp.sum(grad_pre.astype(F32), axis=0, keepdims=True)
    grad_normed_two = dot_transposed(grad_pre, in_w)
    grad_mid_norm, grad_gain_two, grad_bias_two = norm_backward(
        grad_normed_two, hat_two, scale_two, gain_two
    )
    grad_middle = upstream + grad_mid_norm
    grad_branch = grad_middle.astype(BF16)
    grad_out_w = dot_inner(low_attended, grad_branch).astype(BF16)
    grad_out_b = jnp.sum(grad_branch.astype(F32), axis=0, keepdims=True)
    grad_attended = dot_transposed(grad_branch, out_w).astype(BF16)

    ups = to_heads(grad_attended)
    dprompts, dhalo, dquery, delta = backward_remote(
        scalars, starts, packed, ups, prompts, halo, logsum, mixed, heads
    )
    returned = sum(
        shifted(dprompts[shift - 1], parts - shift).astype(F32) for shift in range(1, parts)
    )
    returned_halo = to_latter(dhalo).astype(F32)
    dpacked = backward_local(scalars, starts, packed, ups, logsum, delta, dquery, heads)
    extra = jnp.zeros((HP, 2, stripe, packed_width), F32)
    extra = extra.at[:, 0, :, : 2 * width].set(returned)
    extra = extra.at[:halo_blocks, 1, :, : 2 * width].set(returned_halo)
    dpacked = (dpacked.astype(F32) + extra).astype(BF16)

    blocks = hidden_size // model

    def to_blocks(value):
        split = value.reshape(value.shape[0], blocks, model)
        return split.transpose(1, 0, 2).reshape(-1, model)

    small_mid = jnp.concatenate(
        [grad_out_b, grad_gain_two, grad_bias_two, grad_back_b, grad_in_b.reshape(-1, model)],
        axis=0,
    )
    shard_rows = model // shards
    mid_rows = (2 * blocks + 1) * shard_rows
    mid_total = -(-(mid_rows + 8) // 512) * 512
    if shards == 2:
        keep_in, send_in = own_half(grad_in_w, wsh_at)
        keep_back, send_back = own_half(grad_back_w, wsh_at)
        keep_out, send_out = own_half(grad_out_w, wsh_at)
        filler = jnp.zeros((mid_total - mid_rows - small_mid.shape[0], model), BF16)
        tail = [small_mid.astype(BF16), filler]
        mid_keep = jnp.concatenate([to_blocks(keep_in), keep_back, keep_out] + tail, axis=0)
        mid_send = jnp.concatenate([to_blocks(send_in), send_back, send_out] + tail, axis=0)
        mid_sum = scatter_rows(mid_keep, mid_send)
    else:
        scattered = [
            lax.psum_scatter(part, "wsh", scatter_dimension=0, tiled=True)
            for part in (grad_in_w, grad_back_w, grad_out_w)
        ]
        small_sum = lax.psum(small_mid.astype(BF16), "wsh")
        filler = jnp.zeros((mid_total - mid_rows - small_mid.shape[0], model), BF16)
        mid_sum = jnp.concatenate(
            [to_blocks(scattered[0]), scattered[1], scattered[2], small_sum, filler], axis=0
        )
    third = mid_total // 3 // 256 * 256
    cuts = [third + 256 * (mid_total // 256 - 3 * (third // 256) > at) for at in range(3)]
    edges = [0, cuts[0], cuts[0] + cuts[1], mid_total]
    mid_parts = reduce_parts([mid_sum[edges[at] : edges[at + 1]] for at in range(3)])
    mid_done = jnp.concatenate(mid_parts, axis=0)

    grads = exchange(dpacked.reshape(HP, rows, packed_width)).reshape(triples, count, packed_width)
    keep, send, columns, grad_rows, grad_gain_one, grad_bias_one = finish(
        at_vector, token_rows, gain_one, grad_middle, low_one, grads, first_w, second_w
    )
    small_last = jnp.concatenate(
        [
            columns.reshape(triples, packed_width),
            jnp.pad(
                jnp.concatenate([grad_gain_one, grad_bias_one], axis=0),
                ((0, 0), (0, 2 * packed_width - model)),
            ).reshape(4, packed_width),
        ],
        axis=0,
    ).astype(BF16)
    last_rows = triples * shard_rows
    last_total = -(-(last_rows + 8) // 128) * 128
    filler = jnp.zeros((last_total - last_rows - small_last.shape[0], packed_width), BF16)
    if shards == 2:
        tail = [small_last, filler]
        last_sum = scatter_rows(
            jnp.concatenate([keep.reshape(last_rows, packed_width)] + tail, axis=0),
            jnp.concatenate([send.reshape(last_rows, packed_width)] + tail, axis=0),
        )
    else:
        scattered = scatter_rows(keep, send).reshape(last_rows, packed_width)
        last_sum = jnp.concatenate([scattered, lax.psum(small_last, "wsh"), filler], axis=0)
    third = last_total // 3 // 128 * 128
    cuts = [third + 128 * (last_total // 128 - 3 * (third // 128) > at) for at in range(3)]
    edges = [0, cuts[0], cuts[0] + cuts[1], last_total]
    last_parts = reduce_parts([last_sum[edges[at] : edges[at + 1]] for at in range(3)])
    last_done = jnp.concatenate(last_parts, axis=0)

    def own(vector):
        size = vector.shape[0] // shards
        return lax.dynamic_slice_in_dim(vector, wsh_at * size, size, 0).astype(F32)

    at = blocks * shard_rows
    new_in_w = mid_done[:at].reshape(blocks, shard_rows, model).transpose(1, 0, 2)
    new_in_w = new_in_w.reshape(shard_rows, hidden_size).astype(F32)
    new_back_w = mid_done[at : 2 * at].astype(F32)
    new_out_w = mid_done[2 * at : mid_rows].astype(F32)
    tail = mid_done[mid_rows : mid_rows + 4 + blocks]
    new_out_b, new_gain_two, new_bias_two, new_back_b = [own(tail[i]) for i in range(4)]
    new_in_b = own(tail[4:].reshape(hidden_size))

    last_w = last_done[:last_rows].reshape(triples, shard_rows, packed_width)
    tail = last_done[last_rows : last_rows + triples + 4]

    def untriple(kind):
        piece = last_w[:, :, kind * width : (kind + 1) * width]
        return piece.transpose(1, 0, 2).reshape(shard_rows, model).astype(F32)

    def unvector(kind):
        return own(tail[:triples, kind * width : (kind + 1) * width].reshape(model))

    new_key_w, new_value_w, new_query_w = [untriple(kind) for kind in range(3)]
    new_value_b, new_query_b = unvector(1), unvector(2)
    new_gain_one = own(tail[triples : triples + 2].reshape(-1)[:model])
    new_bias_one = own(tail[triples + 2 :].reshape(-1)[:model])
    return (
        out_tokens,
        grad_rows.reshape(groups, rows, model),
        new_gain_one,
        new_bias_one,
        new_query_w,
        new_query_b,
        new_key_w,
        new_value_w,
        new_value_b,
        new_out_w,
        new_out_b,
        new_gain_two,
        new_bias_two,
        new_in_w,
        new_in_b,
        new_back_w,
        new_back_b,
    )


def solution(mesh):
    placed = (
        P("wsh", "ctx", None),
        P("wsh", None),
        P("wsh", "ctx", None),
        P("wsh"),
        P("wsh"),
        P("wsh", None),
        P("wsh"),
        P("wsh", None),
        P("wsh", None),
        P("wsh"),
        P("wsh", None),
        P("wsh"),
        P("wsh"),
        P("wsh"),
        P("wsh", None),
        P("wsh"),
        P("wsh", None),
        P("wsh"),
    )
    return jax.shard_map(
        body,
        mesh=mesh,
        in_specs=placed,
        out_specs=(
            P("wsh", "ctx", None),
            P("wsh", "ctx", None),
            P("wsh"),
            P("wsh"),
            P("wsh", None),
            P("wsh"),
            P("wsh", None),
            P("wsh", None),
            P("wsh"),
            P("wsh", None),
            P("wsh"),
            P("wsh"),
            P("wsh"),
            P("wsh", None),
            P("wsh"),
            P("wsh", None),
            P("wsh"),
        ),
        check_vma=False,
    )
```

time: 1480 us -> 657 us (0.44)
  waiting for transfers between devices: 741 us -> 153 us
  matrix products: 402 us -> 51.9 us
  Pallas kernels: 0 us -> 125 us
  starting transfers between devices: 0.77 us -> 113 us
  blocking collectives: 101 us -> 16 us
  other arithmetic: 116 us -> 51.4 us
  local copies, waits for them, and re-layouts: 86 us -> 124 us
    dot_general x26 -> x3, matrix products: 355 us -> 16.6 us  [dot_plain(): return jnp.dot(left_side, right_side, preferred_element_type=F32)]
    reduce_scatter x8 -> x0, waiting for transfers between devices: 313 us -> none  [the longest x2 243 us: body(): lax.psum_scatter(term.astype(jnp.bfloat16), 'ctx', scatter_dimension=1, t...]
    all_gather x10 -> x3, waiting for transfers between devices: 297 us -> 0.04 us  [the longest x1 0.02 us: body(): out_w = lax.all_gather(w_out, 'wsh', axis=0, tiled=True)]
    psum x1 -> x0, waiting for transfers between devices: 126 us -> none  [body(): lax.psum(shortened(shares), 'ctx')]
    pallas_call x0 -> x6, Pallas kernels: none -> 125 us  [the longest x1 35.8 us: backward_local(): pl.pallas_call(backward_local_kernel, in_specs=[SMEM_SPEC] + vmem_specs(6...]
    ppermute x0 -> x56, waiting for transfers between devices: none -> 109 us  [the longest x48 90.2 us: traded(): return lax.ppermute(value, axis, [(i, i ^ 1 << bit) for i in range(ways)])]
    ppermute x0 -> x56, starting transfers between devices: none -> 94.4 us  [the longest x48 67.8 us: traded(): return lax.ppermute(value, axis, [(i, i ^ 1 << bit) for i in range(ways)])]
    psum x1 -> x0, blocking collectives: 80.4 us -> none  [body(): lax.psum(shortened(shares), 'ctx')]
  transfers between devices with their start and end apart: 19 -> 62, of which waited for: 14 -> 27; matrix products, arithmetic and copies ran while one was open for 29% -> 19% of each run, Pallas kernels for 0% -> 19%
where the time goes in v1:
time: 657 us; the launch traced here: 650 us
  waiting for transfers between devices  153 us (23%)
  Pallas kernels  125 us (19%)
  local copies, waits for them, and re-layouts  124 us (19%)
  starting transfers between devices  113 us (17%)
  matrix products  51.9 us (8%)
  other arithmetic  51.4 us (8%)
  blocking collectives  16 us (2%)
  between operations  15.5 us (2%)
    ppermute x48, waiting for transfers between devices, traded(): return lax.ppermute(value, axis, [(i, i ^ 1 << bit) for i in range(ways)])  90.2 us
    ppermute x48, starting transfers between devices, traded(): return lax.ppermute(value, axis, [(i, i ^ 1 << bit) for i in range(ways)])  67.8 us
    all_to_all x3, waiting for transfers between devices, exchange(): return lax.all_to_all(value, 'ctx', 0, 0, axis_index_groups=cube)  42.2 us
    pallas_call x1, Pallas kernels, backward_local(): pl.pallas_call(backward_local_kernel, in_specs=[SMEM_SPEC] + vmem_specs(6...  35.8 us
    pallas_call x1, Pallas kernels, forward_local(): pl.pallas_call(forward_local_kernel, in_specs=[SMEM_SPEC] + vmem_specs(2)...  31.5 us
    dot_general x3, matrix products, dot_transposed(): lax.dot_general(left_side, right_side, (((1,), (1,)), ((), ())), preferre...  24.7 us
    concatenate x1, local copies, waits for them, and re-layouts, body(): jnp.concatenate([to_blocks(send_in), send_back, send_out] + tail, axis=0)  24.6 us
    ppermute x2, starting transfers between devices, shifted(): return lax.ppermute(value, 'ctx', pairs)  22.4 us
  transfers between devices with their start and end apart: 62, of which 27 were waited for; matrix products, arithmetic and copies ran while one was open for 19% of the time, Pallas kernels for 19%

profile of v1, /device:TPU:0, one launch (start us, length us, event | category | flops | bytes accessed | tf_op | source)
XLA Modules:
  0.0 649.9 jit_solution(142760678391375010)
XLA Ops:
  20.3 7.4 %project.1 = (bf16[4,512,640]{2,1,0:T(8,128)(2,1)}, bf16[2,512,384]{2,1,0:T(8,128)(2,1)}) custom-call(s32[1]{0:T(128)} %bitcast.5.wsh_ref, bf16[512,768]{1,0:T(8,128)(2,1)} %bitcast.111, f32[1,768]{1,0:T(1,128)} %convert.76.gain_ref, f32[1,768]{1,0:T(1,128)} %convert.77.bias_ref, bf16[4,384,640]{2,1,0:T(8,128)(2,1)} %copy-done.3, ...), custom_call_target="tpu_custom_call" | custom-call | tf_op jit(solution)/shard_map/project/pallas_call | solution.py:92
  27.7 6.1 all-to-all-start
  34.9 30.6 %all-to-all-done = bf16[8,256,640]{2,1,0:T(8,128)(2,1)S(1)} async-done(((bf16[8,256,640]{2,1,0:T(8,128)(2,1)}), bf16[8,256,640]{2,1,0:T(8,128)(2,1)S(1)}, u32[]{:S(2)}, u32[]{:S(2)}) %all-to-all-start) | async-done | bytes 2621472 | tf_op jit(solution)/shard_map/all_to_all | solution.py:904
  71.0 31.5 %forward_local.1 = (f32[8,3,1,256]{3,2,1,0:T(1,128)}, f32[8,3,1,256]{3,2,1,0:T(1,128)}, f32[8,3,64,256]{3,2,1,0:T(8,128)}) custom-call(s32[9]{0:T(128)} %pad_add_fusion.scalars_ref, s32[4,1,256]{2,1,0:T(1,128)} %bitcast.134, bf16[8,2,128,640]{3,2,1,0:T(8,128)(2,1)} %bitcast.94), custom_call_target="tpu_custom_call" | custom-call | tf_op jit(solution)/shard_map/forward_local/pallas_call | solution.py:480
  102.5 16.4 %collective-permute-done.3.halo_ref = bf16[4,128,384]{2,1,0:T(8,128)(2,1)S(1)} collective-permute-done((bf16[4,128,384]{2,1,0:T(8,128)(2,1)S(1)}, bf16[4,128,384]{2,1,0:T(8,128)(2,1)S(1)}, u32[]{:S(2)}, u32[]{:S(2)}) %collective-permute-start.3) | collective-permute-done | bytes 393248 | tf_op jit(solution)/shard_map/ppermute | solution.py:938
  119.8 17.0 %forward_remote.1 = (bf16[8,2,128,192]{3,2,1,0:T(8,128)(2,1)}, f32[8,3,1,256]{3,2,1,0:T(1,128)}, f32[8,3,64,256]{3,2,1,0:T(8,128)}) custom-call(s32[9]{0:T(128)} %pad_add_fusion.scalars_ref, s32[4,1,256]{2,1,0:T(1,128)} %bitcast.135, bf16[8,2,128,640]{3,2,1,0:T(8,128)(2,1)} %bitcast.95, bf16[1,8,128,384]{3,2,1,0:T(8,128)(2,1)} %bitcast.118, ...), custom_call_target="tpu_custom_call" | custom-call | tf_op jit(solution)/shard_map/forward_remote/pallas_call | solution.py:505
  139.1 8.5 %all-to-all-start.1 = ((bf16[8,256,192]{1,2,0:T(8,128)(2,1)}), bf16[8,256,192]{1,2,0:T(8,128)(2,1)S(1)}, u32[]{:S(2)}, u32[]{:S(2)}) async-start(bf16[8,256,192]{1,2,0:T(8,128)(2,1)} %copy.107), calls=%async_computation.1 | async-start | bytes 1572864 | tf_op jit(solution)/shard_map/all_to_all | solution.py:904
  147.9 11.6 %all-to-all-done.1 = bf16[8,256,192]{1,2,0:T(8,128)(2,1)S(1)} async-done(((bf16[8,256,192]{1,2,0:T(8,128)(2,1)}), bf16[8,256,192]{1,2,0:T(8,128)(2,1)S(1)}, u32[]{:S(2)}, u32[]{:S(2)}) %all-to-all-start.1) | async-done | bytes 786464 | tf_op jit(solution)/shard_map/all_to_all | solution.py:904
  163.5 7.3 %fusion.27 = f32[512,3072]{1,0:T(8,128)} fusion(bf16[768,3072]{1,0:T(8,128)(2,1)} %all-gather.6.cloned.1.call-done, f32[512,768]{1,0:T(8,128)S(1)} %get-tuple-element.188, f32[768]{0:T(1024)S(1)} %reshape.515, f32[768]{0:T(1024)S(1)} %reshape.514, f32[512]{0:T(512)S(1)} %add_rsqrt_fusion, f32[512]{0:T(512)S(1)} %broadcast_multiply_fusion.2), kind=kOutput, calls=%fused_computation.186 | convolution fusion | flops 2417885184 | bytes 12593152 | tf_op jit(solution)/shard_map/dot_general | solution.py:22
  170.8 19.6 %fusion.28 = (bf16[3072]{0:T(1024)(128)(2,1)S(1)}, bf16[512,3072]{1,0:T(8,128)(2,1)}, f32[512,3072]{1,0:T(8,128)S(1)}) fusion(f32[512,3072]{1,0:T(8,128)} %fusion.27, f32[3072]{0:T(1024)S(1)} %reshape.516, bf16[512,768]{1,0:T(8,128)(2,1)S(1)} %bitcast.120, bf16[3072,768]{1,0:T(8,128)(2,1)} %all-gather.8.cloned.1.call-done), kind=kOutput, calls=%fused_computation.187 | convolution fusion | flops 2532307968 | bytes 21252096 | tf_op jit(solution)/shard_map/dot_general | solution.py:32
  193.6 5.4 convolution_convert_fusion.1
  207.4 4.3 convolution_convert_fusion
  220.4 4.9 constant_dynamic-slice_fusion.20
  225.2 24.6 %concatenate.228 = bf16[3584,768]{1,0:T(8,128)(2,1)} concatenate(bf16[1536,768]{1,0:T(8,128)(2,1)} %bitcast.106, bf16[1536,768]{1,0:T(8,128)(2,1)} %get-tuple-element.165, bf16[384,768]{1,0:T(8,128)(2,1)S(1)} %get-tuple-element.180, bf16[1,768]{1,0:T(2,128)(2,1)S(1)} %broadcast_in_dim.59, bf16[1,768]{1,0:T(2,128)(2,1)S(1)} %broadcast_in_dim.60, ...), dimensions={0} | concatenate | bytes 11010048 | tf_op jit(solution)/shard_map/concatenate | solution.py:1023
  253.2 16.0 %all_to_all.20 = bf16[8,256,192]{1,2,0:T(8,128)(2,1)S(1)} all-to-all(bf16[8,256,192]{1,2,0:T(8,128)(2,1)S(1)} %copy.112), channel_id=1, replica_groups={{0,2,4,6,8,10,12,14},{16,18,20,22,24,26,28,30},{1,3,5,7,9,11,13,15},{17..., dimensions={0} | all-to-all | bytes 1572864 | tf_op jit(solution)/shard_map/all_to_all | solution.py:904
  270.5 21.1 %backward_remote.1 = (bf16[1,8,128,384]{3,2,1,0:T(8,128)(2,1)}, bf16[4,128,384]{2,1,0:T(8,128)(2,1)}, f32[8,3,64,256]{3,2,1,0:T(8,128)}, f32[8,3,1,256]{3,2,1,0:T(1,128)}) custom-call(s32[9]{0:T(128)} %pad_add_fusion.scalars_ref, s32[4,1,256]{2,1,0:T(1,128)} %bitcast.136, bf16[8,2,128,640]{3,2,1,0:T(8,128)(2,1)} %bitcast.96, ...), custom_call_target="tpu_custom_call" | custom-call | tf_op jit(solution)/shard_map/backward_remote/pallas_call | solution.py:720
  291.6 19.8 %collective-permute-start.4 = (bf16[8,128,384]{2,1,0:T(8,128)(2,1)}, bf16[8,128,384]{2,1,0:T(8,128)(2,1)}, u32[]{:S(2)}, u32[]{:S(2)}) collective-permute-start(bf16[8,128,384]{2,1,0:T(8,128)(2,1)} %bitcast.146), channel_id=1, source_target_pairs={{0,16},{2,18},{4,20},{6,22},{8,24},{10,26},{12,28},{14,30},{16,0},... | collective-permute-start | bytes 2359304 | tf_op jit(solution)/shard_map/ppermute | solution.py:934
  316.1 4.5 copy.118
  320.5 20.2 %concatenate.227 = bf16[3584,768]{1,0:T(8,128)(2,1)} concatenate(bf16[1536,768]{1,0:T(8,128)(2,1)} %bitcast.105, bf16[1536,768]{1,0:T(8,128)(2,1)S(1)} %copy-done.8, bf16[384,768]{1,0:T(8,128)(2,1)S(1)} %get-tuple-element.179, bf16[1,768]{1,0:T(2,128)(2,1)S(1)} %broadcast_in_dim.59, bf16[1,768]{1,0:T(2,128)(2,1)S(1)} %broadcast_in_dim.60, bf16[1,768]{1,0:T(2,128)(2,1)S(1)} %broadcast_in_dim.61, ...), dimensions={0} | concatenate | bytes 11010048 | tf_op jit(solution)/shard_map/concatenate | solution.py:1022
  340.8 35.8 %backward_local.1 = bf16[8,2,128,640]{3,2,1,0:T(8,128)(2,1)} custom-call(s32[9]{0:T(128)} %pad_add_fusion.scalars_ref, s32[4,1,256]{2,1,0:T(1,128)} %bitcast.137, bf16[8,2,128,640]{3,2,1,0:T(8,128)(2,1)} %bitcast.97, bf16[8,2,128,192]{3,2,1,0:T(8,128)(2,1)} %bitcast.101, f32[8,3,1,256]{3,2,1,0:T(1,128)} %get-tuple-element.65.log_ref, ...), custom_call_target="tpu_custom_call" | custom-call | tf_op jit(solution)/shard_map/backward_local/pallas_call | solution.py:749
  384.9 5.6 add_convert_fusion
  402.4 28.0 %collective-permute-done.32 = bf16[512,768]{1,0:T(8,128)(2,1)S(1)} collective-permute-done((bf16[512,768]{1,0:T(8,128)(2,1)}, bf16[512,768]{1,0:T(8,128)(2,1)S(1)}, u32[]{:S(2)}, u32[]{:S(2)}) %collective-permute-start.32) | collective-permute-done | bytes 786464 | tf_op jit(solution)/shard_map/ppermute | solution.py:797
  437.9 6.0 collective-permute-done.33
  455.0 12.6 %finish.1 = (bf16[4,384,640]{2,1,0:T(8,128)(2,1)}, bf16[4,384,640]{2,1,0:T(8,128)(2,1)}, f32[4,1,640]{2,1,0:T(1,128)}, f32[512,768]{1,0:T(8,128)}, f32[1,768]{1,0:T(1,128)}, /*index=5*/f32[1,768]{1,0:T(1,128)}) custom-call(s32[1]{0:T(128)} %bitcast.5.wsh_ref, bf16[512,768]{1,0:T(8,128)(2,1)} %bitcast.112, f32[1,768]{1,0:T(1,128)} %convert.76.gain_ref, ...), custom_call_target="tpu_custom_call" | custom-call | tf_op jit(solution)/shard_map/finish/pallas_call | solution.py:165
  479.7 4.8 collective-permute-done.42
  484.9 5.5 collective-permute-done.51
  494.6 6.9 %concatenate.201 = bf16[1664,640]{1,0:T(8,128)(2,1)} concatenate(bf16[1536,640]{1,0:T(8,128)(2,1)S(1)} %bitcast.130, bf16[4,640]{1,0:T(4,128)(2,1)S(1)} %bitcast.139, bf16[4,640]{1,0:T(4,128)(2,1)S(1)} %reshape.495, bf16[120,640]{1,0:T(8,128)(2,1)S(1)} %broadcast_in_dim.58), dimensions={0} | concatenate | bytes 4259840 | tf_op jit(solution)/shard_map/concatenate | solution.py:1062
  510.4 5.2 collective-permute-start.54
  515.8 6.9 %add_convert_fusion.7 = bf16[512,768]{1,0:T(8,128)(2,1)} fusion(f32[512,768]{1,0:T(8,128)S(1)} %copy-done.15, bf16[512,3072]{1,0:T(8,128)(2,1)} %multiply_convert_fusion, bf16[3072,768]{1,0:T(8,128)(2,1)} %all-gather.8.cloned.1.call-done, f32[768]{0:T(1024)S(1)} %reshape.517), kind=kOutput, calls=%fused_computation.42 | convolution fusion | flops 2417098752 | bytes 10226688 | tf_op jit(solution)/shard_map/dot_general | solution.py:22
  522.7 10.5 %concatenate.200 = bf16[1664,640]{1,0:T(8,128)(2,1)} concatenate(bf16[1536,640]{1,0:T(8,128)(2,1)} %bitcast.129, bf16[4,640]{1,0:T(4,128)(2,1)S(1)} %bitcast.140, bf16[4,640]{1,0:T(4,128)(2,1)S(1)} %reshape.495, bf16[120,640]{1,0:T(8,128)(2,1)S(1)} %broadcast_in_dim.58), dimensions={0} | concatenate | bytes 4259840 | tf_op jit(solution)/shard_map/concatenate | solution.py:1061
  533.2 7.9 %collective-permute-done.54 = bf16[320,768]{1,0:T(8,128)(2,1)S(1)} collective-permute-done((bf16[320,768]{1,0:T(8,128)(2,1)S(1)}, bf16[320,768]{1,0:T(8,128)(2,1)S(1)}, u32[]{:S(2)}, u32[]{:S(2)}) %collective-permute-start.54) | collective-permute-done | bytes 491552 | tf_op jit(solution)/shard_map/ppermute | solution.py:797
  560.0 6.3 collective-permute-done.55
  (417 shorter events, 215.6 us)
Async XLA Ops:
  7.2 153.4 %all-gather.4.cloned.1.call-start = ((), (), s32[]{:S(2)}) async-start(), calls=%async_computation.4 | async-start | bytes 1769472 | tf_op jit(solution)/shard_map/all_gather | solution.py:893
  13.9 149.6 %all-gather.6.cloned.1.call-start = ((), (), s32[]{:S(2)}) async-start(), calls=%async_computation.5 | async-start | bytes 7077888 | tf_op jit(solution)/shard_map/all_gather | solution.py:894
  27.7 37.9 %all-to-all-start = ((bf16[8,256,640]{2,1,0:T(8,128)(2,1)}), bf16[8,256,640]{2,1,0:T(8,128)(2,1)S(1)}, u32[]{:S(2)}, u32[]{:S(2)}) async-start(bf16[8,256,640]{2,1,0:T(8,128)(2,1)} %bitcast.125), calls=%async_computation | async-start | bytes 5242880 | tf_op jit(solution)/shard_map/all_to_all | solution.py:904
  33.8 136.9 %all-gather.8.cloned.1.call-start = ((), (), s32[]{:S(2)}) async-start(), calls=%async_computation.6 | async-start | bytes 7077888 | tf_op jit(solution)/shard_map/all_gather | solution.py:895
  65.7 53.2 %collective-permute-start.2 = (bf16[8,128,384]{2,1,0:T(8,128)(2,1)S(1)}, bf16[8,128,384]{2,1,0:T(8,128)(2,1)S(1)}, u32[]{:S(2)}, u32[]{:S(2)}) collective-permute-start(bf16[8,128,384]{2,1,0:T(8,128)(2,1)S(1)} %slice_bitcast_fusion), channel_id=1, source_target_pairs={{0,16},{2,18},{4,20},{6,22},{8,24},{10,26},{12,28},{14,30},{16,0},... | collective-permute-start | bytes 2359304 | tf_op jit(solution)/shard_map/ppermute | solution.py:934
  68.5 50.3 %collective-permute-start.3 = (bf16[4,128,384]{2,1,0:T(8,128)(2,1)S(1)}, bf16[4,128,384]{2,1,0:T(8,128)(2,1)S(1)}, u32[]{:S(2)}, u32[]{:S(2)}) collective-permute-start(bf16[4,128,384]{2,1,0:T(8,128)(2,1)S(1)} %slice_bitcast_fusion.1), channel_id=1, source_target_pairs={{16,0},{18,2},{20,4},{22,6},{24,8},{26,10},{28,12},{30,14},{17,1},... | collective-permute-start | bytes 1179656 | tf_op jit(solution)/shard_map/ppermute | solution.py:938
  139.1 20.3 %all-to-all-start.1 = ((bf16[8,256,192]{1,2,0:T(8,128)(2,1)}), bf16[8,256,192]{1,2,0:T(8,128)(2,1)S(1)}, u32[]{:S(2)}, u32[]{:S(2)}) async-start(bf16[8,256,192]{1,2,0:T(8,128)(2,1)} %copy.107), calls=%async_computation.1 | async-start | bytes 1572864 | tf_op jit(solution)/shard_map/all_to_all | solution.py:904
  249.9 135.1 %collective-permute-start.31 = (bf16[3584,768]{1,0:T(8,128)(2,1)}, bf16[3584,768]{1,0:T(8,128)(2,1)}, u32[]{:S(2)}, u32[]{:S(2)}) collective-permute-start(bf16[3584,768]{1,0:T(8,128)(2,1)} %concatenate.228), channel_id=1, source_target_pairs={{0,1},{1,0},{2,3},{3,2},{4,5},{5,4},{6,7},{7,6},{8,9},{9,8},{10,11... | collective-permute-start | bytes 16515080 | tf_op jit(solution)/shard_map/ppermute | solution.py:782
  291.6 85.0 %collective-permute-start.4 = (bf16[8,128,384]{2,1,0:T(8,128)(2,1)}, bf16[8,128,384]{2,1,0:T(8,128)(2,1)}, u32[]{:S(2)}, u32[]{:S(2)}) collective-permute-start(bf16[8,128,384]{2,1,0:T(8,128)(2,1)} %bitcast.146), channel_id=1, source_target_pairs={{0,16},{2,18},{4,20},{6,22},{8,24},{10,26},{12,28},{14,30},{16,0},... | collective-permute-start | bytes 2359304 | tf_op jit(solution)/shard_map/ppermute | solution.py:934
  311.4 66.9 %collective-permute-start.5 = (bf16[4,128,384]{2,1,0:T(8,128)(2,1)}, bf16[4,128,384]{2,1,0:T(8,128)(2,1)S(1)}, u32[]{:S(2)}, u32[]{:S(2)}) collective-permute-start(bf16[4,128,384]{2,1,0:T(8,128)(2,1)} %get-tuple-element.70), channel_id=1, source_target_pairs={{0,16},{2,18},{4,20},{6,22},{8,24},{10,26},{12,28},{14,30},{1,17},... | collective-permute-start | bytes 1179656 | tf_op jit(solution)/shard_map/ppermute | solution.py:942
  380.8 72.7 %all-to-all-start.3 = ((bf16[8,256,640]{2,1,0:T(8,128)(2,1)}), bf16[8,256,640]{2,1,0:T(8,128)(2,1)S(1)}, u32[]{:S(2)}, u32[]{:S(2)}) async-start(bf16[8,256,640]{2,1,0:T(8,128)(2,1)} %bitcast.33), calls=%async_computation.3 | async-start | bytes 5242880 | tf_op jit(solution)/shard_map/all_to_all | solution.py:904
  392.1 38.3 %collective-permute-start.32 = (bf16[512,768]{1,0:T(8,128)(2,1)}, bf16[512,768]{1,0:T(8,128)(2,1)S(1)}, u32[]{:S(2)}, u32[]{:S(2)}) collective-permute-start(bf16[512,768]{1,0:T(8,128)(2,1)} %constant_dynamic-slice_fusion.15), channel_id=1, source_target_pairs={{0,8},{2,10},{4,12},{6,14},{8,0},{10,2},{12,4},{14,6},{16,24},{18,... | collective-permute-start | bytes 2359304 | tf_op jit(solution)/shard_map/ppermute | solution.py:797
  397.9 38.0 %collective-permute-start.48 = (bf16[640,768]{1,0:T(8,128)(2,1)}, bf16[640,768]{1,0:T(8,128)(2,1)}, u32[]{:S(2)}, u32[]{:S(2)}) collective-permute-start(bf16[640,768]{1,0:T(8,128)(2,1)} %constant_dynamic-slice_fusion.4), channel_id=1, source_target_pairs={{0,4},{2,6},{4,0},{6,2},{8,12},{10,14},{12,8},{14,10},{16,20},{18,... | collective-permute-start | bytes 2949128 | tf_op jit(solution)/shard_map/ppermute | solution.py:797
  400.9 44.8 %collective-permute-start.40 = (bf16[640,768]{1,0:T(8,128)(2,1)S(1)}, bf16[640,768]{1,0:T(8,128)(2,1)S(1)}, u32[]{:S(2)}, u32[]{:S(2)}) collective-permute-start(bf16[640,768]{1,0:T(8,128)(2,1)S(1)} %constant_dynamic-slice_fusion.8), channel_id=1, source_target_pairs={{0,2},{2,0},{4,6},{6,4},{8,10},{10,8},{12,14},{14,12},{16,18},{18,... | collective-permute-start | bytes 2949128 | tf_op jit(solution)/shard_map/ppermute | solution.py:797
  430.6 13.3 %collective-permute-start.33 = (bf16[256,768]{1,0:T(8,128)(2,1)S(1)}, bf16[256,768]{1,0:T(8,128)(2,1)S(1)}, u32[]{:S(2)}, u32[]{:S(2)}) collective-permute-start(bf16[256,768]{1,0:T(8,128)(2,1)S(1)} %constant_dynamic-slice_fusion.14), channel_id=1, source_target_pairs={{0,2},{2,0},{4,6},{6,4},{8,10},{10,8},{12,14},{14,12},{16,18},{18,... | collective-permute-start | bytes 1179656 | tf_op jit(solution)/shard_map/ppermute | solution.py:797
  437.5 33.8 %collective-permute-start.49 = (bf16[320,768]{1,0:T(8,128)(2,1)S(1)}, bf16[320,768]{1,0:T(8,128)(2,1)}, u32[]{:S(2)}, u32[]{:S(2)}) collective-permute-start(bf16[320,768]{1,0:T(8,128)(2,1)S(1)} %constant_dynamic-slice_fusion.3), channel_id=1, source_target_pairs={{0,8},{2,10},{4,12},{6,14},{8,0},{10,2},{12,4},{14,6},{16,24},{18,... | collective-permute-start | bytes 1474568 | tf_op jit(solution)/shard_map/ppermute | solution.py:797
  450.2 18.8 %collective-permute-start.35 = (bf16[64,768]{1,0:T(8,128)(2,1)S(1)}, bf16[64,768]{1,0:T(8,128)(2,1)S(1)}, u32[]{:S(2)}, u32[]{:S(2)}) collective-permute-start(bf16[64,768]{1,0:T(8,128)(2,1)S(1)} %constant_dynamic-slice_fusion.12), channel_id=1, source_target_pairs={{0,16},{2,18},{4,20},{6,22},{8,24},{10,26},{12,28},{14,30},{16,0},... | collective-permute-start | bytes 294920 | tf_op jit(solution)/shard_map/ppermute | solution.py:797
  452.1 22.5 %collective-permute-start.41 = (bf16[320,768]{1,0:T(8,128)(2,1)}, bf16[320,768]{1,0:T(8,128)(2,1)}, u32[]{:S(2)}, u32[]{:S(2)}) collective-permute-start(bf16[320,768]{1,0:T(8,128)(2,1)} %constant_dynamic-slice_fusion.7), channel_id=1, source_target_pairs={{0,4},{2,6},{4,0},{6,2},{8,12},{10,14},{12,8},{14,10},{16,20},{18,... | collective-permute-start | bytes 1474568 | tf_op jit(solution)/shard_map/ppermute | solution.py:797
  479.0 11.5 %collective-permute-start.51 = (bf16[80,768]{1,0:T(8,128)(2,1)S(1)}, bf16[80,768]{1,0:T(8,128)(2,1)S(1)}, u32[]{:S(2)}, u32[]{:S(2)}) collective-permute-start(bf16[80,768]{1,0:T(8,128)(2,1)S(1)} %constant_dynamic-slice_fusion.1), channel_id=1, source_target_pairs={{0,16},{2,18},{4,20},{6,22},{8,24},{10,26},{12,28},{14,30},{16,0},... | collective-permute-start | bytes 368648 | tf_op jit(solution)/shard_map/ppermute | solution.py:797
  484.8 22.4 %collective-permute-start.38 = (bf16[256,768]{1,0:T(8,128)(2,1)S(1)}, bf16[256,768]{1,0:T(8,128)(2,1)S(1)}, u32[]{:S(2)}, u32[]{:S(2)}) collective-permute-start(bf16[256,768]{1,0:T(8,128)(2,1)S(1)} %maximum_select_fusion.12), channel_id=1, source_target_pairs={{0,2},{2,0},{4,6},{6,4},{8,10},{10,8},{12,14},{14,12},{16,18},{18,... | collective-permute-start | bytes 1179656 | tf_op jit(solution)/shard_map/ppermute | solution.py:797
  501.5 51.5 %collective-permute-start.6 = (bf16[1664,640]{1,0:T(8,128)(2,1)}, bf16[1664,640]{1,0:T(8,128)(2,1)}, u32[]{:S(2)}, u32[]{:S(2)}) collective-permute-start(bf16[1664,640]{1,0:T(8,128)(2,1)} %concatenate.201), channel_id=1, source_target_pairs={{0,1},{1,0},{2,3},{3,2},{4,5},{5,4},{6,7},{7,6},{8,9},{9,8},{10,11... | collective-permute-start | bytes 6389768 | tf_op jit(solution)/shard_map/ppermute | solution.py:782
  503.7 11.9 %collective-permute-start.45 = (bf16[160,768]{1,0:T(8,128)(2,1)S(1)}, bf16[160,768]{1,0:T(8,128)(2,1)S(1)}, u32[]{:S(2)}, u32[]{:S(2)}) collective-permute-start(bf16[160,768]{1,0:T(8,128)(2,1)S(1)} %maximum_select_fusion.15), channel_id=1, source_target_pairs={{0,8},{2,10},{4,12},{6,14},{8,0},{10,2},{12,4},{14,6},{16,24},{18,... | collective-permute-start | bytes 737288 | tf_op jit(solution)/shard_map/ppermute | solution.py:797
  507.5 38.1 %collective-permute-start.39 = (bf16[512,768]{1,0:T(8,128)(2,1)S(1)}, bf16[512,768]{1,0:T(8,128)(2,1)}, u32[]{:S(2)}, u32[]{:S(2)}) collective-permute-start(bf16[512,768]{1,0:T(8,128)(2,1)S(1)} %maximum_select_fusion.6), channel_id=1, source_target_pairs={{0,8},{2,10},{4,12},{6,14},{8,0},{10,2},{12,4},{14,6},{16,24},{18,... | collective-permute-start | bytes 2359304 | tf_op jit(solution)/shard_map/ppermute | solution.py:797
  510.4 30.7 %collective-permute-start.54 = (bf16[320,768]{1,0:T(8,128)(2,1)S(1)}, bf16[320,768]{1,0:T(8,128)(2,1)S(1)}, u32[]{:S(2)}, u32[]{:S(2)}) collective-permute-start(bf16[320,768]{1,0:T(8,128)(2,1)S(1)} %maximum_select_fusion.10), channel_id=1, source_target_pairs={{0,8},{2,10},{4,12},{6,14},{8,0},{10,2},{12,4},{14,6},{16,24},{18,... | collective-permute-start | bytes 1474568 | tf_op jit(solution)/shard_map/ppermute | solution.py:797
  515.7 26.2 %collective-permute-start.46 = (bf16[320,768]{1,0:T(8,128)(2,1)S(1)}, bf16[320,768]{1,0:T(8,128)(2,1)}, u32[]{:S(2)}, u32[]{:S(2)}) collective-permute-start(bf16[320,768]{1,0:T(8,128)(2,1)S(1)} %maximum_select_fusion.9), channel_id=1, source_target_pairs={{0,4},{2,6},{4,0},{6,2},{8,12},{10,14},{12,8},{14,10},{16,20},{18,... | collective-permute-start | bytes 1474568 | tf_op jit(solution)/shard_map/ppermute | solution.py:797
  541.5 24.8 %collective-permute-start.55 = (bf16[640,768]{1,0:T(8,128)(2,1)S(1)}, bf16[640,768]{1,0:T(8,128)(2,1)}, u32[]{:S(2)}, u32[]{:S(2)}) collective-permute-start(bf16[640,768]{1,0:T(8,128)(2,1)S(1)} %maximum_select_fusion.4), channel_id=1, source_target_pairs={{0,4},{2,6},{4,0},{6,2},{8,12},{10,14},{12,8},{14,10},{16,20},{18,... | collective-permute-start | bytes 2949128 | tf_op jit(solution)/shard_map/ppermute | solution.py:797
  543.8 24.8 %collective-permute-start.47 = (bf16[640,768]{1,0:T(8,128)(2,1)S(1)}, bf16[640,768]{1,0:T(8,128)(2,1)}, u32[]{:S(2)}, u32[]{:S(2)}) collective-permute-start(bf16[640,768]{1,0:T(8,128)(2,1)S(1)} %maximum_select_fusion.3), channel_id=1, source_target_pairs={{0,2},{2,0},{4,6},{6,4},{8,10},{10,8},{12,14},{14,12},{16,18},{18,... | collective-permute-start | bytes 2949128 | tf_op jit(solution)/shard_map/ppermute | solution.py:797
  556.0 17.1 %collective-permute-start.7 = (bf16[256,640]{1,0:T(8,128)(2,1)S(1)}, bf16[256,640]{1,0:T(8,128)(2,1)S(1)}, u32[]{:S(2)}, u32[]{:S(2)}) collective-permute-start(bf16[256,640]{1,0:T(8,128)(2,1)S(1)} %constant_dynamic-slice_fusion.33), channel_id=1, source_target_pairs={{0,8},{2,10},{4,12},{6,14},{8,0},{10,2},{12,4},{14,6},{16,24},{18,... | collective-permute-start | bytes 983048 | tf_op jit(solution)/shard_map/ppermute | solution.py:797
  557.6 17.5 %collective-permute-start.23 = (bf16[256,640]{1,0:T(8,128)(2,1)S(1)}, bf16[256,640]{1,0:T(8,128)(2,1)S(1)}, u32[]{:S(2)}, u32[]{:S(2)}) collective-permute-start(bf16[256,640]{1,0:T(8,128)(2,1)S(1)} %constant_dynamic-slice_fusion.25), channel_id=1, source_target_pairs={{0,4},{2,6},{4,0},{6,2},{8,12},{10,14},{12,8},{14,10},{16,20},{18,... | collective-permute-start | bytes 983048 | tf_op jit(solution)/shard_map/ppermute | solution.py:797
  559.7 17.6 %collective-permute-start.15 = (bf16[320,640]{1,0:T(8,128)(2,1)S(1)}, bf16[320,640]{1,0:T(8,128)(2,1)S(1)}, u32[]{:S(2)}, u32[]{:S(2)}) collective-permute-start(bf16[320,640]{1,0:T(8,128)(2,1)S(1)} %constant_dynamic-slice_fusion.29), channel_id=1, source_target_pairs={{0,2},{2,0},{4,6},{6,4},{8,10},{10,8},{12,14},{14,12},{16,18},{18,... | collective-permute-start | bytes 1228808 | tf_op jit(solution)/shard_map/ppermute | solution.py:797
  577.4 16.3 %collective-permute-start.16 = (bf16[160,640]{1,0:T(8,128)(2,1)S(1)}, bf16[160,640]{1,0:T(8,128)(2,1)S(1)}, u32[]{:S(2)}, u32[]{:S(2)}) collective-permute-start(bf16[160,640]{1,0:T(8,128)(2,1)S(1)} %constant_dynamic-slice_fusion.28), channel_id=1, source_target_pairs={{0,4},{2,6},{4,0},{6,2},{8,12},{10,14},{12,8},{14,10},{16,20},{18,... | collective-permute-start | bytes 614408 | tf_op jit(solution)/shard_map/ppermute | solution.py:797
  607.3 13.7 %collective-permute-start.29 = (bf16[128,640]{1,0:T(8,128)(2,1)S(1)}, bf16[128,640]{1,0:T(8,128)(2,1)S(1)}, u32[]{:S(2)}, u32[]{:S(2)}) collective-permute-start(bf16[128,640]{1,0:T(8,128)(2,1)S(1)} %maximum_select_fusion.20), channel_id=1, source_target_pairs={{0,8},{2,10},{4,12},{6,14},{8,0},{10,2},{12,4},{14,6},{16,24},{18,... | collective-permute-start | bytes 491528 | tf_op jit(solution)/shard_map/ppermute | solution.py:797
  (82 other events, 745.2 us)
Sparse Core Ops, SparseCore 0:
  14.0 11.5 all-gather.3
  27.2 15.6 all-gather.5
  44.4 15.5 all-gather.7

commit v2 on v1

--- a/solution.py
+++ b/solution.py
@@ -34,10 +34,6 @@
     )
 
 
-def exact_gelu(values):
-    return jax.nn.gelu(values, approximate=False)
-
-
 def norm_forward(values, gain_vec, bias_vec):
     center = values - jnp.mean(values, axis=-1, keepdims=True)
     scaled = lax.rsqrt(jnp.mean(center * center, axis=-1, keepdims=True) + EPSILON)
@@ -67,136 +63,316 @@
 PARAMS = pltpu.CompilerParams(vmem_limit_bytes=56 << 20)
 
 
-def project_kernel(
-    wsh_ref, x_ref, gain_ref, bias_ref, mine_ref, other_ref, add_ref, out_ref, low_ref
-):
-    half = mine_ref.shape[1]
-    mine_at = wsh_ref[0]
+def whole_weight(at_ref, mine_ref, other_ref, weight_ref):
+    half = mine_ref.shape[0]
 
     @pl.when(pl.program_id(0) == 0)
     def _():
-        normed, unused, unused_two = norm_forward(
-            x_ref[...].astype(F32), gain_ref[...], bias_ref[...]
-        )
-        low_ref[0] = normed[:, :half].astype(BF16)
-        low_ref[1] = normed[:, half:].astype(BF16)
-
-    total = dot_plain(low_ref[mine_at], mine_ref[0]) + dot_plain(low_ref[1 - mine_at], other_ref[0])
-    out_ref[0] = (total + add_ref[0]).astype(BF16)
-
-
-def project(mine_at, rows_in, gain, bias, mine, other, add):
-    parts, half, width = mine.shape
-    count, model = rows_in.shape
+        weight_ref[pl.ds(pl.multiple_of(at_ref[0] * half, half), half), :] = mine_ref[...]
+        weight_ref[pl.ds(pl.multiple_of((1 - at_ref[0]) * half, half), half), :] = other_ref[...]
+
+
+def project_kernel(at_ref, low_ref, mine_ref, other_ref, add_ref, out_ref, weight_ref):
+    whole_weight(at_ref, mine_ref, other_ref, weight_ref)
+    step, rows, model = low_ref.shape
+    low = low_ref[...].reshape(step * rows, model)
+    total = dot_plain(low, weight_ref[...]) + add_ref[...]
+    out_ref[...] = total.astype(BF16).reshape(step, rows, total.shape[1])
+
+
+def project(at, low, mine, other, add):
+    sources, rows, model = low.shape
+    half, width = mine.shape
     whole = lambda i, *unused: (0, 0)
+    each = lambda i, *unused: (i, 0, 0)
     return pl.pallas_call(
         project_kernel,
         grid_spec=pltpu.PrefetchScalarGridSpec(
             num_scalar_prefetch=1,
-            grid=(parts,),
+            grid=(sources // 2,),
             in_specs=[
-                pl.BlockSpec((count, model), whole),
-                pl.BlockSpec((1, model), whole),
-                pl.BlockSpec((1, model), whole),
-                pl.BlockSpec((1, half, width), lambda i, *unused: (i, 0, 0)),
-                pl.BlockSpec((1, half, width), lambda i, *unused: (i, 0, 0)),
-                pl.BlockSpec((1, 1, width), lambda i, *unused: (i, 0, 0)),
+                pl.BlockSpec((2, rows, model), each),
+                pl.BlockSpec((half, width), whole),
+                pl.BlockSpec((half, width), whole),
+                pl.BlockSpec((1, width), whole),
+            ],
+            out_specs=pl.BlockSpec((2, rows, width), each),
+            scratch_shapes=[pltpu.VMEM((2 * half, width), BF16)],
+        ),
+        out_shape=jax.ShapeDtypeStruct((sources, rows, width), BF16),
+        compiler_params=PARAMS,
+        name="project",
+    )(at, low, mine, other, add)
+
+
+def unproject_kernel(
+    at_ref,
+    halo_ref,
+    low_ref,
+    packed_ref,
+    extra_ref,
+    extra_halo_ref,
+    mine_ref,
+    other_ref,
+    back_ref,
+    keep_ref,
+    send_ref,
+    cols_ref,
+    weight_ref,
+    acc_ref,
+):
+    whole_weight(at_ref, mine_ref, other_ref, weight_ref)
+    step = pl.program_id(0)
+    sources, halves, stripe, width = packed_ref.shape
+    part = extra_ref.shape[2]
+    half, unused = mine_ref.shape
+    pieces = []
+    for source in range(sources):
+        first = packed_ref[source, 0].astype(F32)
+        second = packed_ref[source, 1].astype(F32)
+        added = extra_halo_ref[source].astype(F32)
+        added = jnp.where(step * sources + source < halo_ref[0], added, 0.0)
+        first = jnp.concatenate([first[:, :part] + extra_ref[source].astype(F32), first[:, part:]], 1)
+        second = jnp.concatenate([second[:, :part] + added, second[:, part:]], 1)
+        pieces = pieces + [first, second]
+    grads = jnp.concatenate(pieces, axis=0).astype(BF16)
+    low = low_ref[...].reshape(grads.shape[0], low_ref.shape[2])
+    back = dot_transposed(grads, weight_ref[...]).astype(BF16)
+    back_ref[...] = back.reshape(back_ref.shape)
+    share = dot_inner(low, grads)
+    columns = jnp.sum(grads.astype(F32), axis=0, keepdims=True)
+
+    @pl.when(step == 0)
+    def _():
+        acc_ref[...] = share
+        cols_ref[...] = columns
+
+    @pl.when(step > 0)
+    def _():
+        acc_ref[...] += share
+        cols_ref[...] += columns
+
+    @pl.when(step == pl.num_programs(0) - 1)
+    def _():
+        own = pl.ds(pl.multiple_of(at_ref[0] * half, half), half)
+        rest = pl.ds(pl.multiple_of((1 - at_ref[0]) * half, half), half)
+        keep_ref[...] = acc_ref[own, :].astype(BF16)
+        send_ref[...] = acc_ref[rest, :].astype(BF16)
+
+
+def unproject(at, halo_count, low, packed, extra, extra_halo, mine, other):
+    sources, rows, model = low.shape
+    stripe = packed.shape[2]
+    half, width = mine.shape
+    part = extra.shape[2]
+    halo_steps = extra_halo.shape[0] // 2
+    whole = lambda i, *unused: (0, 0)
+    each = lambda i, *unused: (i, 0, 0)
+    return pl.pallas_call(
+        unproject_kernel,
+        grid_spec=pltpu.PrefetchScalarGridSpec(
+            num_scalar_prefetch=2,
+            grid=(sources // 2,),
+            in_specs=[
+                pl.BlockSpec((2, rows, model), each),
+                pl.BlockSpec((2, 2, stripe, width), lambda i, *unused: (i, 0, 0, 0)),
+                pl.BlockSpec((2, stripe, part), each),
+                pl.BlockSpec(
+                    (2, stripe, part),
+                    lambda i, *unused: (jnp.minimum(i, halo_steps - 1), 0, 0),
+                ),
+                pl.BlockSpec((half, width), whole),
+                pl.BlockSpec((half, width), whole),
             ],
             out_specs=[
-                pl.BlockSpec((1, count, width), lambda i, *unused: (i, 0, 0)),
-                pl.BlockSpec((2, count, half), lambda i, *unused: (0, 0, 0)),
+                pl.BlockSpec((2, rows, model), each),
+                pl.BlockSpec((half, width), whole),
+                pl.BlockSpec((half, width), whole),
+                pl.BlockSpec((1, width), whole),
+            ],
+            scratch_shapes=[
+                pltpu.VMEM((2 * half, width), BF16),
+                pltpu.VMEM((2 * half, width), F32),
             ],
         ),
         out_shape=[
-            jax.ShapeDtypeStruct((parts, count, width), BF16),
-            jax.ShapeDtypeStruct((2, count, half), BF16),
+            jax.ShapeDtypeStruct((sources, rows, model), BF16),
+            jax.ShapeDtypeStruct((half, width), BF16),
+            jax.ShapeDtypeStruct((half, width), BF16),
+            jax.ShapeDtypeStruct((1, width), F32),
         ],
         compiler_params=PARAMS,
-        name="project",
-    )(mine_at, rows_in, gain, bias, mine, other, add)
-
-
-def finish_kernel(
-    wsh_ref,
+        name="unproject",
+    )(at, halo_count, low, packed, extra, extra_halo, mine, other)
+
+
+def feed_kernel(
+    at_ref,
     x_ref,
+    ups_ref,
+    mixed_ref,
+    out_w_ref,
+    out_b_ref,
     gain_ref,
+    bias_ref,
+    back_b_ref,
+    in_w_ref,
+    in_b_ref,
+    back_w_ref,
+    out_ref,
     dmid_ref,
+    dmixed_ref,
+    din_keep_ref,
+    din_send_ref,
+    dback_ref,
+    dout_keep_ref,
+    dout_send_ref,
+    din_b_ref,
+    vectors_ref,
+    attended_ref,
+    middle_ref,
     low_ref,
-    grads_ref,
-    mine_ref,
-    other_ref,
-    keep_ref,
-    send_ref,
-    cols_ref,
-    out_ref,
-    dgain_ref,
-    dbias_ref,
     acc_ref,
+    grad_acc_ref,
+    square_ref,
 ):
     step = pl.program_id(0)
-    mine_at = wsh_ref[0]
-    grads = grads_ref[0]
-    keep_ref[0] = dot_inner(low_ref[mine_at], grads).astype(BF16)
-    send_ref[0] = dot_inner(low_ref[1 - mine_at], grads).astype(BF16)
-    cols_ref[0] = jnp.sum(grads.astype(F32), axis=0, keepdims=True)
+    sources, rows, width = mixed_ref.shape
+    count, model = x_ref.shape
+    half = model // 2
+    groups = count // rows
+    triples = sources // groups
+    own = pl.ds(pl.multiple_of(at_ref[0] * half, half), half)
+    rest = pl.ds(pl.multiple_of((1 - at_ref[0]) * half, half), half)
 
     @pl.when(step == 0)
     def _():
-        acc_ref[...] = jnp.zeros_like(acc_ref)
-
-    acc_ref[mine_at] += dot_transposed(grads, mine_ref[0])
-    acc_ref[1 - mine_at] += dot_transposed(grads, other_ref[0])
+        for group in range(groups):
+            attended_ref[group * rows : (group + 1) * rows, :] = jnp.concatenate(
+                [mixed_ref[triple * groups + group] for triple in range(triples)], axis=1
+            )
+        middle = x_ref[...].astype(F32) + dot_plain(attended_ref[...], out_w_ref[...])
+        middle = middle + out_b_ref[...]
+        middle_ref[...] = middle
+        low_ref[...] = norm_forward(middle, gain_ref[...], bias_ref[...])[0].astype(BF16)
+
+    hidden_pre = dot_plain(low_ref[...], in_w_ref[...]) + in_b_ref[...]
+    grad_hidden = dot_transposed(ups_ref[...], back_w_ref[...])
+    below = 0.5 * (1.0 + lax.erf(hidden_pre * 0.5**0.5))
+    hidden = (hidden_pre * below).astype(BF16)
+    density = jnp.exp(-0.5 * hidden_pre * hidden_pre) * 0.3989422804014327
+    grad_pre_wide = grad_hidden * (below + hidden_pre * density)
+    grad_pre = grad_pre_wide.astype(BF16)
+    din_b_ref[0] = jnp.sum(grad_pre.astype(F32), axis=0, keepdims=True)
+    share = dot_plain(hidden, back_w_ref[...])
+    grad_share = dot_transposed(grad_pre, in_w_ref[...])
+    dback_ref[0] = dot_inner(hidden, ups_ref[...]).astype(BF16)
+    square_ref[...] = dot_inner(low_ref[...], grad_pre).astype(BF16)
+    din_keep_ref[0] = square_ref[own, :]
+    din_send_ref[0] = square_ref[rest, :]
+
+    @pl.when(step == 0)
+    def _():
+        acc_ref[...] = share
+        grad_acc_ref[...] = grad_share
+
+    @pl.when(step > 0)
+    def _():
+        acc_ref[...] += share
+        grad_acc_ref[...] += grad_share
 
     @pl.when(step == pl.num_programs(0) - 1)
     def _():
-        unused, normed, scaled = norm_forward(x_ref[...].astype(F32), 1.0, 0.0)
-        upstream = jnp.concatenate([acc_ref[0], acc_ref[1]], axis=1)
-        result, dgain, dbias = norm_backward(upstream, normed, scaled, gain_ref[...])
-        out_ref[...] = dmid_ref[...] + result
-        dgain_ref[...] = dgain
-        dbias_ref[...] = dbias
-
-
-def finish(mine_at, rows_in, gain, dmid, low, grads, mine, other):
-    parts, half, width = mine.shape
+        middle = middle_ref[...]
+        out_ref[...] = (middle + acc_ref[...] + back_b_ref[...]).astype(BF16)
+        upstream = ups_ref[...].astype(F32)
+        unused, normed, scaled = norm_forward(middle, 1.0, 0.0)
+        change, dgain, dbias = norm_backward(grad_acc_ref[...], normed, scaled, gain_ref[...])
+        dmid = upstream + change
+        dmid_ref[...] = dmid
+        branch = dmid.astype(BF16)
+        square_ref[...] = dot_inner(attended_ref[...], branch).astype(BF16)
+        dout_keep_ref[...] = square_ref[own, :]
+        dout_send_ref[...] = square_ref[rest, :]
+        vectors_ref[0:1, :] = jnp.sum(branch.astype(F32), axis=0, keepdims=True)
+        vectors_ref[1:2, :] = dgain
+        vectors_ref[2:3, :] = dbias
+        vectors_ref[3:4, :] = jnp.sum(upstream, axis=0, keepdims=True)
+        dattended = dot_transposed(branch, out_w_ref[...]).astype(BF16)
+        for group in range(groups):
+            for triple in range(triples):
+                dmixed_ref[triple * groups + group] = dattended[
+                    group * rows : (group + 1) * rows, triple * width : (triple + 1) * width
+                ]
+
+
+def feed(at, rows_in, ups, mixed, out_w, out_b, gain, bias, back_b, in_w, in_b, back_w):
     count, model = rows_in.shape
+    hidden = in_w.shape[1]
+    blocks = hidden // model
+    half = model // 2
     whole = lambda i, *unused: (0, 0)
-    each = lambda i, *unused: (i, 0, 0)
+    whole_three = lambda i, *unused: (0, 0, 0)
+
+    def block_at(i, at_ref):
+        return (i + at_ref[0] * (blocks // 2)) % blocks
+
+    full = pl.BlockSpec((count, model), whole)
+    vector = pl.BlockSpec((1, model), whole)
     return pl.pallas_call(
-        finish_kernel,
+        feed_kernel,
         grid_spec=pltpu.PrefetchScalarGridSpec(
             num_scalar_prefetch=1,
-            grid=(parts,),
+            grid=(blocks,),
             in_specs=[
-                pl.BlockSpec((count, model), whole),
-                pl.BlockSpec((1, model), whole),
-                pl.BlockSpec((count, model), whole),
-                pl.BlockSpec((2, count, half), lambda i, *unused: (0, 0, 0)),
-                pl.BlockSpec((1, count, width), each),
-                pl.BlockSpec((1, half, width), each),
-                pl.BlockSpec((1, half, width), each),
+                full,
+                full,
+                pl.BlockSpec(mixed.shape, whole_three),
+                pl.BlockSpec((model, model), whole),
+                vector,
+                vector,
+                vector,
+                vector,
+                pl.BlockSpec((model, model), lambda i, at_ref: (0, block_at(i, at_ref))),
+                pl.BlockSpec((1, model), lambda i, at_ref: (0, block_at(i, at_ref))),
+                pl.BlockSpec((model, model), lambda i, at_ref: (block_at(i, at_ref), 0)),
             ],
             out_specs=[
-                pl.BlockSpec((1, half, width), each),
-                pl.BlockSpec((1, half, width), each),
-                pl.BlockSpec((1, 1, width), each),
-                pl.BlockSpec((count, model), whole),
-                pl.BlockSpec((1, model), whole),
-                pl.BlockSpec((1, model), whole),
+                full,
+                full,
+                pl.BlockSpec(mixed.shape, whole_three),
+                pl.BlockSpec((1, half, model), lambda i, at_ref: (block_at(i, at_ref), 0, 0)),
+                pl.BlockSpec((1, half, model), lambda i, at_ref: (block_at(i, at_ref), 0, 0)),
+                pl.BlockSpec((1, model, model), lambda i, *unused: (i, 0, 0)),
+                pl.BlockSpec((half, model), whole),
+                pl.BlockSpec((half, model), whole),
+                pl.BlockSpec((1, 1, model), lambda i, at_ref: (block_at(i, at_ref), 0, 0)),
+                pl.BlockSpec((4, model), whole),
             ],
-            scratch_shapes=[pltpu.VMEM((2, count, half), F32)],
+            scratch_shapes=[
+                pltpu.VMEM((count, model), BF16),
+                pltpu.VMEM((count, model), F32),
+                pltpu.VMEM((count, model), BF16),
+                pltpu.VMEM((count, model), F32),
+                pltpu.VMEM((count, model), F32),
+                pltpu.VMEM((model, model), BF16),
+            ],
         ),
         out_shape=[
-            jax.ShapeDtypeStruct((parts, half, width), BF16),
-            jax.ShapeDtypeStruct((parts, half, width), BF16),
-            jax.ShapeDtypeStruct((parts, 1, width), F32),
+            jax.ShapeDtypeStruct((count, model), BF16),
             jax.ShapeDtypeStruct((count, model), F32),
-            jax.ShapeDtypeStruct((1, model), F32),
-            jax.ShapeDtypeStruct((1, model), F32),
+            jax.ShapeDtypeStruct(mixed.shape, BF16),
+            jax.ShapeDtypeStruct((blocks, half, model), BF16),
+            jax.ShapeDtypeStruct((blocks, half, model), BF16),
+            jax.ShapeDtypeStruct((blocks, model, model), BF16),
+            jax.ShapeDtypeStruct((half, model), BF16),
+            jax.ShapeDtypeStruct((half, model), BF16),
+            jax.ShapeDtypeStruct((blocks, 1, model), F32),
+            jax.ShapeDtypeStruct((4, model), F32),
         ],
         compiler_params=PARAMS,
-        name="finish",
-    )(mine_at, rows_in, gain, dmid, low, grads, mine, other)
+        name="feed",
+    )(at, rows_in, ups, mixed, out_w, out_b, gain, bias, back_b, in_w, in_b, back_w)
 
 
 def head_columns(block, kind, head, heads):
@@ -766,64 +942,99 @@
     )(scalars, starts, packed, ups, logsum, delta, dquery)
 
 
-def gather_pair(shard, axis):
-    ways = lax.axis_size("wsh")
-    if ways == 2:
+def gather_pair(shard):
+    if lax.axis_size("wsh") == 2:
         other = lax.ppermute(shard, "wsh", [(0, 1), (1, 0)])
-        return (shard, other, lax.axis_index("wsh"))
-    whole = lax.all_gather(shard, "wsh", axis=axis, tiled=True)
-    first, second = jnp.split(whole, 2, axis=axis)
-    return (first, second, jnp.zeros((), jnp.int32))
-
-
-def scatter_rows(keep, send):
-    ways = lax.axis_size("wsh")
-    if ways == 2:
+        return (shard, other)
+    whole = lax.all_gather(shard, "wsh", axis=0, tiled=True)
+    return tuple(jnp.split(whole, 2, axis=0))
+
+
+def scatter_rows(keep, send, axis):
+    if lax.axis_size("wsh") == 2:
         got = lax.ppermute(send, "wsh", [(0, 1), (1, 0)])
         return (keep.astype(F32) + got.astype(F32)).astype(BF16)
-    whole = jnp.concatenate([keep, send], axis=-2)
-    return lax.psum_scatter(whole, "wsh", scatter_dimension=whole.ndim - 2, tiled=True)
-
-
-def reduce_parts(parts, axis="ctx"):
-    ways = lax.axis_size(axis)
-    bits = ways.bit_length() - 1
-    index = lax.axis_index(axis)
-    rest = tuple(range(3, bits))
-    orders = [(0, 1, 2) + rest, (1, 2, 0) + rest, (2, 0, 1) + rest]
-    parts = list(parts)
-
-    def traded(value, bit):
-        return lax.ppermute(value, axis, [(i, i ^ (1 << bit)) for i in range(ways)])
-
-    for step in range(bits):
-        for at in range(len(parts)):
-            bit = orders[at % 3][step]
-            flag = (index >> bit) & 1
+    whole = jnp.concatenate([keep, send], axis=axis)
+    return lax.psum_scatter(whole, "wsh", scatter_dimension=axis, tiled=True)
+
+
+def traded(value, bit):
+    ways = lax.axis_size("ctx")
+    return lax.ppermute(value, "ctx", [(i, i ^ (1 << bit)) for i in range(ways)])
+
+
+def reduce_gather(value, sum_bits, gather_bits, pieces):
+    index = lax.axis_index("ctx")
+    rows, width = value.shape
+    size = rows // pieces
+    parts = [value[at * size : (at + 1) * size] for at in range(pieces)]
+    for bit in sum_bits:
+        flag = (index >> bit) & 1
+        for at in range(pieces):
             count = parts[at].shape[0] // 2
             keep = lax.dynamic_slice_in_dim(parts[at], flag * count, count, 0)
             send = lax.dynamic_slice_in_dim(parts[at], (1 - flag) * count, count, 0)
             got = traded(send, bit)
             parts[at] = (keep.astype(F32) + got.astype(F32)).astype(BF16)
-    for step in reversed(range(bits)):
-        for at in range(len(parts)):
-            bit = orders[at % 3][step]
-            flag = (index >> bit) & 1
+    near = [bit for bit in sum_bits if bit < 3] + list(gather_bits)
+    far = [bit for bit in sum_bits if bit >= 3]
+    orders = [far + near[at % len(near) :] + near[: at % len(near)] for at in range(pieces)]
+    parts = [part[None] for part in parts]
+    for step in range(len(orders[0])):
+        for at in range(pieces):
+            flag = (index >> orders[at][step]) & 1
             mine = parts[at]
-            got = traded(mine, bit)
+            got = traded(mine, orders[at][step])
             parts[at] = jnp.where(
                 flag == 0,
                 jnp.concatenate([mine, got], axis=0),
                 jnp.concatenate([got, mine], axis=0),
             )
-    return parts
-
-
-def own_half(value, at, axis=0):
-    count = value.shape[axis] // 2
-    keep = lax.dynamic_slice_in_dim(value, at * count, count, axis)
-    send = lax.dynamic_slice_in_dim(value, (1 - at) * count, count, axis)
-    return keep, send
+    wanted = sorted(gather_bits, reverse=True) + list(sum_bits)
+    done = []
+    for at in range(pieces):
+        held = list(reversed(orders[at]))
+        count = parts[at].shape[1]
+        split = parts[at].reshape((2,) * len(held) + (count, width))
+        split = split.transpose([held.index(bit) for bit in wanted] + [len(held), len(held) + 1])
+        done.append(split.reshape(1 << len(gather_bits), size, width))
+    return jnp.concatenate(done, axis=1)
+
+
+def scatter_step(parts, orders, step):
+    index = lax.axis_index("ctx")
+    done = []
+    for part, order in zip(parts, orders):
+        flag = (index >> order[step]) & 1
+        count = part.shape[0] // 2
+        keep = lax.dynamic_slice_in_dim(part, flag * count, count, 0)
+        send = lax.dynamic_slice_in_dim(part, (1 - flag) * count, count, 0)
+        got = traded(send, order[step])
+        done.append((keep.astype(F32) + got.astype(F32)).astype(BF16))
+    return done
+
+
+def gather_step(parts, orders, step):
+    index = lax.axis_index("ctx")
+    done = []
+    for part, order in zip(parts, orders):
+        flag = (index >> order[step]) & 1
+        got = traded(part, order[step])
+        first = jnp.where(flag == 0, part, got)
+        second = jnp.where(flag == 0, got, part)
+        done.append(jnp.concatenate([first, second], axis=0))
+    return done
+
+
+def small_sum(value):
+    ways = lax.axis_size("ctx")
+    if lax.axis_size("wsh") == 2:
+        value = value + lax.ppermute(value, "wsh", [(0, 1), (1, 0)])
+    else:
+        value = lax.psum(value, "wsh")
+    for bit in range(ways.bit_length() - 1):
+        value = value + traded(value, bit)
+    return value
 
 
 def body(
@@ -861,49 +1072,53 @@
     pad = packed_width - 3 * width
     count = groups * rows
     hidden_size = w_in.shape[1]
+    blocks = hidden_size // model
+    shard_rows = model // shards
     my_ctx = lax.axis_index("ctx")
     part_at = my_ctx // HP
     group_at = (my_ctx % HP) % groups
+    triple_at = (my_ctx % HP) // groups
+    half_at = wsh_at if shards == 2 else jnp.zeros((), jnp.int32)
+    at_vector = half_at.astype(jnp.int32).reshape(1)
 
     small_rows = [ln_gain_one, ln_bias_one, b_query, b_value, b_out, ln_gain_two, ln_bias_two]
     small_rows = small_rows + [b_back, b_in]
-    shard_width = model // shards
-    small = jnp.concatenate([row.reshape(-1, shard_width) for row in small_rows], axis=0)
-    small = lax.all_gather(small, "wsh", axis=0, tiled=False) if shards != 2 else None or (
-        lambda mine: (
-            lambda got: jnp.where(wsh_at == 0, jnp.stack([mine, got]), jnp.stack([got, mine]))
-        )(lax.ppermute(mine, "wsh", [(0, 1), (1, 0)]))
-    )(small)
+    small = jnp.concatenate([row.reshape(-1, shard_rows) for row in small_rows], axis=0)
+    if shards == 2:
+        got = lax.ppermute(small, "wsh", [(0, 1), (1, 0)])
+        small = jnp.where(wsh_at == 0, jnp.stack([small, got]), jnp.stack([got, small]))
+    else:
+        small = lax.all_gather(small, "wsh", axis=0, tiled=False)
     vectors = [small[:, at].reshape(1, model).astype(F32) for at in range(8)]
     gain_one, bias_one, query_b, value_b, out_b, gain_two, bias_two, back_b = vectors
     in_b = small[:, 8:].reshape(1, hidden_size).astype(F32)
-
-    def by_triple(value):
-        return value.reshape(value.shape[0], triples, width).transpose(1, 0, 2)
-
-    stacked = [by_triple(w_key), by_triple(w_value), by_triple(w_query)]
-    stacked_b = [jnp.zeros((triples, 1, width), F32), by_triple(value_b), by_triple(query_b)]
-    if pad:
-        stacked.append(jnp.zeros((triples, w_key.shape[0], pad), BF16))
-        stacked_b.append(jnp.zeros((triples, 1, pad), F32))
-    stacked = jnp.concatenate(stacked, axis=2)
-    stacked_b = jnp.concatenate(stacked_b, axis=2)
-    first_w, second_w, first_at = gather_pair(stacked, 1)
-    at_vector = first_at.reshape(1)
     out_w = lax.all_gather(w_out, "wsh", axis=0, tiled=True)
     in_w = lax.all_gather(w_in, "wsh", axis=0, tiled=True)
     back_w = lax.all_gather(w_back, "wsh", axis=0, tiled=True)
 
     token_rows = tokens.reshape(count, model)
-    packed, low_one = project(
-        at_vector, token_rows, gain_one, bias_one, first_w, second_w, stacked_b
-    )
+    inputs = token_rows.astype(F32)
     cube = [[part * HP + at for at in range(HP)] for part in range(parts)]
 
     def exchange(value):
         return lax.all_to_all(value, "ctx", 0, 0, axis_index_groups=cube)
 
-    packed = exchange(packed.reshape(HP, rows, packed_width)).reshape(HP, 2, stripe, packed_width)
+    low_one = norm_forward(inputs, gain_one, bias_one)[0].astype(BF16)
+    low_one = low_one.reshape(1, groups, rows, model)
+    low_one = jnp.broadcast_to(low_one, (HP // groups, groups, rows, model))
+    low_all = exchange(low_one.reshape(HP, rows, model))
+
+    def own_columns(value):
+        return lax.dynamic_slice_in_dim(value, triple_at * width, width, 1)
+
+    stacked = [own_columns(w_key), own_columns(w_value), own_columns(w_query)]
+    stacked_b = [jnp.zeros((1, width), F32), own_columns(value_b), own_columns(query_b)]
+    if pad:
+        stacked.append(jnp.zeros((shard_rows, pad), BF16))
+        stacked_b.append(jnp.zeros((1, pad), F32))
+    first_w, second_w = gather_pair(jnp.concatenate(stacked, axis=1))
+    packed = project(at_vector, low_all, first_w, second_w, jnp.concatenate(stacked_b, axis=1))
+    packed = packed.reshape(HP, 2, stripe, packed_width)
 
     lengths = lax.dynamic_index_in_dim(cont_lengths, group_at, 0, keepdims=False)
     seg_ends = jnp.cumsum(lengths, dtype=jnp.int32)
@@ -948,172 +1163,124 @@
     mixed_rows, logsum, mixed = forward_remote(
         scalars, starts, packed, prompts, halo, state, heads
     )
-
-    def to_tokens(value):
-        back = exchange(value.reshape(HP, rows, width)).reshape(triples, count, width)
-        return back.transpose(1, 0, 2).reshape(count, model)
-
-    def to_heads(value):
-        split = value.reshape(count, triples, width).transpose(1, 0, 2)
-        return exchange(split.reshape(HP, rows, width)).reshape(HP, 2, stripe, width)
-
-    low_attended = to_tokens(mixed_rows)
-
-    inputs = token_rows.astype(F32)
-    middle = inputs + dot_plain(low_attended, out_w) + out_b
-    normed_two, hat_two, scale_two = norm_forward(middle, gain_two, bias_two)
-    low_two = normed_two.astype(BF16)
-    hidden_pre = dot_plain(low_two, in_w) + in_b
-    hidden, gelu_back = jax.vjp(exact_gelu, hidden_pre)
-    low_hidden = hidden.astype(BF16)
-    result = middle + dot_plain(low_hidden, back_w) + back_b
-    out_tokens = result.astype(BF16).reshape(groups, rows, model)
-    upstream_low = grad_out.reshape(count, model)
-    upstream = upstream_low.astype(F32)
-    grad_back_w = dot_inner(low_hidden, upstream_low).astype(BF16)
-    grad_back_b = jnp.sum(upstream, axis=0, keepdims=True)
-    grad_hidden = dot_transposed(upstream_low, back_w)
-    grad_pre = gelu_back(grad_hidden)[0].astype(BF16)
-    grad_in_w = dot_inner(low_two, grad_pre).astype(BF16)
-    grad_in_b = jnp.sum(grad_pre.astype(F32), axis=0, keepdims=True)
-    grad_normed_two = dot_transposed(grad_pre, in_w)
-    grad_mid_norm, grad_gain_two, grad_bias_two = norm_backward(
-        grad_normed_two, hat_two, scale_two, gain_two
-    )
-    grad_middle = upstream + grad_mid_norm
-    grad_branch = grad_middle.astype(BF16)
-    grad_out_w = dot_inner(low_attended, grad_branch).astype(BF16)
-    grad_out_b = jnp.sum(grad_branch.astype(F32), axis=0, keepdims=True)
-    grad_attended = dot_transposed(grad_branch, out_w).astype(BF16)
-
-    ups = to_heads(grad_attended)
+    attended = exchange(mixed_rows.reshape(HP, rows, width))
+
+    (
+        out_rows,
+        grad_middle,
+        dattended,
+        din_keep,
+        din_send,
+        dback,
+        dout_keep,
+        dout_send,
+        din_b,
+        mid_vectors,
+    ) = feed(
+        at_vector,
+        token_rows,
+        grad_out.reshape(count, model),
+        attended,
+        out_w,
+        out_b,
+        gain_two,
+        bias_two,
+        back_b,
+        in_w,
+        in_b,
+        back_w,
+    )
+    ups = exchange(dattended).reshape(HP, 2, stripe, width)
+    in_sum = scatter_rows(din_keep, din_send, 1)
+    back_sum = scatter_rows(
+        dback[: blocks // 2].reshape(-1, model), dback[blocks // 2 :].reshape(-1, model), 0
+    )
+    out_sum = scatter_rows(dout_keep, dout_send, 0)
+    sums = [in_sum.reshape(-1, model), back_sum, out_sum]
+    bits = ways.bit_length() - 1
+    rest = tuple(range(3, bits))
+    orders = [(0, 1, 2) + rest, (1, 0, 2) + rest, (2, 0, 1) + rest]
+    *sums, ups = lax.optimization_barrier((*sums, ups))
+    sums = scatter_step(sums, orders, 0)
+
     dprompts, dhalo, dquery, delta = backward_remote(
         scalars, starts, packed, ups, prompts, halo, logsum, mixed, heads
     )
-    returned = sum(
-        shifted(dprompts[shift - 1], parts - shift).astype(F32) for shift in range(1, parts)
-    )
-    returned_halo = to_latter(dhalo).astype(F32)
+    *sums, dprompts, dhalo, dquery = lax.optimization_barrier((*sums, dprompts, dhalo, dquery))
+    sums = scatter_step(sums, orders, 1)
+    returned = [shifted(dprompts[shift - 1], parts - shift) for shift in range(1, parts)]
+    if parts > 2:
+        returned = [sum(piece.astype(F32) for piece in returned).astype(BF16)]
+    returned_halo = to_latter(dhalo)
     dpacked = backward_local(scalars, starts, packed, ups, logsum, delta, dquery, heads)
-    extra = jnp.zeros((HP, 2, stripe, packed_width), F32)
-    extra = extra.at[:, 0, :, : 2 * width].set(returned)
-    extra = extra.at[:halo_blocks, 1, :, : 2 * width].set(returned_halo)
-    dpacked = (dpacked.astype(F32) + extra).astype(BF16)
-
-    blocks = hidden_size // model
-
-    def to_blocks(value):
-        split = value.reshape(value.shape[0], blocks, model)
-        return split.transpose(1, 0, 2).reshape(-1, model)
-
-    small_mid = jnp.concatenate(
-        [grad_out_b, grad_gain_two, grad_bias_two, grad_back_b, grad_in_b.reshape(-1, model)],
-        axis=0,
-    )
-    shard_rows = model // shards
-    mid_rows = (2 * blocks + 1) * shard_rows
-    mid_total = -(-(mid_rows + 8) // 512) * 512
-    if shards == 2:
-        keep_in, send_in = own_half(grad_in_w, wsh_at)
-        keep_back, send_back = own_half(grad_back_w, wsh_at)
-        keep_out, send_out = own_half(grad_out_w, wsh_at)
-        filler = jnp.zeros((mid_total - mid_rows - small_mid.shape[0], model), BF16)
-        tail = [small_mid.astype(BF16), filler]
-        mid_keep = jnp.concatenate([to_blocks(keep_in), keep_back, keep_out] + tail, axis=0)
-        mid_send = jnp.concatenate([to_blocks(send_in), send_back, send_out] + tail, axis=0)
-        mid_sum = scatter_rows(mid_keep, mid_send)
-    else:
-        scattered = [
-            lax.psum_scatter(part, "wsh", scatter_dimension=0, tiled=True)
-            for part in (grad_in_w, grad_back_w, grad_out_w)
-        ]
-        small_sum = lax.psum(small_mid.astype(BF16), "wsh")
-        filler = jnp.zeros((mid_total - mid_rows - small_mid.shape[0], model), BF16)
-        mid_sum = jnp.concatenate(
-            [to_blocks(scattered[0]), scattered[1], scattered[2], small_sum, filler], axis=0
-        )
-    third = mid_total // 3 // 256 * 256
-    cuts = [third + 256 * (mid_total // 256 - 3 * (third // 256) > at) for at in range(3)]
-    edges = [0, cuts[0], cuts[0] + cuts[1], mid_total]
-    mid_parts = reduce_parts([mid_sum[edges[at] : edges[at + 1]] for at in range(3)])
-    mid_done = jnp.concatenate(mid_parts, axis=0)
-
-    grads = exchange(dpacked.reshape(HP, rows, packed_width)).reshape(triples, count, packed_width)
-    keep, send, columns, grad_rows, grad_gain_one, grad_bias_one = finish(
-        at_vector, token_rows, gain_one, grad_middle, low_one, grads, first_w, second_w
-    )
-    small_last = jnp.concatenate(
-        [
-            columns.reshape(triples, packed_width),
-            jnp.pad(
-                jnp.concatenate([grad_gain_one, grad_bias_one], axis=0),
-                ((0, 0), (0, 2 * packed_width - model)),
-            ).reshape(4, packed_width),
-        ],
-        axis=0,
-    ).astype(BF16)
-    last_rows = triples * shard_rows
-    last_total = -(-(last_rows + 8) // 128) * 128
-    filler = jnp.zeros((last_total - last_rows - small_last.shape[0], packed_width), BF16)
-    if shards == 2:
-        tail = [small_last, filler]
-        last_sum = scatter_rows(
-            jnp.concatenate([keep.reshape(last_rows, packed_width)] + tail, axis=0),
-            jnp.concatenate([send.reshape(last_rows, packed_width)] + tail, axis=0),
-        )
-    else:
-        scattered = scatter_rows(keep, send).reshape(last_rows, packed_width)
-        last_sum = jnp.concatenate([scattered, lax.psum(small_last, "wsh"), filler], axis=0)
-    third = last_total // 3 // 128 * 128
-    cuts = [third + 128 * (last_total // 128 - 3 * (third // 128) > at) for at in range(3)]
-    edges = [0, cuts[0], cuts[0] + cuts[1], last_total]
-    last_parts = reduce_parts([last_sum[edges[at] : edges[at + 1]] for at in range(3)])
-    last_done = jnp.concatenate(last_parts, axis=0)
+    *sums, dpacked = lax.optimization_barrier((*sums, dpacked))
+    sums = scatter_step(sums, orders, 2)
+    halo_count = jnp.full((1,), halo_blocks, jnp.int32)
+    dlow, keep, send, columns = unproject(
+        at_vector, halo_count, low_all, dpacked, returned[0], returned_halo, first_w, second_w
+    )
+
+    *sums, dlow = lax.optimization_barrier((*sums, dlow))
+    for step in range(3, bits):
+        sums = scatter_step(sums, orders, step)
+    for step in reversed(range(bits)):
+        sums = gather_step(sums, orders, step)
+    in_done, back_done, out_done = sums
+
+    group_bits = groups.bit_length() - 1
+    sum_bits = list(range(group_bits)) + list(range(3, ways.bit_length() - 1))
+    last = reduce_gather(scatter_rows(keep, send, 0), sum_bits, range(group_bits, 3), 3)
+
+    upstream = exchange(dlow).reshape(triples, count, model)
+    upstream = jnp.sum(upstream.astype(F32), axis=0)
+    unused, hat_one, scale_one = norm_forward(inputs, gain_one, bias_one)
+    change, grad_gain_one, grad_bias_one = norm_backward(upstream, hat_one, scale_one, gain_one)
+    grad_rows = grad_middle + change
+    place = (jnp.arange(triples) == triple_at)[:, None]
+    spread = jnp.where(place, columns, 0.0)
+    pieces = [mid_vectors, din_b, grad_gain_one, grad_bias_one, spread]
+    flat = jnp.concatenate([piece.reshape(-1) for piece in pieces])
+    length = flat.shape[0]
+    flat = small_sum(flat.reshape(-1, 128)).reshape(-1)
 
     def own(vector):
         size = vector.shape[0] // shards
-        return lax.dynamic_slice_in_dim(vector, wsh_at * size, size, 0).astype(F32)
-
-    at = blocks * shard_rows
-    new_in_w = mid_done[:at].reshape(blocks, shard_rows, model).transpose(1, 0, 2)
-    new_in_w = new_in_w.reshape(shard_rows, hidden_size).astype(F32)
-    new_back_w = mid_done[at : 2 * at].astype(F32)
-    new_out_w = mid_done[2 * at : mid_rows].astype(F32)
-    tail = mid_done[mid_rows : mid_rows + 4 + blocks]
-    new_out_b, new_gain_two, new_bias_two, new_back_b = [own(tail[i]) for i in range(4)]
-    new_in_b = own(tail[4:].reshape(hidden_size))
-
-    last_w = last_done[:last_rows].reshape(triples, shard_rows, packed_width)
-    tail = last_done[last_rows : last_rows + triples + 4]
+        return lax.dynamic_slice_in_dim(vector, wsh_at * size, size, 0)
+
+    new_out_b, new_gain_two, new_bias_two, new_back_b = [
+        own(flat[at * model : (at + 1) * model]) for at in range(4)
+    ]
+    at = 4 * model + hidden_size
+    new_in_b = own(flat[4 * model : at])
+    new_gain_one = own(flat[at : at + model])
+    new_bias_one = own(flat[at + model : at + 2 * model])
+    columns = flat[at + 2 * model : length].reshape(triples, packed_width)
+
+    def unvector(kind):
+        return own(columns[:, kind * width : (kind + 1) * width].reshape(model))
 
     def untriple(kind):
-        piece = last_w[:, :, kind * width : (kind + 1) * width]
+        piece = last[:, :, kind * width : (kind + 1) * width]
         return piece.transpose(1, 0, 2).reshape(shard_rows, model).astype(F32)
 
-    def unvector(kind):
-        return own(tail[:triples, kind * width : (kind + 1) * width].reshape(model))
-
     new_key_w, new_value_w, new_query_w = [untriple(kind) for kind in range(3)]
-    new_value_b, new_query_b = unvector(1), unvector(2)
-    new_gain_one = own(tail[triples : triples + 2].reshape(-1)[:model])
-    new_bias_one = own(tail[triples + 2 :].reshape(-1)[:model])
     return (
-        out_tokens,
+        out_rows.reshape(groups, rows, model),
         grad_rows.reshape(groups, rows, model),
         new_gain_one,
         new_bias_one,
         new_query_w,
-        new_query_b,
+        unvector(2),
         new_key_w,
         new_value_w,
-        new_value_b,
-        new_out_w,
+        unvector(1),
+        out_done.astype(F32),
         new_out_b,
         new_gain_two,
         new_bias_two,
-        new_in_w,
+        in_done.reshape(blocks, shard_rows, model).transpose(1, 0, 2).reshape(shard_rows, hidden_size).astype(F32),
         new_in_b,
-        new_back_w,
+        back_done.astype(F32),
         new_back_b,
     )
 

time: 657 us -> 544 us (0.83)
  local copies, waits for them, and re-layouts: 124 us -> 55.1 us
  matrix products: 51.9 us -> 0 us
  starting transfers between devices: 113 us -> 158 us
  waiting for transfers between devices: 153 us -> 114 us
  Pallas kernels: 125 us -> 147 us
  blocking collectives: 16 us -> 0 us
    concatenate x8 -> x5, local copies, waits for them, and re-layouts: 62.5 us -> 0.22 us  [the longest x2 0.08 us: body(): jnp.concatenate(stacked_b, axis=1)]
    dot_general x9 -> x0, matrix products: 51.9 us -> none  [the longest x3 24.7 us: dot_transposed(): lax.dot_general(left_side, right_side, (((1,), (1,)), ((), ())), preferre...]
    ppermute x49 -> x48, waiting for transfers between devices: 92.7 us -> 41.3 us  [the longest x46 41.3 us: traded(): return lax.ppermute(value, 'ctx', [(i, i ^ 1 << bit) for i in range(ways)])]
    ppermute x49 -> x48, starting transfers between devices: 67.9 us -> 102 us  [the longest x46 102 us: traded(): return lax.ppermute(value, 'ctx', [(i, i ^ 1 << bit) for i in range(ways)])]
    pallas_call x1 -> x2, Pallas kernels: 12.6 us -> 37 us  [the longest x1 27 us: feed(): pl.pallas_call(feed_kernel, grid_spec=pltpu.PrefetchScalarGridSpec(num_sc...]
    all_to_all x1 -> x0, blocking collectives: 16 us -> none  [exchange(): return lax.all_to_all(value, 'ctx', 0, 0, axis_index_groups=cube)]
    all_to_all x3 -> x4, starting transfers between devices: 18.7 us -> 28.9 us  [exchange(): return lax.all_to_all(value, 'ctx', 0, 0, axis_index_groups=cube)]
    convert_element_type x37 -> x19, other arithmetic: 20.5 us -> 10.3 us  [the longest x12 5.71 us: scatter_step(): done.append((keep.astype(F32) + got.astype(F32)).astype(BF16))]
  transfers between devices with their start and end apart: 62 -> 64, of which waited for: 27 -> 23; matrix products, arithmetic and copies ran while one was open for 19% -> 14% of each run, Pallas kernels for 19% -> 22%
where the time goes in v2:
time: 544 us; the launch traced here: 535 us
  starting transfers between devices  158 us (29%)
  Pallas kernels  147 us (27%)
  waiting for transfers between devices  114 us (21%)
  local copies, waits for them, and re-layouts  55.1 us (10%)
  other arithmetic  46 us (8%)
  between operations  15.5 us (3%)
    ppermute x46, starting transfers between devices, traded(): return lax.ppermute(value, 'ctx', [(i, i ^ 1 << bit) for i in range(ways)])  102 us
    all_to_all x4, waiting for transfers between devices, exchange(): return lax.all_to_all(value, 'ctx', 0, 0, axis_index_groups=cube)  48.9 us
    ppermute x46, waiting for transfers between devices, traded(): return lax.ppermute(value, 'ctx', [(i, i ^ 1 << bit) for i in range(ways)])  41.3 us
    pallas_call x1, Pallas kernels, backward_local(): pl.pallas_call(backward_local_kernel, in_specs=[SMEM_SPEC] + vmem_specs(6...  34.9 us
    pallas_call x1, Pallas kernels, forward_local(): pl.pallas_call(forward_local_kernel, in_specs=[SMEM_SPEC] + vmem_specs(2)...  30.5 us
    all_to_all x4, starting transfers between devices, exchange(): return lax.all_to_all(value, 'ctx', 0, 0, axis_index_groups=cube)  28.9 us
    pallas_call x1, Pallas kernels, feed(): pl.pallas_call(feed_kernel, grid_spec=pltpu.PrefetchScalarGridSpec(num_sc...  27 us
    ppermute x2, starting transfers between devices, shifted(): return lax.ppermute(value, 'ctx', pairs)  22.1 us
  transfers between devices with their start and end apart: 64, of which 23 were waited for; matrix products, arithmetic and copies ran while one was open for 14% of the time, Pallas kernels for 22%

profile of v2, /device:TPU:0, one launch (start us, length us, event | category | flops | bytes accessed | tf_op | source)
XLA Modules:
  0.0 534.6 jit_solution(11724729718091347449)
XLA Ops:
  13.6 5.7 %all-to-all-start = ((bf16[8,256,768]{2,1,0:T(8,128)(2,1)}), bf16[8,256,768]{2,1,0:T(8,128)(2,1)}, u32[]{:S(2)}, u32[]{:S(2)}) async-start(bf16[8,256,768]{2,1,0:T(8,128)(2,1)} %bitcast.114), calls=%async_computation | async-start | bytes 6291456 | tf_op jit(solution)/shard_map/all_to_all | solution.py:1104
  23.8 33.9 %all-to-all-done.low_ref = bf16[8,256,768]{2,1,0:T(8,128)(2,1)} async-done(((bf16[8,256,768]{2,1,0:T(8,128)(2,1)}), bf16[8,256,768]{2,1,0:T(8,128)(2,1)}, u32[]{:S(2)}, u32[]{:S(2)}) %all-to-all-start) | async-done | bytes 3145760 | tf_op jit(solution)/shard_map/all_to_all | solution.py:1104
  57.7 6.2 %project.1 = bf16[8,256,640]{2,1,0:T(8,128)(2,1)} custom-call(s32[1]{0:T(128)} %bitcast.at_ref, bf16[8,256,768]{2,1,0:T(8,128)(2,1)} %all-to-all-done.low_ref, bf16[384,640]{1,0:T(8,128)(2,1)} %copy-done.14, bf16[384,640]{1,0:T(8,128)(2,1)} %copy-done.18, f32[1,640]{1,0:T(1,128)} %reshape_maximum_fusion.add_ref), custom_call_target="tpu_custom_call" | custom-call | tf_op jit(solution)/shard_map/project/pallas_call | solution.py:88
  71.1 30.5 %forward_local.1 = (f32[8,3,1,256]{3,2,1,0:T(1,128)}, f32[8,3,1,256]{3,2,1,0:T(1,128)}, f32[8,3,64,256]{3,2,1,0:T(8,128)}) custom-call(s32[9]{0:T(128)} %pad_add_fusion.scalars_ref, s32[4,1,256]{2,1,0:T(1,128)} %bitcast.137, bf16[8,2,128,640]{3,2,1,0:T(8,128)(2,1)} %bitcast.105), custom_call_target="tpu_custom_call" | custom-call | tf_op jit(solution)/shard_map/forward_local/pallas_call | solution.py:656
  101.5 17.3 %collective-permute-done.3.halo_ref = bf16[4,128,384]{2,1,0:T(8,128)(2,1)S(1)} collective-permute-done((bf16[4,128,384]{2,1,0:T(8,128)(2,1)S(1)}, bf16[4,128,384]{2,1,0:T(8,128)(2,1)S(1)}, u32[]{:S(2)}, u32[]{:S(2)}) %collective-permute-start.3) | collective-permute-done | bytes 393248 | tf_op jit(solution)/shard_map/ppermute | solution.py:1153
  119.8 16.9 %forward_remote.1 = (bf16[8,2,128,192]{3,2,1,0:T(8,128)(2,1)}, f32[8,3,1,256]{3,2,1,0:T(1,128)}, f32[8,3,64,256]{3,2,1,0:T(8,128)}) custom-call(s32[9]{0:T(128)} %pad_add_fusion.scalars_ref, s32[4,1,256]{2,1,0:T(1,128)} %bitcast.138, bf16[8,2,128,640]{3,2,1,0:T(8,128)(2,1)} %bitcast.106, bf16[1,8,128,384]{3,2,1,0:T(8,128)(2,1)} %bitcast.124, ...), custom_call_target="tpu_custom_call" | custom-call | tf_op jit(solution)/shard_map/forward_remote/pallas_call | solution.py:681
  139.0 8.3 %all-to-all-start.1 = ((bf16[8,256,192]{1,2,0:T(8,128)(2,1)}), bf16[8,256,192]{1,2,0:T(8,128)(2,1)S(1)}, u32[]{:S(2)}, u32[]{:S(2)}) async-start(bf16[8,256,192]{1,2,0:T(8,128)(2,1)} %copy.61), calls=%async_computation.1 | async-start | bytes 1572864 | tf_op jit(solution)/shard_map/all_to_all | solution.py:1104
  150.3 8.9 %all-to-all-done.1 = bf16[8,256,192]{1,2,0:T(8,128)(2,1)S(1)} async-done(((bf16[8,256,192]{1,2,0:T(8,128)(2,1)}), bf16[8,256,192]{1,2,0:T(8,128)(2,1)S(1)}, u32[]{:S(2)}, u32[]{:S(2)}) %all-to-all-start.1) | async-done | bytes 786464 | tf_op jit(solution)/shard_map/all_to_all | solution.py:1104
  160.4 27.0 %feed.1 = (bf16[512,768]{1,0:T(8,128)(2,1)}, f32[512,768]{1,0:T(8,128)}, bf16[8,256,192]{2,1,0:T(8,128)(2,1)}, bf16[4,384,768]{2,1,0:T(8,128)(2,1)}, bf16[4,384,...) custom-call(s32[1]{0:T(128)} %bitcast.at_ref, ...), custom_call_target="tpu_custom_call" | custom-call | tf_op jit(solution)/shard_map/feed/pallas_call | solution.py:322
  187.5 4.2 fusion.22
  193.4 3.7 all-to-all-start.2
  197.2 3.5 collective-permute-done.6
  203.0 6.2 %all-to-all-done.2 = bf16[8,256,192]{1,2,0:T(8,128)(2,1)S(1)} async-done(((bf16[8,256,192]{1,2,0:T(8,128)(2,1)}), bf16[8,256,192]{1,2,0:T(8,128)(2,1)S(1)}, u32[]{:S(2)}, u32[]{:S(2)}) %all-to-all-start.2) | async-done | bytes 786464 | tf_op jit(solution)/shard_map/all_to_all | solution.py:1104
  212.9 3.1 add_convert_fusion
  224.9 21.1 %backward_remote.1 = (bf16[1,8,128,384]{3,2,1,0:T(8,128)(2,1)}, bf16[4,128,384]{2,1,0:T(8,128)(2,1)}, f32[8,3,64,256]{3,2,1,0:T(8,128)}, f32[8,3,1,256]{3,2,1,0:T(1,128)}) custom-call(s32[9]{0:T(128)} %pad_add_fusion.scalars_ref, s32[4,1,256]{2,1,0:T(1,128)} %bitcast.139, bf16[8,2,128,640]{3,2,1,0:T(8,128)(2,1)} %bitcast.107, ...), custom_call_target="tpu_custom_call" | custom-call | tf_op jit(solution)/shard_map/backward_remote/pallas_call | solution.py:896
  253.0 19.4 %collective-permute-start.16 = (bf16[8,128,384]{2,1,0:T(8,128)(2,1)S(1)}, bf16[8,128,384]{2,1,0:T(8,128)(2,1)S(1)}, u32[]{:S(2)}, u32[]{:S(2)}) collective-permute-start(bf16[8,128,384]{2,1,0:T(8,128)(2,1)S(1)} %bitcast.155), channel_id=1, source_target_pairs={{0,16},{2,18},{4,20},{6,22},{8,24},{10,26},{12,28},{14,30},{16,0},... | collective-permute-start | bytes 2359304 | tf_op jit(solution)/shard_map/ppermute | solution.py:1149
  274.6 34.9 %backward_local.1.packed_ref = bf16[8,2,128,640]{3,2,1,0:T(8,128)(2,1)} custom-call(s32[9]{0:T(128)} %pad_add_fusion.scalars_ref, s32[4,1,256]{2,1,0:T(1,128)} %bitcast.140, bf16[8,2,128,640]{3,2,1,0:T(8,128)(2,1)} %bitcast.108, bf16[8,2,128,192]{3,2,1,0:T(8,128)(2,1)} %bitcast.119, f32[8,3,1,256]{3,2,1,0:T(1,128)} %get-tuple-element.75.log_ref, ...), custom_call_target="tpu_custom_call" | custom-call | tf_op jit(solution)/shard_map/backward_local/pallas_call | solution.py:925
  316.0 10.0 %unproject.1 = (bf16[8,256,768]{2,1,0:T(8,128)(2,1)}, bf16[384,640]{1,0:T(8,128)(2,1)}, bf16[384,640]{1,0:T(8,128)(2,1)}, f32[1,640]{1,0:T(1,128)}) custom-call(s32[1]{0:T(128)} %bitcast.at_ref, s32[1]{0:T(128)} %constant.124.clone.1.halo_ref, bf16[8,256,768]{2,1,0:T(8,128)(2,1)} %all-to-all-done.low_ref, bf16[8,2,128,640]{3,2,1,0:T(8,128)(2,1)} %backward_local.1.packed_ref, ...), custom_call_target="tpu_custom_call" | custom-call | tf_op jit(solution)/shard_map/unproject/pallas_call | solution.py:171
  327.1 8.6 %collective-permute-start.42 = (bf16[24,768]{1,0:T(8,128)(2,1)S(1)}, bf16[24,768]{1,0:T(8,128)(2,1)S(1)}, u32[]{:S(2)}, u32[]{:S(2)}) collective-permute-start(bf16[24,768]{1,0:T(8,128)(2,1)S(1)} %constant_dynamic-slice_fusion.2), channel_id=1, source_target_pairs={{0,16},{2,18},{4,20},{6,22},{8,24},{10,26},{12,28},{14,30},{16,0},... | collective-permute-start | bytes 110600 | tf_op jit(solution)/shard_map/ppermute | solution.py:963
  337.7 3.4 collective-permute-start.43
  341.7 11.1 %all-to-all-start.3 = ((bf16[8,256,768]{2,1,0:T(8,128)(2,1)}), bf16[8,256,768]{2,1,0:T(8,128)(2,1)S(1)}, u32[]{:S(2)}, u32[]{:S(2)}) async-start(bf16[8,256,768]{2,1,0:T(8,128)(2,1)} %get-tuple-element.92), calls=%async_computation.3 | async-start | bytes 6291456 | tf_op jit(solution)/shard_map/all_to_all | solution.py:1104
  356.8 3.0 collective-permute-start.53
  360.8 4.1 collective-permute-done.44
  365.0 26.8 %collective-permute-start.45 = (bf16[96,768]{1,0:T(8,128)(2,1)S(1)}, bf16[96,768]{1,0:T(8,128)(2,1)S(1)}, u32[]{:S(2)}, u32[]{:S(2)}) collective-permute-start(bf16[96,768]{1,0:T(8,128)(2,1)S(1)} %pad_maximum_fusion.9), channel_id=1, source_target_pairs={{0,2},{2,0},{4,6},{6,4},{8,10},{10,8},{12,14},{14,12},{16,18},{18,... | collective-permute-start | bytes 442376 | tf_op jit(solution)/shard_map/ppermute | solution.py:963
  391.9 4.5 collective-permute-start.54
  400.3 6.8 %collective-permute-start.24 = (bf16[64,640]{1,0:T(8,128)(2,1)S(1)}, bf16[64,640]{1,0:T(8,128)(2,1)S(1)}, u32[]{:S(2)}, u32[]{:S(2)}) collective-permute-start(bf16[64,640]{1,0:T(8,128)(2,1)S(1)} %constant_dynamic-slice_fusion.8), channel_id=1, source_target_pairs={{0,2},{2,0},{4,6},{6,4},{8,10},{10,8},{12,14},{14,12},{16,18},{18,... | collective-permute-start | bytes 245768 | tf_op jit(solution)/shard_map/ppermute | solution.py:963
  427.3 4.2 collective-permute-start.27
  441.6 9.4 %collective-permute-done.28 = bf16[4,32,640]{2,1,0:T(8,128)(2,1)S(1)} collective-permute-done((bf16[4,32,640]{2,1,0:T(8,128)(2,1)S(1)}, bf16[4,32,640]{2,1,0:T(8,128)(2,1)S(1)}, u32[]{:S(2)}, u32[]{:S(2)}) %collective-permute-start.28) | collective-permute-done | bytes 163872 | tf_op jit(solution)/shard_map/ppermute | solution.py:963
  468.8 2.9 copy.67
  474.3 2.9 copy.68
  479.9 2.9 copy.69
  488.7 3.1 broadcast_select_fusion.1
  (384 shorter events, 164.7 us)
Async XLA Ops:
  7.3 153.1 %all-gather.4.cloned.1.call-start = ((), (), s32[]{:S(2)}) async-start(), calls=%async_computation.4 | async-start | bytes 1769472 | tf_op jit(solution)/shard_map/all_gather | solution.py:1095
  8.0 152.4 %all-gather.6.cloned.1.call-start = ((), (), s32[]{:S(2)}) async-start(), calls=%async_computation.5 | async-start | bytes 7077888 | tf_op jit(solution)/shard_map/all_gather | solution.py:1096
  13.6 44.0 %all-to-all-start = ((bf16[8,256,768]{2,1,0:T(8,128)(2,1)}), bf16[8,256,768]{2,1,0:T(8,128)(2,1)}, u32[]{:S(2)}, u32[]{:S(2)}) async-start(bf16[8,256,768]{2,1,0:T(8,128)(2,1)} %bitcast.114), calls=%async_computation | async-start | bytes 6291456 | tf_op jit(solution)/shard_map/all_to_all | solution.py:1104
  19.4 141.1 %all-gather.8.cloned.1.call-start = ((), (), s32[]{:S(2)}) async-start(), calls=%async_computation.6 | async-start | bytes 7077888 | tf_op jit(solution)/shard_map/all_gather | solution.py:1097
  65.1 53.8 %collective-permute-start.2 = (bf16[8,128,384]{2,1,0:T(8,128)(2,1)S(1)}, bf16[8,128,384]{2,1,0:T(8,128)(2,1)S(1)}, u32[]{:S(2)}, u32[]{:S(2)}) collective-permute-start(bf16[8,128,384]{2,1,0:T(8,128)(2,1)S(1)} %slice_bitcast_fusion), channel_id=1, source_target_pairs={{0,16},{2,18},{4,20},{6,22},{8,24},{10,26},{12,28},{14,30},{16,0},... | collective-permute-start | bytes 2359304 | tf_op jit(solution)/shard_map/ppermute | solution.py:1149
  68.9 49.9 %collective-permute-start.3 = (bf16[4,128,384]{2,1,0:T(8,128)(2,1)S(1)}, bf16[4,128,384]{2,1,0:T(8,128)(2,1)S(1)}, u32[]{:S(2)}, u32[]{:S(2)}) collective-permute-start(bf16[4,128,384]{2,1,0:T(8,128)(2,1)S(1)} %slice_bitcast_fusion.1), channel_id=1, source_target_pairs={{16,0},{18,2},{20,4},{22,6},{24,8},{26,10},{28,12},{30,14},{17,1},... | collective-permute-start | bytes 1179656 | tf_op jit(solution)/shard_map/ppermute | solution.py:1153
  139.0 20.2 %all-to-all-start.1 = ((bf16[8,256,192]{1,2,0:T(8,128)(2,1)}), bf16[8,256,192]{1,2,0:T(8,128)(2,1)S(1)}, u32[]{:S(2)}, u32[]{:S(2)}) async-start(bf16[8,256,192]{1,2,0:T(8,128)(2,1)} %copy.61), calls=%async_computation.1 | async-start | bytes 1572864 | tf_op jit(solution)/shard_map/all_to_all | solution.py:1104
  191.6 18.8 %collective-permute-start.5 = (bf16[1536,768]{1,0:T(8,128)(2,1)}, bf16[1536,768]{1,0:T(8,128)(2,1)}, u32[]{:S(2)}, u32[]{:S(2)}) collective-permute-start(bf16[1536,768]{1,0:T(8,128)(2,1)} %bitcast.24), channel_id=1, source_target_pairs={{0,1},{1,0},{2,3},{3,2},{4,5},{5,4},{6,7},{7,6},{8,9},{9,8},{10,11... | collective-permute-start | bytes 7077896 | tf_op jit(solution)/shard_map/ppermute | solution.py:955
  191.6 21.3 %collective-permute-start.4 = (bf16[4,384,768]{2,1,0:T(8,128)(2,1)}, bf16[4,384,768]{2,1,0:T(8,128)(2,1)}, u32[]{:S(2)}, u32[]{:S(2)}) collective-permute-start(bf16[4,384,768]{2,1,0:T(8,128)(2,1)} %get-tuple-element.66), channel_id=1, source_target_pairs={{0,1},{1,0},{2,3},{3,2},{4,5},{5,4},{6,7},{7,6},{8,9},{9,8},{10,11... | collective-permute-start | bytes 7077896 | tf_op jit(solution)/shard_map/ppermute | solution.py:955
  217.1 29.0 %collective-permute-start.8 = (bf16[768,768]{1,0:T(8,128)(2,1)}, bf16[768,768]{1,0:T(8,128)(2,1)}, u32[]{:S(2)}, u32[]{:S(2)}) collective-permute-start(bf16[768,768]{1,0:T(8,128)(2,1)} %constant_dynamic-slice_fusion.16), channel_id=1, source_target_pairs={{0,4},{2,6},{4,0},{6,2},{8,12},{10,14},{12,8},{14,10},{16,20},{18,... | collective-permute-start | bytes 3538952 | tf_op jit(solution)/shard_map/ppermute | solution.py:963
  218.8 28.9 %collective-permute-start.7 = (bf16[768,768]{1,0:T(8,128)(2,1)}, bf16[768,768]{1,0:T(8,128)(2,1)}, u32[]{:S(2)}, u32[]{:S(2)}) collective-permute-start(bf16[768,768]{1,0:T(8,128)(2,1)} %constant_dynamic-slice_fusion.17), channel_id=1, source_target_pairs={{0,2},{2,0},{4,6},{6,4},{8,10},{10,8},{12,14},{14,12},{16,18},{18,... | collective-permute-start | bytes 3538952 | tf_op jit(solution)/shard_map/ppermute | solution.py:963
  220.3 25.7 %collective-permute-start.9 = (bf16[192,768]{1,0:T(8,128)(2,1)S(1)}, bf16[192,768]{1,0:T(8,128)(2,1)S(1)}, u32[]{:S(2)}, u32[]{:S(2)}) collective-permute-start(bf16[192,768]{1,0:T(8,128)(2,1)S(1)} %constant_dynamic-slice_fusion.15), channel_id=1, source_target_pairs={{0,8},{2,10},{4,12},{6,14},{8,0},{10,2},{12,4},{14,6},{16,24},{18,... | collective-permute-start | bytes 884744 | tf_op jit(solution)/shard_map/ppermute | solution.py:963
  249.3 60.2 %collective-permute-start.11 = (bf16[384,768]{1,0:T(8,128)(2,1)S(1)}, bf16[384,768]{1,0:T(8,128)(2,1)S(1)}, u32[]{:S(2)}, u32[]{:S(2)}) collective-permute-start(bf16[384,768]{1,0:T(8,128)(2,1)S(1)} %constant_dynamic-slice_fusion.13), channel_id=1, source_target_pairs={{0,2},{2,0},{4,6},{6,4},{8,10},{10,8},{12,14},{14,12},{16,18},{18,... | collective-permute-start | bytes 1769480 | tf_op jit(solution)/shard_map/ppermute | solution.py:963
  251.3 58.2 %collective-permute-start.12 = (bf16[96,768]{1,0:T(8,128)(2,1)S(1)}, bf16[96,768]{1,0:T(8,128)(2,1)S(1)}, u32[]{:S(2)}, u32[]{:S(2)}) collective-permute-start(bf16[96,768]{1,0:T(8,128)(2,1)S(1)} %constant_dynamic-slice_fusion.12), channel_id=1, source_target_pairs={{0,2},{2,0},{4,6},{6,4},{8,10},{10,8},{12,14},{14,12},{16,18},{18,... | collective-permute-start | bytes 442376 | tf_op jit(solution)/shard_map/ppermute | solution.py:963
  251.5 58.2 %collective-permute-start.10 = (bf16[384,768]{1,0:T(8,128)(2,1)S(1)}, bf16[384,768]{1,0:T(8,128)(2,1)S(1)}, u32[]{:S(2)}, u32[]{:S(2)}) collective-permute-start(bf16[384,768]{1,0:T(8,128)(2,1)S(1)} %constant_dynamic-slice_fusion.14), channel_id=1, source_target_pairs={{0,4},{2,6},{4,0},{6,2},{8,12},{10,14},{12,8},{14,10},{16,20},{18,... | collective-permute-start | bytes 1769480 | tf_op jit(solution)/shard_map/ppermute | solution.py:963
  253.0 61.4 %collective-permute-start.16 = (bf16[8,128,384]{2,1,0:T(8,128)(2,1)S(1)}, bf16[8,128,384]{2,1,0:T(8,128)(2,1)S(1)}, u32[]{:S(2)}, u32[]{:S(2)}) collective-permute-start(bf16[8,128,384]{2,1,0:T(8,128)(2,1)S(1)} %bitcast.155), channel_id=1, source_target_pairs={{0,16},{2,18},{4,20},{6,22},{8,24},{10,26},{12,28},{14,30},{16,0},... | collective-permute-start | bytes 2359304 | tf_op jit(solution)/shard_map/ppermute | solution.py:1149
  272.4 42.0 %collective-permute-start.17 = (bf16[4,128,384]{2,1,0:T(8,128)(2,1)}, bf16[4,128,384]{2,1,0:T(8,128)(2,1)S(1)}, u32[]{:S(2)}, u32[]{:S(2)}) collective-permute-start(bf16[4,128,384]{2,1,0:T(8,128)(2,1)} %get-tuple-element.90), channel_id=1, source_target_pairs={{0,16},{2,18},{4,20},{6,22},{8,24},{10,26},{12,28},{14,30},{1,17},... | collective-permute-start | bytes 1179656 | tf_op jit(solution)/shard_map/ppermute | solution.py:1157
  311.0 15.9 %collective-permute-start.14 = (bf16[192,768]{1,0:T(8,128)(2,1)S(1)}, bf16[192,768]{1,0:T(8,128)(2,1)S(1)}, u32[]{:S(2)}, u32[]{:S(2)}) collective-permute-start(bf16[192,768]{1,0:T(8,128)(2,1)S(1)} %constant_dynamic-slice_fusion.10), channel_id=1, source_target_pairs={{0,8},{2,10},{4,12},{6,14},{8,0},{10,2},{12,4},{14,6},{16,24},{18,... | collective-permute-start | bytes 884744 | tf_op jit(solution)/shard_map/ppermute | solution.py:963
  326.0 73.1 %collective-permute-start.23 = (bf16[384,640]{1,0:T(8,128)(2,1)}, bf16[384,640]{1,0:T(8,128)(2,1)}, u32[]{:S(2)}, u32[]{:S(2)}) collective-permute-start(bf16[384,640]{1,0:T(8,128)(2,1)} %get-tuple-element.97), channel_id=1, source_target_pairs={{0,1},{1,0},{2,3},{3,2},{4,5},{5,4},{6,7},{7,6},{8,9},{9,8},{10,11... | collective-permute-start | bytes 1474568 | tf_op jit(solution)/shard_map/ppermute | solution.py:955
  336.4 19.4 %collective-permute-start.52 = (bf16[96,768]{1,0:T(8,128)(2,1)}, bf16[96,768]{1,0:T(8,128)(2,1)}, u32[]{:S(2)}, u32[]{:S(2)}) collective-permute-start(bf16[96,768]{1,0:T(8,128)(2,1)} %constant_dynamic-slice_fusion), channel_id=1, source_target_pairs={{0,16},{2,18},{4,20},{6,22},{8,24},{10,26},{12,28},{14,30},{16,0},... | collective-permute-start | bytes 442376 | tf_op jit(solution)/shard_map/ppermute | solution.py:963
  341.7 18.1 %collective-permute-start.47 = (bf16[96,768]{1,0:T(8,128)(2,1)}, bf16[96,768]{1,0:T(8,128)(2,1)}, u32[]{:S(2)}, u32[]{:S(2)}) collective-permute-start(bf16[96,768]{1,0:T(8,128)(2,1)} %constant_dynamic-slice_fusion.1), channel_id=1, source_target_pairs={{0,16},{2,18},{4,20},{6,22},{8,24},{10,26},{12,28},{14,30},{16,0},... | collective-permute-start | bytes 442376 | tf_op jit(solution)/shard_map/ppermute | solution.py:963
  341.7 152.6 %all-to-all-start.3 = ((bf16[8,256,768]{2,1,0:T(8,128)(2,1)}), bf16[8,256,768]{2,1,0:T(8,128)(2,1)S(1)}, u32[]{:S(2)}, u32[]{:S(2)}) async-start(bf16[8,256,768]{2,1,0:T(8,128)(2,1)} %get-tuple-element.92), calls=%async_computation.3 | async-start | bytes 6291456 | tf_op jit(solution)/shard_map/all_to_all | solution.py:1104
  356.8 35.0 %collective-permute-start.53 = (bf16[96,768]{1,0:T(8,128)(2,1)S(1)}, bf16[96,768]{1,0:T(8,128)(2,1)S(1)}, u32[]{:S(2)}, u32[]{:S(2)}) collective-permute-start(bf16[96,768]{1,0:T(8,128)(2,1)S(1)} %add_convert_fusion.10), channel_id=1, source_target_pairs={{0,16},{2,18},{4,20},{6,22},{8,24},{10,26},{12,28},{14,30},{16,0},... | collective-permute-start | bytes 442376 | tf_op jit(solution)/shard_map/ppermute | solution.py:963
  360.7 35.7 %collective-permute-start.48 = (bf16[96,768]{1,0:T(8,128)(2,1)S(1)}, bf16[96,768]{1,0:T(8,128)(2,1)S(1)}, u32[]{:S(2)}, u32[]{:S(2)}) collective-permute-start(bf16[96,768]{1,0:T(8,128)(2,1)S(1)} %add_convert_fusion.11), channel_id=1, source_target_pairs={{0,16},{2,18},{4,20},{6,22},{8,24},{10,26},{12,28},{14,30},{16,0},... | collective-permute-start | bytes 442376 | tf_op jit(solution)/shard_map/ppermute | solution.py:963
  365.0 33.9 %collective-permute-start.45 = (bf16[96,768]{1,0:T(8,128)(2,1)S(1)}, bf16[96,768]{1,0:T(8,128)(2,1)S(1)}, u32[]{:S(2)}, u32[]{:S(2)}) collective-permute-start(bf16[96,768]{1,0:T(8,128)(2,1)S(1)} %pad_maximum_fusion.9), channel_id=1, source_target_pairs={{0,2},{2,0},{4,6},{6,4},{8,10},{10,8},{12,14},{14,12},{16,18},{18,... | collective-permute-start | bytes 442376 | tf_op jit(solution)/shard_map/ppermute | solution.py:963
  391.9 41.3 %collective-permute-start.54 = (bf16[192,768]{1,0:T(8,128)(2,1)S(1)}, bf16[192,768]{1,0:T(8,128)(2,1)S(1)}, u32[]{:S(2)}, u32[]{:S(2)}) collective-permute-start(bf16[192,768]{1,0:T(8,128)(2,1)S(1)} %pad_maximum_fusion.8), channel_id=1, source_target_pairs={{0,8},{2,10},{4,12},{6,14},{8,0},{10,2},{12,4},{14,6},{16,24},{18,... | collective-permute-start | bytes 884744 | tf_op jit(solution)/shard_map/ppermute | solution.py:963
  396.4 39.3 %collective-permute-start.49 = (bf16[192,768]{1,0:T(8,128)(2,1)S(1)}, bf16[192,768]{1,0:T(8,128)(2,1)S(1)}, u32[]{:S(2)}, u32[]{:S(2)}) collective-permute-start(bf16[192,768]{1,0:T(8,128)(2,1)S(1)} %pad_maximum_fusion.7), channel_id=1, source_target_pairs={{0,8},{2,10},{4,12},{6,14},{8,0},{10,2},{12,4},{14,6},{16,24},{18,... | collective-permute-start | bytes 884744 | tf_op jit(solution)/shard_map/ppermute | solution.py:963
  399.0 38.2 %collective-permute-start.46 = (bf16[192,768]{1,0:T(8,128)(2,1)S(1)}, bf16[192,768]{1,0:T(8,128)(2,1)S(1)}, u32[]{:S(2)}, u32[]{:S(2)}) collective-permute-start(bf16[192,768]{1,0:T(8,128)(2,1)S(1)} %pad_maximum_fusion.6), channel_id=1, source_target_pairs={{0,8},{2,10},{4,12},{6,14},{8,0},{10,2},{12,4},{14,6},{16,24},{18,... | collective-permute-start | bytes 884744 | tf_op jit(solution)/shard_map/ppermute | solution.py:963
  435.7 27.9 %collective-permute-start.55 = (bf16[384,768]{1,0:T(8,128)(2,1)S(1)}, bf16[384,768]{1,0:T(8,128)(2,1)S(1)}, u32[]{:S(2)}, u32[]{:S(2)}) collective-permute-start(bf16[384,768]{1,0:T(8,128)(2,1)S(1)} %pad_maximum_fusion.5), channel_id=1, source_target_pairs={{0,2},{2,0},{4,6},{6,4},{8,10},{10,8},{12,14},{14,12},{16,18},{18,... | collective-permute-start | bytes 1769480 | tf_op jit(solution)/shard_map/ppermute | solution.py:963
  437.2 21.1 %collective-permute-start.50 = (bf16[384,768]{1,0:T(8,128)(2,1)S(1)}, bf16[384,768]{1,0:T(8,128)(2,1)S(1)}, u32[]{:S(2)}, u32[]{:S(2)}) collective-permute-start(bf16[384,768]{1,0:T(8,128)(2,1)S(1)} %pad_maximum_fusion.4), channel_id=1, source_target_pairs={{0,4},{2,6},{4,0},{6,2},{8,12},{10,14},{12,8},{14,10},{16,20},{18,... | collective-permute-start | bytes 1769480 | tf_op jit(solution)/shard_map/ppermute | solution.py:963
  459.8 25.6 %collective-permute-start.51 = (bf16[768,768]{1,0:T(8,128)(2,1)}, bf16[768,768]{1,0:T(8,128)(2,1)}, u32[]{:S(2)}, u32[]{:S(2)}) collective-permute-start(bf16[768,768]{1,0:T(8,128)(2,1)} %pad_maximum_fusion.2), channel_id=1, source_target_pairs={{0,2},{2,0},{4,6},{6,4},{8,10},{10,8},{12,14},{14,12},{16,18},{18,... | collective-permute-start | bytes 3538952 | tf_op jit(solution)/shard_map/ppermute | solution.py:963
  465.1 22.5 %collective-permute-start.56 = (bf16[768,768]{1,0:T(8,128)(2,1)}, bf16[768,768]{1,0:T(8,128)(2,1)}, u32[]{:S(2)}, u32[]{:S(2)}) collective-permute-start(bf16[768,768]{1,0:T(8,128)(2,1)} %pad_maximum_fusion.3), channel_id=1, source_target_pairs={{0,4},{2,6},{4,0},{6,2},{8,12},{10,14},{12,8},{14,10},{16,20},{18,... | collective-permute-start | bytes 3538952 | tf_op jit(solution)/shard_map/ppermute | solution.py:963
  (78 other events, 575.3 us)
Sparse Core Ops, SparseCore 0:
  9.7 11.9 all-gather.3
  23.2 15.6 all-gather.5
  40.4 15.5 all-gather.7

commit v3 on v2

--- a/solution.py
+++ b/solution.py
@@ -118,6 +118,8 @@
     keep_ref,
     send_ref,
     cols_ref,
+    gain_ref,
+    shift_ref,
     weight_ref,
     acc_ref,
 ):
@@ -156,8 +158,12 @@
     def _():
         own = pl.ds(pl.multiple_of(at_ref[0] * half, half), half)
         rest = pl.ds(pl.multiple_of((1 - at_ref[0]) * half, half), half)
-        keep_ref[...] = acc_ref[own, :].astype(BF16)
-        send_ref[...] = acc_ref[rest, :].astype(BF16)
+        weight = weight_ref[...].astype(F32)
+        gain_ref[...] = jnp.sum(acc_ref[...] * weight, axis=1, keepdims=True)
+        shift_ref[...] = jnp.sum(cols_ref[...] * weight, axis=1, keepdims=True)
+        for ref, at in ((keep_ref, own), (send_ref, rest)):
+            ref[:, :width] = acc_ref[at, :].astype(BF16)
+            ref[:, width:] = jnp.zeros((half, ref.shape[1] - width), BF16)
 
 
 def unproject(at, halo_count, low, packed, extra, extra_halo, mine, other):
@@ -186,9 +192,11 @@
             ],
             out_specs=[
                 pl.BlockSpec((2, rows, model), each),
-                pl.BlockSpec((half, width), whole),
-                pl.BlockSpec((half, width), whole),
+                pl.BlockSpec((half, model), whole),
+                pl.BlockSpec((half, model), whole),
                 pl.BlockSpec((1, width), whole),
+                pl.BlockSpec((model, 1), whole),
+                pl.BlockSpec((model, 1), whole),
             ],
             scratch_shapes=[
                 pltpu.VMEM((2 * half, width), BF16),
@@ -197,9 +205,11 @@
         ),
         out_shape=[
             jax.ShapeDtypeStruct((sources, rows, model), BF16),
-            jax.ShapeDtypeStruct((half, width), BF16),
-            jax.ShapeDtypeStruct((half, width), BF16),
+            jax.ShapeDtypeStruct((half, model), BF16),
+            jax.ShapeDtypeStruct((half, model), BF16),
             jax.ShapeDtypeStruct((1, width), F32),
+            jax.ShapeDtypeStruct((model, 1), F32),
+            jax.ShapeDtypeStruct((model, 1), F32),
         ],
         compiler_params=PARAMS,
         name="unproject",
@@ -224,9 +234,8 @@
     dmixed_ref,
     din_keep_ref,
     din_send_ref,
-    dback_ref,
-    dout_keep_ref,
-    dout_send_ref,
+    dback_keep_ref,
+    dback_send_ref,
     din_b_ref,
     vectors_ref,
     attended_ref,
@@ -255,29 +264,35 @@
         middle = middle + out_b_ref[...]
         middle_ref[...] = middle
         low_ref[...] = norm_forward(middle, gain_ref[...], bias_ref[...])[0].astype(BF16)
-
-    hidden_pre = dot_plain(low_ref[...], in_w_ref[...]) + in_b_ref[...]
-    grad_hidden = dot_transposed(ups_ref[...], back_w_ref[...])
-    below = 0.5 * (1.0 + lax.erf(hidden_pre * 0.5**0.5))
-    hidden = (hidden_pre * below).astype(BF16)
-    density = jnp.exp(-0.5 * hidden_pre * hidden_pre) * 0.3989422804014327
-    grad_pre_wide = grad_hidden * (below + hidden_pre * density)
-    grad_pre = grad_pre_wide.astype(BF16)
-    din_b_ref[0] = jnp.sum(grad_pre.astype(F32), axis=0, keepdims=True)
-    share = dot_plain(hidden, back_w_ref[...])
-    grad_share = dot_transposed(grad_pre, in_w_ref[...])
-    dback_ref[0] = dot_inner(hidden, ups_ref[...]).astype(BF16)
-    square_ref[...] = dot_inner(low_ref[...], grad_pre).astype(BF16)
-    din_keep_ref[0] = square_ref[own, :]
-    din_send_ref[0] = square_ref[rest, :]
-
-    @pl.when(step == 0)
+        acc_ref[...] = jnp.zeros_like(acc_ref)
+        grad_acc_ref[...] = jnp.zeros_like(grad_acc_ref)
+
+    @pl.when(step < pl.num_programs(0) - 1)
     def _():
-        acc_ref[...] = share
-        grad_acc_ref[...] = grad_share
-
-    @pl.when(step > 0)
-    def _():
+        hidden_pre = dot_plain(low_ref[...], in_w_ref[...]) + in_b_ref[...]
+        grad_hidden = dot_transposed(ups_ref[...], back_w_ref[...])
+        below = 0.5 * (1.0 + lax.erf(hidden_pre * 0.5**0.5))
+        hidden = (hidden_pre * below).astype(BF16)
+        density = jnp.exp(-0.5 * hidden_pre * hidden_pre) * 0.3989422804014327
+        grad_pre_wide = grad_hidden * (below + hidden_pre * density)
+        grad_pre = grad_pre_wide.astype(BF16)
+        din_b_ref[0] = jnp.sum(grad_pre.astype(F32), axis=0, keepdims=True)
+        share = dot_plain(hidden, back_w_ref[...])
+        grad_share = dot_transposed(grad_pre, in_w_ref[...])
+        dback = dot_inner(hidden, ups_ref[...]).astype(BF16)
+
+        @pl.when(step < (pl.num_programs(0) - 1) // 2)
+        def _():
+            dback_keep_ref[0] = dback
+
+        @pl.when(step >= (pl.num_programs(0) - 1) // 2)
+        def _():
+            dback_send_ref[0] = dback
+
+        square_ref[...] = dot_inner(low_ref[...], grad_pre).astype(BF16)
+        din_keep_ref[0] = square_ref[own, :]
+        din_send_ref[0] = square_ref[rest, :]
+
         acc_ref[...] += share
         grad_acc_ref[...] += grad_share
 
@@ -292,8 +307,8 @@
         dmid_ref[...] = dmid
         branch = dmid.astype(BF16)
         square_ref[...] = dot_inner(attended_ref[...], branch).astype(BF16)
-        dout_keep_ref[...] = square_ref[own, :]
-        dout_send_ref[...] = square_ref[rest, :]
+        din_keep_ref[0] = square_ref[own, :]
+        din_send_ref[0] = square_ref[rest, :]
         vectors_ref[0:1, :] = jnp.sum(branch.astype(F32), axis=0, keepdims=True)
         vectors_ref[1:2, :] = dgain
         vectors_ref[2:3, :] = dbias
@@ -314,8 +329,14 @@
     whole = lambda i, *unused: (0, 0)
     whole_three = lambda i, *unused: (0, 0, 0)
 
+    def step_at(i):
+        return jnp.minimum(i, blocks - 1)
+
     def block_at(i, at_ref):
-        return (i + at_ref[0] * (blocks // 2)) % blocks
+        return (step_at(i) + at_ref[0] * (blocks // 2)) % blocks
+
+    def grad_at(i, at_ref):
+        return jnp.where(i < blocks, block_at(i, at_ref), blocks)
 
     full = pl.BlockSpec((count, model), whole)
     vector = pl.BlockSpec((1, model), whole)
@@ -323,7 +344,7 @@
         feed_kernel,
         grid_spec=pltpu.PrefetchScalarGridSpec(
             num_scalar_prefetch=1,
-            grid=(blocks,),
+            grid=(blocks + 1,),
             in_specs=[
                 full,
                 full,
@@ -341,11 +362,16 @@
                 full,
                 full,
                 pl.BlockSpec(mixed.shape, whole_three),
-                pl.BlockSpec((1, half, model), lambda i, at_ref: (block_at(i, at_ref), 0, 0)),
-                pl.BlockSpec((1, half, model), lambda i, at_ref: (block_at(i, at_ref), 0, 0)),
-                pl.BlockSpec((1, model, model), lambda i, *unused: (i, 0, 0)),
-                pl.BlockSpec((half, model), whole),
-                pl.BlockSpec((half, model), whole),
+                pl.BlockSpec((1, half, model), lambda i, at_ref: (grad_at(i, at_ref), 0, 0)),
+                pl.BlockSpec((1, half, model), lambda i, at_ref: (grad_at(i, at_ref), 0, 0)),
+                pl.BlockSpec(
+                    (1, model, model),
+                    lambda i, *unused: (jnp.minimum(i, blocks // 2 - 1), 0, 0),
+                ),
+                pl.BlockSpec(
+                    (1, model, model),
+                    lambda i, *unused: (jnp.maximum(step_at(i) - blocks // 2, 0), 0, 0),
+                ),
                 pl.BlockSpec((1, 1, model), lambda i, at_ref: (block_at(i, at_ref), 0, 0)),
                 pl.BlockSpec((4, model), whole),
             ],
@@ -362,11 +388,10 @@
             jax.ShapeDtypeStruct((count, model), BF16),
             jax.ShapeDtypeStruct((count, model), F32),
             jax.ShapeDtypeStruct(mixed.shape, BF16),
-            jax.ShapeDtypeStruct((blocks, half, model), BF16),
-            jax.ShapeDtypeStruct((blocks, half, model), BF16),
-            jax.ShapeDtypeStruct((blocks, model, model), BF16),
-            jax.ShapeDtypeStruct((half, model), BF16),
-            jax.ShapeDtypeStruct((half, model), BF16),
+            jax.ShapeDtypeStruct((blocks + 1, half, model), BF16),
+            jax.ShapeDtypeStruct((blocks + 1, half, model), BF16),
+            jax.ShapeDtypeStruct((blocks // 2, model, model), BF16),
+            jax.ShapeDtypeStruct((blocks // 2, model, model), BF16),
             jax.ShapeDtypeStruct((blocks, 1, model), F32),
             jax.ShapeDtypeStruct((4, model), F32),
         ],
@@ -437,6 +462,8 @@
 
 
 def row_slice(index, size=TILE):
+    if isinstance(index, int):
+        return pl.ds(index * size, size)
     return pl.ds(pl.multiple_of(index * size, size), size)
 
 
@@ -454,7 +481,7 @@
         scores = []
         for sub in range(subs):
             part = dot_transposed(keys_ref[head, row_slice(chunk + sub), :], query)
-            if mask is not None:
+            if mask is not None and sub == subs - 1:
                 part = jnp.where(mask, part, NEGATIVE)
             scores.append(part)
         old = top_ref[query_tile, head]
@@ -482,12 +509,11 @@
 
 
 def walk_local(tiles, scalars_ref, starts_ref, step):
-    wide = 2 if tiles % 2 == 0 else 1
+    wide = 4 if tiles % 4 == 0 else 1
 
     def prompt_tile(tile):
-        loop(0, tile, lambda chunk: step(tile, chunk, 1, None))
         down, across = tile_iotas()
-        step(tile, tile, 1, down <= across)
+        step(tile, 0, tile + 1, down <= across)
 
     def cont_tile(tile):
         query_tile = tiles + tile
@@ -502,12 +528,13 @@
 
         loop(scalars_ref[tile], tile + 1, band)
 
-    loop(0, tiles, prompt_tile)
+    for tile in range(tiles):
+        prompt_tile(tile)
     loop(0, tiles, cont_tile)
 
 
 def walk_remote(tiles, parts, halo_tiles, scalars_ref, starts_ref, step, done):
-    wide = 2 if tiles % 2 == 0 else 1
+    wide = 4 if tiles % 4 == 0 else 1
 
     def whole(query_tile, part):
         loop(
@@ -725,7 +752,7 @@
             scores = dot_transposed(keys_ref[head, rows, :], query)
             grad_soft = dot_transposed(values_ref[head, rows, :], ups)
             soft = jnp.exp(scores - logsum)
-            if mask is not None:
+            if mask is not None and sub == subs - 1:
                 soft = jnp.where(mask, soft, 0.0)
             grad_scores = (soft * (grad_soft - delta)).astype(BF16)
             dvalues_ref[head, rows, :] += dot_plain(soft.astype(BF16), ups)
@@ -963,44 +990,6 @@
     return lax.ppermute(value, "ctx", [(i, i ^ (1 << bit)) for i in range(ways)])
 
 
-def reduce_gather(value, sum_bits, gather_bits, pieces):
-    index = lax.axis_index("ctx")
-    rows, width = value.shape
-    size = rows // pieces
-    parts = [value[at * size : (at + 1) * size] for at in range(pieces)]
-    for bit in sum_bits:
-        flag = (index >> bit) & 1
-        for at in range(pieces):
-            count = parts[at].shape[0] // 2
-            keep = lax.dynamic_slice_in_dim(parts[at], flag * count, count, 0)
-            send = lax.dynamic_slice_in_dim(parts[at], (1 - flag) * count, count, 0)
-            got = traded(send, bit)
-            parts[at] = (keep.astype(F32) + got.astype(F32)).astype(BF16)
-    near = [bit for bit in sum_bits if bit < 3] + list(gather_bits)
-    far = [bit for bit in sum_bits if bit >= 3]
-    orders = [far + near[at % len(near) :] + near[: at % len(near)] for at in range(pieces)]
-    parts = [part[None] for part in parts]
-    for step in range(len(orders[0])):
-        for at in range(pieces):
-            flag = (index >> orders[at][step]) & 1
-            mine = parts[at]
-            got = traded(mine, orders[at][step])
-            parts[at] = jnp.where(
-                flag == 0,
-                jnp.concatenate([mine, got], axis=0),
-                jnp.concatenate([got, mine], axis=0),
-            )
-    wanted = sorted(gather_bits, reverse=True) + list(sum_bits)
-    done = []
-    for at in range(pieces):
-        held = list(reversed(orders[at]))
-        count = parts[at].shape[1]
-        split = parts[at].reshape((2,) * len(held) + (count, width))
-        split = split.transpose([held.index(bit) for bit in wanted] + [len(held), len(held) + 1])
-        done.append(split.reshape(1 << len(gather_bits), size, width))
-    return jnp.concatenate(done, axis=1)
-
-
 def scatter_step(parts, orders, step):
     index = lax.axis_index("ctx")
     done = []
@@ -1024,17 +1013,6 @@
         second = jnp.where(flag == 0, got, part)
         done.append(jnp.concatenate([first, second], axis=0))
     return done
-
-
-def small_sum(value):
-    ways = lax.axis_size("ctx")
-    if lax.axis_size("wsh") == 2:
-        value = value + lax.ppermute(value, "wsh", [(0, 1), (1, 0)])
-    else:
-        value = lax.psum(value, "wsh")
-    for bit in range(ways.bit_length() - 1):
-        value = value + traded(value, bit)
-    return value
 
 
 def body(
@@ -1171,9 +1149,8 @@
         dattended,
         din_keep,
         din_send,
-        dback,
-        dout_keep,
-        dout_send,
+        dback_keep,
+        dback_send,
         din_b,
         mid_vectors,
     ) = feed(
@@ -1191,15 +1168,16 @@
         back_w,
     )
     ups = exchange(dattended).reshape(HP, 2, stripe, width)
-    in_sum = scatter_rows(din_keep, din_send, 1)
-    back_sum = scatter_rows(
-        dback[: blocks // 2].reshape(-1, model), dback[blocks // 2 :].reshape(-1, model), 0
-    )
-    out_sum = scatter_rows(dout_keep, dout_send, 0)
-    sums = [in_sum.reshape(-1, model), back_sum, out_sum]
+    back_keep = dback_keep.reshape(-1, model)
+    back_send = dback_send.reshape(-1, model)
+    sums = [
+        scatter_rows(din_keep, din_send, 1).reshape(-1, model),
+        scatter_rows(back_keep, back_send, 0),
+    ]
     bits = ways.bit_length() - 1
-    rest = tuple(range(3, bits))
-    orders = [(0, 1, 2) + rest, (1, 0, 2) + rest, (2, 0, 1) + rest]
+    rest = tuple(range(2, bits))
+    orders = [(0, 1) + rest, (1, 0) + rest]
+    own_order = (2, 0, 1) + tuple(range(3, bits))
     *sums, ups = lax.optimization_barrier((*sums, ups))
     sums = scatter_step(sums, orders, 0)
 
@@ -1216,32 +1194,51 @@
     *sums, dpacked = lax.optimization_barrier((*sums, dpacked))
     sums = scatter_step(sums, orders, 2)
     halo_count = jnp.full((1,), halo_blocks, jnp.int32)
-    dlow, keep, send, columns = unproject(
+    dlow, keep, send, columns, gain_rows, shift_rows = unproject(
         at_vector, halo_count, low_all, dpacked, returned[0], returned_halo, first_w, second_w
     )
 
-    *sums, dlow = lax.optimization_barrier((*sums, dlow))
+    upstream = exchange(dlow).reshape(triples, count, model)
     for step in range(3, bits):
         sums = scatter_step(sums, orders, step)
-    for step in reversed(range(bits)):
-        sums = gather_step(sums, orders, step)
-    in_done, back_done, out_done = sums
-
     group_bits = groups.bit_length() - 1
-    sum_bits = list(range(group_bits)) + list(range(3, ways.bit_length() - 1))
-    last = reduce_gather(scatter_rows(keep, send, 0), sum_bits, range(group_bits, 3), 3)
-
-    upstream = exchange(dlow).reshape(triples, count, model)
+    sum_bits = list(range(group_bits)) + list(range(3, bits))
+    own_sum = scatter_rows(keep, send, 0)
+    for bit in sum_bits:
+        (own_sum,) = scatter_step([own_sum], [(bit,)], 0)
     upstream = jnp.sum(upstream.astype(F32), axis=0)
     unused, hat_one, scale_one = norm_forward(inputs, gain_one, bias_one)
-    change, grad_gain_one, grad_bias_one = norm_backward(upstream, hat_one, scale_one, gain_one)
+    change = norm_backward(upstream, hat_one, scale_one, gain_one)[0]
     grad_rows = grad_middle + change
+
+    grad_bias_one = shift_rows.reshape(1, model)
+    grad_gain_one = (gain_rows.reshape(1, model) - bias_one * grad_bias_one) / gain_one
     place = (jnp.arange(triples) == triple_at)[:, None]
     spread = jnp.where(place, columns, 0.0)
     pieces = [mid_vectors, din_b, grad_gain_one, grad_bias_one, spread]
     flat = jnp.concatenate([piece.reshape(-1) for piece in pieces])
     length = flat.shape[0]
-    flat = small_sum(flat.reshape(-1, 128)).reshape(-1)
+    flat = flat.reshape(-1, 128)
+    if shards == 2:
+        flat = flat + lax.ppermute(flat, "wsh", [(0, 1), (1, 0)])
+    else:
+        flat = lax.psum(flat, "wsh")
+    for bit in range(bits):
+        flat = flat + traded(flat, bit)
+    own_piece = own_sum[None]
+    for step in reversed(range(bits)):
+        (own_piece,) = gather_step([own_piece], [own_order], step)
+        sums = gather_step(sums, orders, step)
+    flat = flat.reshape(-1)
+    in_rows = blocks * shard_rows
+    first_sum = sums[0].reshape(-1, model)
+    in_done, out_done = first_sum[:in_rows], first_sum[in_rows:]
+    back_done = sums[1]
+    piece_rows = own_piece.shape[1]
+    own_piece = own_piece.reshape((2,) * bits + (piece_rows, model))
+    wanted = list(range(2, group_bits - 1, -1)) + sum_bits
+    own_piece = own_piece.transpose([own_order.index(bit) for bit in wanted] + [bits, bits + 1])
+    last = own_piece.reshape(triples, shard_rows, model)
 
     def own(vector):
         size = vector.shape[0] // shards

time: 544 us -> 529 us (0.972)
  starting transfers between devices: 158 us -> 107 us
  waiting for transfers between devices: 114 us -> 160 us
  Pallas kernels: 147 us -> 135 us
    ppermute x46 -> x26, waiting for transfers between devices: 41.3 us -> 76.6 us  [traded(): return lax.ppermute(value, 'ctx', [(i, i ^ 1 << bit) for i in range(ways)])]
    ppermute x46 -> x26, starting transfers between devices: 102 us -> 71.1 us  [traded(): return lax.ppermute(value, 'ctx', [(i, i ^ 1 << bit) for i in range(ways)])]
    ppermute x2, starting transfers between devices: 22.1 us -> 9.1 us  [shifted(): return lax.ppermute(value, 'ctx', pairs)]
    pallas_call x1, Pallas kernels: 30.5 us -> 22.6 us  [forward_local(): pl.pallas_call(forward_local_kernel, in_specs=[SMEM_SPEC] + vmem_specs(2)...]
    ppermute x1, waiting for transfers between devices: 17.3 us -> 25 us  [to_former(): return lax.ppermute(value, 'ctx', pairs)]
    all_to_all x4, starting transfers between devices: 28.9 us -> 21.8 us  [exchange(): return lax.all_to_all(value, 'ctx', 0, 0, axis_index_groups=cube)]
    all_to_all x4, waiting for transfers between devices: 48.9 us -> 54.8 us  [exchange(): return lax.all_to_all(value, 'ctx', 0, 0, axis_index_groups=cube)]
    unnamed x102 -> x124, local copies, waits for them, and re-layouts: 15.6 us -> 19.4 us
  transfers between devices with their start and end apart: 64 -> 43, of which waited for: 23 -> 24; matrix products, arithmetic and copies ran while one was open for 14% -> 17% of each run, Pallas kernels for 22% -> 18%
where the time goes in v3:
time: 529 us; the launch traced here: 523 us
  waiting for transfers between devices  160 us (30%)
  Pallas kernels  135 us (26%)
  starting transfers between devices  107 us (20%)
  local copies, waits for them, and re-layouts  56.3 us (11%)
  other arithmetic  49.6 us (9%)
  between operations  15.1 us (3%)
    ppermute x26, waiting for transfers between devices, traded(): return lax.ppermute(value, 'ctx', [(i, i ^ 1 << bit) for i in range(ways)])  76.6 us
    ppermute x26, starting transfers between devices, traded(): return lax.ppermute(value, 'ctx', [(i, i ^ 1 << bit) for i in range(ways)])  71.1 us
    all_to_all x4, waiting for transfers between devices, exchange(): return lax.all_to_all(value, 'ctx', 0, 0, axis_index_groups=cube)  54.8 us
    pallas_call x1, Pallas kernels, backward_local(): pl.pallas_call(backward_local_kernel, in_specs=[SMEM_SPEC] + vmem_specs(6...  30.9 us
    pallas_call x1, Pallas kernels, feed(): pl.pallas_call(feed_kernel, grid_spec=pltpu.PrefetchScalarGridSpec(num_sc...  30.4 us
    ppermute x1, waiting for transfers between devices, to_former(): return lax.ppermute(value, 'ctx', pairs)  25 us
    pallas_call x1, Pallas kernels, forward_local(): pl.pallas_call(forward_local_kernel, in_specs=[SMEM_SPEC] + vmem_specs(2)...  22.6 us
    all_to_all x4, starting transfers between devices, exchange(): return lax.all_to_all(value, 'ctx', 0, 0, axis_index_groups=cube)  21.8 us
  transfers between devices with their start and end apart: 43, of which 24 were waited for; matrix products, arithmetic and copies ran while one was open for 17% of the time, Pallas kernels for 18%

profile of v3, /device:TPU:0, one launch (start us, length us, event | category | flops | bytes accessed | tf_op | source)
XLA Modules:
  0.0 522.9 jit_solution(6351959190996025223)
XLA Ops:
  13.1 5.7 %all-to-all-start = ((bf16[8,256,768]{2,1,0:T(8,128)(2,1)}), bf16[8,256,768]{2,1,0:T(8,128)(2,1)}, u32[]{:S(2)}, u32[]{:S(2)}) async-start(bf16[8,256,768]{2,1,0:T(8,128)(2,1)} %bitcast.103), calls=%async_computation | async-start | bytes 6291456 | tf_op jit(solution)/shard_map/all_to_all | solution.py:1082
  23.4 33.7 %all-to-all-done.low_ref = bf16[8,256,768]{2,1,0:T(8,128)(2,1)} async-done(((bf16[8,256,768]{2,1,0:T(8,128)(2,1)}), bf16[8,256,768]{2,1,0:T(8,128)(2,1)}, u32[]{:S(2)}, u32[]{:S(2)}) %all-to-all-start) | async-done | bytes 3145760 | tf_op jit(solution)/shard_map/all_to_all | solution.py:1082
  57.1 6.2 %project.1 = bf16[8,256,640]{2,1,0:T(8,128)(2,1)} custom-call(s32[1]{0:T(128)} %bitcast.at_ref, bf16[8,256,768]{2,1,0:T(8,128)(2,1)} %all-to-all-done.low_ref, bf16[384,640]{1,0:T(8,128)(2,1)} %copy-done.18, bf16[384,640]{1,0:T(8,128)(2,1)} %copy-done.28, f32[1,640]{1,0:T(1,128)} %reshape_maximum_fusion.add_ref), custom_call_target="tpu_custom_call" | custom-call | tf_op jit(solution)/shard_map/project/pallas_call | solution.py:88
  70.7 22.6 %forward_local.1 = (f32[8,3,1,256]{3,2,1,0:T(1,128)}, f32[8,3,1,256]{3,2,1,0:T(1,128)}, f32[8,3,64,256]{3,2,1,0:T(8,128)}) custom-call(s32[9]{0:T(128)} %pad_add_fusion.scalars_ref, s32[4,1,256]{2,1,0:T(1,128)} %bitcast.123, bf16[8,2,128,640]{3,2,1,0:T(8,128)(2,1)} %bitcast.95), custom_call_target="tpu_custom_call" | custom-call | tf_op jit(solution)/shard_map/forward_local/pallas_call | solution.py:683
  93.3 25.0 %collective-permute-done.3.halo_ref = bf16[4,128,384]{2,1,0:T(8,128)(2,1)S(1)} collective-permute-done((bf16[4,128,384]{2,1,0:T(8,128)(2,1)S(1)}, bf16[4,128,384]{2,1,0:T(8,128)(2,1)S(1)}, u32[]{:S(2)}, u32[]{:S(2)}) %collective-permute-start.3) | collective-permute-done | bytes 393248 | tf_op jit(solution)/shard_map/ppermute | solution.py:1131
  119.3 14.6 %forward_remote.1 = (bf16[8,2,128,192]{3,2,1,0:T(8,128)(2,1)}, f32[8,3,1,256]{3,2,1,0:T(1,128)}, f32[8,3,64,256]{3,2,1,0:T(8,128)}) custom-call(s32[9]{0:T(128)} %pad_add_fusion.scalars_ref, s32[4,1,256]{2,1,0:T(1,128)} %bitcast.124, bf16[8,2,128,640]{3,2,1,0:T(8,128)(2,1)} %bitcast.96, bf16[1,8,128,384]{3,2,1,0:T(8,128)(2,1)} %bitcast.115, ...), custom_call_target="tpu_custom_call" | custom-call | tf_op jit(solution)/shard_map/forward_remote/pallas_call | solution.py:708
  136.1 8.1 %all-to-all-start.1 = ((bf16[8,256,192]{1,2,0:T(8,128)(2,1)}), bf16[8,256,192]{1,2,0:T(8,128)(2,1)S(1)}, u32[]{:S(2)}, u32[]{:S(2)}) async-start(bf16[8,256,192]{1,2,0:T(8,128)(2,1)} %copy.56), calls=%async_computation.1 | async-start | bytes 1572864 | tf_op jit(solution)/shard_map/all_to_all | solution.py:1082
  147.2 8.9 %all-to-all-done.1 = bf16[8,256,192]{1,2,0:T(8,128)(2,1)S(1)} async-done(((bf16[8,256,192]{1,2,0:T(8,128)(2,1)}), bf16[8,256,192]{1,2,0:T(8,128)(2,1)S(1)}, u32[]{:S(2)}, u32[]{:S(2)}) %all-to-all-start.1) | async-done | bytes 786464 | tf_op jit(solution)/shard_map/all_to_all | solution.py:1082
  157.3 30.4 %feed.1 = (bf16[512,768]{1,0:T(8,128)(2,1)}, f32[512,768]{1,0:T(8,128)}, bf16[8,256,192]{2,1,0:T(8,128)(2,1)}, bf16[5,384,768]{2,1,0:T(8,128)(2,1)}, bf16[5,384,...) custom-call(s32[1]{0:T(128)} %bitcast.at_ref, ...), custom_call_target="tpu_custom_call" | custom-call | tf_op jit(solution)/shard_map/feed/pallas_call | solution.py:343
  190.5 4.1 all-to-all-start.2
  194.7 12.1 %all-to-all-done.2 = bf16[8,256,192]{1,2,0:T(8,128)(2,1)S(1)} async-done(((bf16[8,256,192]{1,2,0:T(8,128)(2,1)}), bf16[8,256,192]{1,2,0:T(8,128)(2,1)S(1)}, u32[]{:S(2)}, u32[]{:S(2)}) %all-to-all-start.2) | async-done | bytes 786464 | tf_op jit(solution)/shard_map/all_to_all | solution.py:1082
  210.6 3.4 add_convert_fusion
  218.4 19.4 %backward_remote.1 = (bf16[1,8,128,384]{3,2,1,0:T(8,128)(2,1)}, bf16[4,128,384]{2,1,0:T(8,128)(2,1)}, f32[8,3,64,256]{3,2,1,0:T(8,128)}, f32[8,3,1,256]{3,2,1,0:T(1,128)}) custom-call(s32[9]{0:T(128)} %pad_add_fusion.scalars_ref, s32[4,1,256]{2,1,0:T(1,128)} %bitcast.125, bf16[8,2,128,640]{3,2,1,0:T(8,128)(2,1)} %bitcast.97, ...), custom_call_target="tpu_custom_call" | custom-call | tf_op jit(solution)/shard_map/backward_remote/pallas_call | solution.py:923
  237.9 7.0 %collective-permute-done.7 = bf16[768,768]{1,0:T(8,128)(2,1)} collective-permute-done((bf16[768,768]{1,0:T(8,128)(2,1)}, bf16[768,768]{1,0:T(8,128)(2,1)}, u32[]{:S(2)}, u32[]{:S(2)}) %collective-permute-start.7) | collective-permute-done | bytes 1179680 | tf_op jit(solution)/shard_map/ppermute | solution.py:990
  253.1 6.4 %collective-permute-start.10 = (bf16[8,128,384]{2,1,0:T(8,128)(2,1)}, bf16[8,128,384]{2,1,0:T(8,128)(2,1)S(1)}, u32[]{:S(2)}, u32[]{:S(2)}) collective-permute-start(bf16[8,128,384]{2,1,0:T(8,128)(2,1)} %bitcast.26), channel_id=1, source_target_pairs={{0,16},{2,18},{4,20},{6,22},{8,24},{10,26},{12,28},{14,30},{16,0},... | collective-permute-start | bytes 2359304 | tf_op jit(solution)/shard_map/ppermute | solution.py:1127
  261.7 30.9 %backward_local.1.packed_ref = bf16[8,2,128,640]{3,2,1,0:T(8,128)(2,1)} custom-call(s32[9]{0:T(128)} %pad_add_fusion.scalars_ref, s32[4,1,256]{2,1,0:T(1,128)} %bitcast.126, bf16[8,2,128,640]{3,2,1,0:T(8,128)(2,1)} %bitcast.98, bf16[8,2,128,192]{3,2,1,0:T(8,128)(2,1)} %bitcast.108, f32[8,3,1,256]{3,2,1,0:T(1,128)} %get-tuple-element.67.log_ref, ...), custom_call_target="tpu_custom_call" | custom-call | tf_op jit(solution)/shard_map/backward_local/pallas_call | solution.py:952
  296.1 10.6 %unproject.1 = (bf16[8,256,768]{2,1,0:T(8,128)(2,1)}, bf16[384,768]{1,0:T(8,128)(2,1)}, bf16[384,768]{1,0:T(8,128)(2,1)}, f32[1,640]{1,0:T(1,128)}, f32[768,1]{1,0:T(8,128)}, /*index=5*/f32[768,1]{1,0:T(8,128)}) custom-call(s32[1]{0:T(128)} %bitcast.at_ref, s32[1]{0:T(128)} %constant.120.clone.1.halo_ref, bf16[8,256,768]{2,1,0:T(8,128)(2,1)} %all-to-all-done.low_ref, ...), custom_call_target="tpu_custom_call" | custom-call | tf_op jit(solution)/shard_map/unproject/pallas_call | solution.py:177
  311.2 4.0 collective-permute-done.13
  319.3 16.2 %collective-permute-start.15 = (f32[80,128]{1,0:T(8,128)S(1)}, f32[80,128]{1,0:T(8,128)S(1)}, u32[]{:S(2)}, u32[]{:S(2)}) collective-permute-start(f32[80,128]{1,0:T(8,128)S(1)} %add.211), channel_id=1, source_target_pairs={{0,8},{2,10},{4,12},{6,14},{8,0},{10,2},{12,4},{14,6},{16,24},{18,... | collective-permute-start | bytes 122888 | tf_op jit(solution)/shard_map/ppermute | solution.py:990
  337.9 3.3 collective-permute-start.16
  343.7 3.9 all-to-all-start.3
  354.8 7.3 %collective-permute-start.25 = (bf16[120,768]{1,0:T(8,128)(2,1)S(1)}, bf16[120,768]{1,0:T(8,128)(2,1)S(1)}, u32[]{:S(2)}, u32[]{:S(2)}) collective-permute-start(bf16[120,768]{1,0:T(8,128)(2,1)S(1)} %constant_dynamic-slice_fusion.2), channel_id=1, source_target_pairs={{0,16},{2,18},{4,20},{6,22},{8,24},{10,26},{12,28},{14,30},{16,0},... | collective-permute-start | bytes 552968 | tf_op jit(solution)/shard_map/ppermute | solution.py:990
  362.1 26.2 %collective-permute-done.31 = bf16[96,768]{1,0:T(8,128)(2,1)S(1)} collective-permute-done((bf16[96,768]{1,0:T(8,128)(2,1)S(1)}, bf16[96,768]{1,0:T(8,128)(2,1)S(1)}, u32[]{:S(2)}, u32[]{:S(2)}) %collective-permute-start.31) | collective-permute-done | bytes 147488 | tf_op jit(solution)/shard_map/ppermute | solution.py:990
  388.3 3.4 collective-permute-start.32
  392.3 3.5 collective-permute-start.26
  397.1 5.7 %collective-permute-start.18 = (bf16[192,768]{1,0:T(8,128)(2,1)S(1)}, bf16[192,768]{1,0:T(8,128)(2,1)S(1)}, u32[]{:S(2)}, u32[]{:S(2)}) collective-permute-start(bf16[192,768]{1,0:T(8,128)(2,1)S(1)} %constant_dynamic-slice_fusion.5), channel_id=1, source_target_pairs={{0,2},{2,0},{4,6},{6,4},{8,10},{10,8},{12,14},{14,12},{16,18},{18,... | collective-permute-start | bytes 884744 | tf_op jit(solution)/shard_map/ppermute | solution.py:990
  402.8 4.5 collective-permute-done.32
  411.9 6.1 %collective-permute-done.19 = bf16[96,768]{1,0:T(8,128)(2,1)S(1)} collective-permute-done((bf16[96,768]{1,0:T(8,128)(2,1)S(1)}, bf16[96,768]{1,0:T(8,128)(2,1)S(1)}, u32[]{:S(2)}, u32[]{:S(2)}) %collective-permute-start.19) | collective-permute-done | bytes 147488 | tf_op jit(solution)/shard_map/ppermute | solution.py:990
  418.0 3.4 collective-permute-start.20
  433.1 7.8 %collective-permute-start.22 = (bf16[4,96,768]{2,1,0:T(8,128)(2,1)}, bf16[4,96,768]{2,1,0:T(8,128)(2,1)}, u32[]{:S(2)}, u32[]{:S(2)}) collective-permute-start(bf16[4,96,768]{2,1,0:T(8,128)(2,1)} %pad_maximum_fusion.6), channel_id=1, source_target_pairs={{0,2},{2,0},{4,6},{6,4},{8,10},{10,8},{12,14},{14,12},{16,18},{18,... | collective-permute-start | bytes 1769480 | tf_op jit(solution)/shard_map/ppermute | solution.py:990
  443.7 8.5 %collective-permute-done.22 = bf16[4,96,768]{2,1,0:T(8,128)(2,1)} collective-permute-done((bf16[4,96,768]{2,1,0:T(8,128)(2,1)}, bf16[4,96,768]{2,1,0:T(8,128)(2,1)}, u32[]{:S(2)}, u32[]{:S(2)}) %collective-permute-start.22) | collective-permute-done | bytes 589856 | tf_op jit(solution)/shard_map/ppermute | solution.py:990
  455.4 3.4 collective-permute-start.23
  (331 shorter events, 151.5 us)
Async XLA Ops:
  7.3 150.0 %all-gather.4.cloned.1.call-start = ((), (), s32[]{:S(2)}) async-start(), calls=%async_computation.4 | async-start | bytes 1769472 | tf_op jit(solution)/shard_map/all_gather | solution.py:1073
  8.0 149.3 %all-gather.6.cloned.1.call-start = ((), (), s32[]{:S(2)}) async-start(), calls=%async_computation.5 | async-start | bytes 7077888 | tf_op jit(solution)/shard_map/all_gather | solution.py:1074
  13.1 44.0 %all-to-all-start = ((bf16[8,256,768]{2,1,0:T(8,128)(2,1)}), bf16[8,256,768]{2,1,0:T(8,128)(2,1)}, u32[]{:S(2)}, u32[]{:S(2)}) async-start(bf16[8,256,768]{2,1,0:T(8,128)(2,1)} %bitcast.103), calls=%async_computation | async-start | bytes 6291456 | tf_op jit(solution)/shard_map/all_to_all | solution.py:1082
  18.8 138.5 %all-gather.8.cloned.1.call-start = ((), (), s32[]{:S(2)}) async-start(), calls=%async_computation.6 | async-start | bytes 7077888 | tf_op jit(solution)/shard_map/all_gather | solution.py:1075
  64.5 53.8 %collective-permute-start.2 = (bf16[8,128,384]{2,1,0:T(8,128)(2,1)S(1)}, bf16[8,128,384]{2,1,0:T(8,128)(2,1)S(1)}, u32[]{:S(2)}, u32[]{:S(2)}) collective-permute-start(bf16[8,128,384]{2,1,0:T(8,128)(2,1)S(1)} %slice_bitcast_fusion), channel_id=1, source_target_pairs={{0,16},{2,18},{4,20},{6,22},{8,24},{10,26},{12,28},{14,30},{16,0},... | collective-permute-start | bytes 2359304 | tf_op jit(solution)/shard_map/ppermute | solution.py:1127
  68.4 49.9 %collective-permute-start.3 = (bf16[4,128,384]{2,1,0:T(8,128)(2,1)S(1)}, bf16[4,128,384]{2,1,0:T(8,128)(2,1)S(1)}, u32[]{:S(2)}, u32[]{:S(2)}) collective-permute-start(bf16[4,128,384]{2,1,0:T(8,128)(2,1)S(1)} %slice_bitcast_fusion.1), channel_id=1, source_target_pairs={{16,0},{18,2},{20,4},{22,6},{24,8},{26,10},{28,12},{30,14},{17,1},... | collective-permute-start | bytes 1179656 | tf_op jit(solution)/shard_map/ppermute | solution.py:1131
  136.1 19.9 %all-to-all-start.1 = ((bf16[8,256,192]{1,2,0:T(8,128)(2,1)}), bf16[8,256,192]{1,2,0:T(8,128)(2,1)S(1)}, u32[]{:S(2)}, u32[]{:S(2)}) async-start(bf16[8,256,192]{1,2,0:T(8,128)(2,1)} %copy.56), calls=%async_computation.1 | async-start | bytes 1572864 | tf_op jit(solution)/shard_map/all_to_all | solution.py:1082
  187.7 20.4 %collective-permute-start.5 = (bf16[1536,768]{1,0:T(8,128)(2,1)}, bf16[1536,768]{1,0:T(8,128)(2,1)}, u32[]{:S(2)}, u32[]{:S(2)}) collective-permute-start(bf16[1536,768]{1,0:T(8,128)(2,1)} %bitcast.140), channel_id=1, source_target_pairs={{0,1},{1,0},{2,3},{3,2},{4,5},{5,4},{6,7},{7,6},{8,9},{9,8},{10,11... | collective-permute-start | bytes 7077896 | tf_op jit(solution)/shard_map/ppermute | solution.py:982
  187.8 22.7 %collective-permute-start.4 = (bf16[5,384,768]{2,1,0:T(8,128)(2,1)}, bf16[5,384,768]{2,1,0:T(8,128)(2,1)}, u32[]{:S(2)}, u32[]{:S(2)}) collective-permute-start(bf16[5,384,768]{2,1,0:T(8,128)(2,1)} %get-tuple-element.60), channel_id=1, source_target_pairs={{0,1},{1,0},{2,3},{3,2},{4,5},{5,4},{6,7},{7,6},{8,9},{9,8},{10,11... | collective-permute-start | bytes 8847368 | tf_op jit(solution)/shard_map/ppermute | solution.py:982
  190.5 16.3 %all-to-all-start.2 = ((bf16[8,256,192]{1,2,0:T(8,128)(2,1)}), bf16[8,256,192]{1,2,0:T(8,128)(2,1)S(1)}, u32[]{:S(2)}, u32[]{:S(2)}) async-start(bf16[8,256,192]{1,2,0:T(8,128)(2,1)} %copy.58), calls=%async_computation.2 | async-start | bytes 1572864 | tf_op jit(solution)/shard_map/all_to_all | solution.py:1082
  215.3 33.3 %collective-permute-start.6 = (bf16[960,768]{1,0:T(8,128)(2,1)}, bf16[960,768]{1,0:T(8,128)(2,1)}, u32[]{:S(2)}, u32[]{:S(2)}) collective-permute-start(bf16[960,768]{1,0:T(8,128)(2,1)} %constant_dynamic-slice_fusion.9), channel_id=1, source_target_pairs={{0,2},{2,0},{4,6},{6,4},{8,10},{10,8},{12,14},{14,12},{16,18},{18,... | collective-permute-start | bytes 4423688 | tf_op jit(solution)/shard_map/ppermute | solution.py:990
  217.0 27.9 %collective-permute-start.7 = (bf16[768,768]{1,0:T(8,128)(2,1)}, bf16[768,768]{1,0:T(8,128)(2,1)}, u32[]{:S(2)}, u32[]{:S(2)}) collective-permute-start(bf16[768,768]{1,0:T(8,128)(2,1)} %constant_dynamic-slice_fusion.8), channel_id=1, source_target_pairs={{0,4},{2,6},{4,0},{6,2},{8,12},{10,14},{12,8},{14,10},{16,20},{18,... | collective-permute-start | bytes 3538952 | tf_op jit(solution)/shard_map/ppermute | solution.py:990
  250.4 42.2 %collective-permute-start.9 = (bf16[384,768]{1,0:T(8,128)(2,1)S(1)}, bf16[384,768]{1,0:T(8,128)(2,1)S(1)}, u32[]{:S(2)}, u32[]{:S(2)}) collective-permute-start(bf16[384,768]{1,0:T(8,128)(2,1)S(1)} %constant_dynamic-slice_fusion.6), channel_id=1, source_target_pairs={{0,2},{2,0},{4,6},{6,4},{8,10},{10,8},{12,14},{14,12},{16,18},{18,... | collective-permute-start | bytes 1769480 | tf_op jit(solution)/shard_map/ppermute | solution.py:990
  252.3 40.5 %collective-permute-start.8 = (bf16[480,768]{1,0:T(8,128)(2,1)S(1)}, bf16[480,768]{1,0:T(8,128)(2,1)S(1)}, u32[]{:S(2)}, u32[]{:S(2)}) collective-permute-start(bf16[480,768]{1,0:T(8,128)(2,1)S(1)} %constant_dynamic-slice_fusion.7), channel_id=1, source_target_pairs={{0,4},{2,6},{4,0},{6,2},{8,12},{10,14},{12,8},{14,10},{16,20},{18,... | collective-permute-start | bytes 2211848 | tf_op jit(solution)/shard_map/ppermute | solution.py:990
  253.1 41.4 %collective-permute-start.10 = (bf16[8,128,384]{2,1,0:T(8,128)(2,1)}, bf16[8,128,384]{2,1,0:T(8,128)(2,1)S(1)}, u32[]{:S(2)}, u32[]{:S(2)}) collective-permute-start(bf16[8,128,384]{2,1,0:T(8,128)(2,1)} %bitcast.26), channel_id=1, source_target_pairs={{0,16},{2,18},{4,20},{6,22},{8,24},{10,26},{12,28},{14,30},{16,0},... | collective-permute-start | bytes 2359304 | tf_op jit(solution)/shard_map/ppermute | solution.py:1127
  259.6 34.8 %collective-permute-start.11 = (bf16[4,128,384]{2,1,0:T(8,128)(2,1)}, bf16[4,128,384]{2,1,0:T(8,128)(2,1)S(1)}, u32[]{:S(2)}, u32[]{:S(2)}) collective-permute-start(bf16[4,128,384]{2,1,0:T(8,128)(2,1)} %get-tuple-element.78), channel_id=1, source_target_pairs={{0,16},{2,18},{4,20},{6,22},{8,24},{10,26},{12,28},{14,30},{1,17},... | collective-permute-start | bytes 1179656 | tf_op jit(solution)/shard_map/ppermute | solution.py:1135
  319.3 18.6 %collective-permute-start.15 = (f32[80,128]{1,0:T(8,128)S(1)}, f32[80,128]{1,0:T(8,128)S(1)}, u32[]{:S(2)}, u32[]{:S(2)}) collective-permute-start(f32[80,128]{1,0:T(8,128)S(1)} %add.211), channel_id=1, source_target_pairs={{0,8},{2,10},{4,12},{6,14},{8,0},{10,2},{12,4},{14,6},{16,24},{18,... | collective-permute-start | bytes 122888 | tf_op jit(solution)/shard_map/ppermute | solution.py:990
  336.2 12.9 %collective-permute-start.30 = (bf16[192,768]{1,0:T(8,128)(2,1)}, bf16[192,768]{1,0:T(8,128)(2,1)}, u32[]{:S(2)}, u32[]{:S(2)}) collective-permute-start(bf16[192,768]{1,0:T(8,128)(2,1)} %constant_dynamic-slice_fusion.1), channel_id=1, source_target_pairs={{0,8},{2,10},{4,12},{6,14},{8,0},{10,2},{12,4},{14,6},{16,24},{18,... | collective-permute-start | bytes 884744 | tf_op jit(solution)/shard_map/ppermute | solution.py:990
  343.7 52.1 %collective-permute-start.17 = (bf16[384,768]{1,0:T(8,128)(2,1)}, bf16[384,768]{1,0:T(8,128)(2,1)}, u32[]{:S(2)}, u32[]{:S(2)}) collective-permute-start(bf16[384,768]{1,0:T(8,128)(2,1)} %get-tuple-element.86), channel_id=1, source_target_pairs={{0,1},{1,0},{2,3},{3,2},{4,5},{5,4},{6,7},{7,6},{8,9},{9,8},{10,11... | collective-permute-start | bytes 1769480 | tf_op jit(solution)/shard_map/ppermute | solution.py:982
  343.7 168.3 %all-to-all-start.3 = ((bf16[8,256,768]{2,1,0:T(8,128)(2,1)}), bf16[8,256,768]{2,1,0:T(8,128)(2,1)S(1)}, u32[]{:S(2)}, u32[]{:S(2)}) async-start(bf16[8,256,768]{2,1,0:T(8,128)(2,1)} %get-tuple-element.79), calls=%async_computation.3 | async-start | bytes 6291456 | tf_op jit(solution)/shard_map/all_to_all | solution.py:1082
  350.2 38.1 %collective-permute-start.31 = (bf16[96,768]{1,0:T(8,128)(2,1)S(1)}, bf16[96,768]{1,0:T(8,128)(2,1)S(1)}, u32[]{:S(2)}, u32[]{:S(2)}) collective-permute-start(bf16[96,768]{1,0:T(8,128)(2,1)S(1)} %constant_dynamic-slice_fusion), channel_id=1, source_target_pairs={{0,16},{2,18},{4,20},{6,22},{8,24},{10,26},{12,28},{14,30},{16,0},... | collective-permute-start | bytes 442376 | tf_op jit(solution)/shard_map/ppermute | solution.py:990
  354.8 37.4 %collective-permute-start.25 = (bf16[120,768]{1,0:T(8,128)(2,1)S(1)}, bf16[120,768]{1,0:T(8,128)(2,1)S(1)}, u32[]{:S(2)}, u32[]{:S(2)}) collective-permute-start(bf16[120,768]{1,0:T(8,128)(2,1)S(1)} %constant_dynamic-slice_fusion.2), channel_id=1, source_target_pairs={{0,16},{2,18},{4,20},{6,22},{8,24},{10,26},{12,28},{14,30},{16,0},... | collective-permute-start | bytes 552968 | tf_op jit(solution)/shard_map/ppermute | solution.py:990
  388.3 19.0 %collective-permute-start.32 = (bf16[96,768]{1,0:T(8,128)(2,1)S(1)}, bf16[96,768]{1,0:T(8,128)(2,1)S(1)}, u32[]{:S(2)}, u32[]{:S(2)}) collective-permute-start(bf16[96,768]{1,0:T(8,128)(2,1)S(1)} %add_convert_fusion.10), channel_id=1, source_target_pairs={{0,16},{2,18},{4,20},{6,22},{8,24},{10,26},{12,28},{14,30},{16,0},... | collective-permute-start | bytes 442376 | tf_op jit(solution)/shard_map/ppermute | solution.py:990
  392.3 19.4 %collective-permute-start.26 = (bf16[120,768]{1,0:T(8,128)(2,1)S(1)}, bf16[120,768]{1,0:T(8,128)(2,1)S(1)}, u32[]{:S(2)}, u32[]{:S(2)}) collective-permute-start(bf16[120,768]{1,0:T(8,128)(2,1)S(1)} %add_convert_fusion.9), channel_id=1, source_target_pairs={{0,16},{2,18},{4,20},{6,22},{8,24},{10,26},{12,28},{14,30},{16,0},... | collective-permute-start | bytes 552968 | tf_op jit(solution)/shard_map/ppermute | solution.py:990
  407.4 14.7 %collective-permute-start.33 = (bf16[192,768]{1,0:T(8,128)(2,1)S(1)}, bf16[192,768]{1,0:T(8,128)(2,1)S(1)}, u32[]{:S(2)}, u32[]{:S(2)}) collective-permute-start(bf16[192,768]{1,0:T(8,128)(2,1)S(1)} %pad_maximum_fusion.10), channel_id=1, source_target_pairs={{0,8},{2,10},{4,12},{6,14},{8,0},{10,2},{12,4},{14,6},{16,24},{18,... | collective-permute-start | bytes 884744 | tf_op jit(solution)/shard_map/ppermute | solution.py:990
  411.8 16.5 %collective-permute-start.27 = (bf16[240,768]{1,0:T(8,128)(2,1)S(1)}, bf16[240,768]{1,0:T(8,128)(2,1)S(1)}, u32[]{:S(2)}, u32[]{:S(2)}) collective-permute-start(bf16[240,768]{1,0:T(8,128)(2,1)S(1)} %pad_maximum_fusion.8), channel_id=1, source_target_pairs={{0,8},{2,10},{4,12},{6,14},{8,0},{10,2},{12,4},{14,6},{16,24},{18,... | collective-permute-start | bytes 1105928 | tf_op jit(solution)/shard_map/ppermute | solution.py:990
  422.2 18.7 %collective-permute-start.34 = (bf16[384,768]{1,0:T(8,128)(2,1)S(1)}, bf16[384,768]{1,0:T(8,128)(2,1)S(1)}, u32[]{:S(2)}, u32[]{:S(2)}) collective-permute-start(bf16[384,768]{1,0:T(8,128)(2,1)S(1)} %pad_maximum_fusion.7), channel_id=1, source_target_pairs={{0,2},{2,0},{4,6},{6,4},{8,10},{10,8},{12,14},{14,12},{16,18},{18,... | collective-permute-start | bytes 1769480 | tf_op jit(solution)/shard_map/ppermute | solution.py:990
  429.4 38.2 %collective-permute-start.28 = (bf16[480,768]{1,0:T(8,128)(2,1)}, bf16[480,768]{1,0:T(8,128)(2,1)}, u32[]{:S(2)}, u32[]{:S(2)}) collective-permute-start(bf16[480,768]{1,0:T(8,128)(2,1)} %pad_maximum_fusion.5), channel_id=1, source_target_pairs={{0,4},{2,6},{4,0},{6,2},{8,12},{10,14},{12,8},{14,10},{16,20},{18,... | collective-permute-start | bytes 2211848 | tf_op jit(solution)/shard_map/ppermute | solution.py:990
  433.1 19.0 %collective-permute-start.22 = (bf16[4,96,768]{2,1,0:T(8,128)(2,1)}, bf16[4,96,768]{2,1,0:T(8,128)(2,1)}, u32[]{:S(2)}, u32[]{:S(2)}) collective-permute-start(bf16[4,96,768]{2,1,0:T(8,128)(2,1)} %pad_maximum_fusion.6), channel_id=1, source_target_pairs={{0,2},{2,0},{4,6},{6,4},{8,10},{10,8},{12,14},{14,12},{16,18},{18,... | collective-permute-start | bytes 1769480 | tf_op jit(solution)/shard_map/ppermute | solution.py:990
  443.0 31.6 %collective-permute-start.35 = (bf16[768,768]{1,0:T(8,128)(2,1)}, bf16[768,768]{1,0:T(8,128)(2,1)}, u32[]{:S(2)}, u32[]{:S(2)}) collective-permute-start(bf16[768,768]{1,0:T(8,128)(2,1)} %pad_maximum_fusion.4), channel_id=1, source_target_pairs={{0,4},{2,6},{4,0},{6,2},{8,12},{10,14},{12,8},{14,10},{16,20},{18,... | collective-permute-start | bytes 3538952 | tf_op jit(solution)/shard_map/ppermute | solution.py:990
  455.4 26.2 %collective-permute-start.23 = (bf16[8,96,768]{2,1,0:T(8,128)(2,1)}, bf16[8,96,768]{2,1,0:T(8,128)(2,1)}, u32[]{:S(2)}, u32[]{:S(2)}) collective-permute-start(bf16[8,96,768]{2,1,0:T(8,128)(2,1)} %pad_maximum_fusion.3), channel_id=1, source_target_pairs={{0,8},{2,10},{4,12},{6,14},{8,0},{10,2},{12,4},{14,6},{16,24},{18,... | collective-permute-start | bytes 3538952 | tf_op jit(solution)/shard_map/ppermute | solution.py:990
  472.9 30.5 %collective-permute-start.29 = (bf16[960,768]{1,0:T(8,128)(2,1)}, bf16[960,768]{1,0:T(8,128)(2,1)}, u32[]{:S(2)}, u32[]{:S(2)}) collective-permute-start(bf16[960,768]{1,0:T(8,128)(2,1)} %pad_maximum_fusion.2), channel_id=1, source_target_pairs={{0,2},{2,0},{4,6},{6,4},{8,10},{10,8},{12,14},{14,12},{16,18},{18,... | collective-permute-start | bytes 4423688 | tf_op jit(solution)/shard_map/ppermute | solution.py:990
  (68 other events, 867.3 us)
Sparse Core Ops, SparseCore 0:
  9.7 11.9 all-gather.3
  23.2 15.6 all-gather.5
  40.4 15.5 all-gather.7

commit v4 on v3

--- a/solution.py
+++ b/solution.py
@@ -1202,7 +1202,7 @@
     for step in range(3, bits):
         sums = scatter_step(sums, orders, step)
     group_bits = groups.bit_length() - 1
-    sum_bits = list(range(group_bits)) + list(range(3, bits))
+    sum_bits = list(range(3, bits)) + list(range(group_bits))
     own_sum = scatter_rows(keep, send, 0)
     for bit in sum_bits:
         (own_sum,) = scatter_step([own_sum], [(bit,)], 0)

time: 529 us -> 537 us (1.015)
  waiting for transfers between devices: 160 us -> 180 us
  starting transfers between devices: 107 us -> 93.6 us
    ppermute x26, waiting for transfers between devices: 76.6 us -> 97.8 us  [traded(): return lax.ppermute(value, 'ctx', [(i, i ^ 1 << bit) for i in range(ways)])]
    ppermute x26, starting transfers between devices: 71.1 us -> 57.6 us  [traded(): return lax.ppermute(value, 'ctx', [(i, i ^ 1 << bit) for i in range(ways)])]
  transfers between devices with their start and end apart: 43 -> 43, of which waited for: 24 -> 22; matrix products, arithmetic and copies ran while one was open for 17% -> 16% of each run, Pallas kernels for 18% -> 18%
where the time goes in v4:
time: 537 us; the launch traced here: 532 us
  waiting for transfers between devices  180 us (34%)
  Pallas kernels  137 us (26%)
  starting transfers between devices  93.6 us (17%)
  local copies, waits for them, and re-layouts  56.3 us (10%)
  other arithmetic  49.6 us (9%)
  between operations  15.2 us (3%)
    ppermute x26, waiting for transfers between devices, traded(): return lax.ppermute(value, 'ctx', [(i, i ^ 1 << bit) for i in range(ways)])  97.8 us
    ppermute x26, starting transfers between devices, traded(): return lax.ppermute(value, 'ctx', [(i, i ^ 1 << bit) for i in range(ways)])  57.6 us
    all_to_all x4, waiting for transfers between devices, exchange(): return lax.all_to_all(value, 'ctx', 0, 0, axis_index_groups=cube)  53.8 us
    pallas_call x1, Pallas kernels, backward_local(): pl.pallas_call(backward_local_kernel, in_specs=[SMEM_SPEC] + vmem_specs(6...  30.9 us
    pallas_call x1, Pallas kernels, feed(): pl.pallas_call(feed_kernel, grid_spec=pltpu.PrefetchScalarGridSpec(num_sc...  30.4 us
    ppermute x1, waiting for transfers between devices, to_former(): return lax.ppermute(value, 'ctx', pairs)  25 us
    pallas_call x1, Pallas kernels, forward_local(): pl.pallas_call(forward_local_kernel, in_specs=[SMEM_SPEC] + vmem_specs(2)...  22.6 us
    all_to_all x4, starting transfers between devices, exchange(): return lax.all_to_all(value, 'ctx', 0, 0, axis_index_groups=cube)  20.9 us
  transfers between devices with their start and end apart: 43, of which 22 were waited for; matrix products, arithmetic and copies ran while one was open for 16% of the time, Pallas kernels for 18%

profile of v4, /device:TPU:0, one launch (start us, length us, event | category | flops | bytes accessed | tf_op | source)
XLA Modules:
  0.0 531.6 jit_solution(4727328424966150529)
XLA Ops:
  13.1 5.7 %all-to-all-start = ((bf16[8,256,768]{2,1,0:T(8,128)(2,1)}), bf16[8,256,768]{2,1,0:T(8,128)(2,1)}, u32[]{:S(2)}, u32[]{:S(2)}) async-start(bf16[8,256,768]{2,1,0:T(8,128)(2,1)} %bitcast.103), calls=%async_computation | async-start | bytes 6291456 | tf_op jit(solution)/shard_map/all_to_all | solution.py:1082
  23.4 33.7 %all-to-all-done.low_ref = bf16[8,256,768]{2,1,0:T(8,128)(2,1)} async-done(((bf16[8,256,768]{2,1,0:T(8,128)(2,1)}), bf16[8,256,768]{2,1,0:T(8,128)(2,1)}, u32[]{:S(2)}, u32[]{:S(2)}) %all-to-all-start) | async-done | bytes 3145760 | tf_op jit(solution)/shard_map/all_to_all | solution.py:1082
  57.1 6.2 %project.1 = bf16[8,256,640]{2,1,0:T(8,128)(2,1)} custom-call(s32[1]{0:T(128)} %bitcast.at_ref, bf16[8,256,768]{2,1,0:T(8,128)(2,1)} %all-to-all-done.low_ref, bf16[384,640]{1,0:T(8,128)(2,1)} %copy-done.18, bf16[384,640]{1,0:T(8,128)(2,1)} %copy-done.28, f32[1,640]{1,0:T(1,128)} %reshape_maximum_fusion.add_ref), custom_call_target="tpu_custom_call" | custom-call | tf_op jit(solution)/shard_map/project/pallas_call | solution.py:88
  70.7 22.6 %forward_local.1 = (f32[8,3,1,256]{3,2,1,0:T(1,128)}, f32[8,3,1,256]{3,2,1,0:T(1,128)}, f32[8,3,64,256]{3,2,1,0:T(8,128)}) custom-call(s32[9]{0:T(128)} %pad_add_fusion.scalars_ref, s32[4,1,256]{2,1,0:T(1,128)} %bitcast.123, bf16[8,2,128,640]{3,2,1,0:T(8,128)(2,1)} %bitcast.95), custom_call_target="tpu_custom_call" | custom-call | tf_op jit(solution)/shard_map/forward_local/pallas_call | solution.py:683
  93.3 25.0 %collective-permute-done.3.halo_ref = bf16[4,128,384]{2,1,0:T(8,128)(2,1)S(1)} collective-permute-done((bf16[4,128,384]{2,1,0:T(8,128)(2,1)S(1)}, bf16[4,128,384]{2,1,0:T(8,128)(2,1)S(1)}, u32[]{:S(2)}, u32[]{:S(2)}) %collective-permute-start.3) | collective-permute-done | bytes 393248 | tf_op jit(solution)/shard_map/ppermute | solution.py:1131
  119.3 15.5 %forward_remote.1 = (bf16[8,2,128,192]{3,2,1,0:T(8,128)(2,1)}, f32[8,3,1,256]{3,2,1,0:T(1,128)}, f32[8,3,64,256]{3,2,1,0:T(8,128)}) custom-call(s32[9]{0:T(128)} %pad_add_fusion.scalars_ref, s32[4,1,256]{2,1,0:T(1,128)} %bitcast.124, bf16[8,2,128,640]{3,2,1,0:T(8,128)(2,1)} %bitcast.96, bf16[1,8,128,384]{3,2,1,0:T(8,128)(2,1)} %bitcast.115, ...), custom_call_target="tpu_custom_call" | custom-call | tf_op jit(solution)/shard_map/forward_remote/pallas_call | solution.py:708
  137.0 7.1 %all-to-all-start.1 = ((bf16[8,256,192]{1,2,0:T(8,128)(2,1)}), bf16[8,256,192]{1,2,0:T(8,128)(2,1)S(1)}, u32[]{:S(2)}, u32[]{:S(2)}) async-start(bf16[8,256,192]{1,2,0:T(8,128)(2,1)} %copy.56), calls=%async_computation.1 | async-start | bytes 1572864 | tf_op jit(solution)/shard_map/all_to_all | solution.py:1082
  147.2 8.0 %all-to-all-done.1 = bf16[8,256,192]{1,2,0:T(8,128)(2,1)S(1)} async-done(((bf16[8,256,192]{1,2,0:T(8,128)(2,1)}), bf16[8,256,192]{1,2,0:T(8,128)(2,1)S(1)}, u32[]{:S(2)}, u32[]{:S(2)}) %all-to-all-start.1) | async-done | bytes 786464 | tf_op jit(solution)/shard_map/all_to_all | solution.py:1082
  156.4 30.4 %feed.1 = (bf16[512,768]{1,0:T(8,128)(2,1)}, f32[512,768]{1,0:T(8,128)}, bf16[8,256,192]{2,1,0:T(8,128)(2,1)}, bf16[5,384,768]{2,1,0:T(8,128)(2,1)}, bf16[5,384,...) custom-call(s32[1]{0:T(128)} %bitcast.at_ref, ...), custom_call_target="tpu_custom_call" | custom-call | tf_op jit(solution)/shard_map/feed/pallas_call | solution.py:343
  189.6 4.1 all-to-all-start.2
  193.8 12.1 %all-to-all-done.2 = bf16[8,256,192]{1,2,0:T(8,128)(2,1)S(1)} async-done(((bf16[8,256,192]{1,2,0:T(8,128)(2,1)}), bf16[8,256,192]{1,2,0:T(8,128)(2,1)S(1)}, u32[]{:S(2)}, u32[]{:S(2)}) %all-to-all-start.2) | async-done | bytes 786464 | tf_op jit(solution)/shard_map/all_to_all | solution.py:1082
  209.7 3.4 add_convert_fusion
  217.5 20.3 %backward_remote.1 = (bf16[1,8,128,384]{3,2,1,0:T(8,128)(2,1)}, bf16[4,128,384]{2,1,0:T(8,128)(2,1)}, f32[8,3,64,256]{3,2,1,0:T(8,128)}, f32[8,3,1,256]{3,2,1,0:T(1,128)}) custom-call(s32[9]{0:T(128)} %pad_add_fusion.scalars_ref, s32[4,1,256]{2,1,0:T(1,128)} %bitcast.125, bf16[8,2,128,640]{3,2,1,0:T(8,128)(2,1)} %bitcast.97, ...), custom_call_target="tpu_custom_call" | custom-call | tf_op jit(solution)/shard_map/backward_remote/pallas_call | solution.py:923
  237.8 6.1 %collective-permute-done.7 = bf16[768,768]{1,0:T(8,128)(2,1)} collective-permute-done((bf16[768,768]{1,0:T(8,128)(2,1)}, bf16[768,768]{1,0:T(8,128)(2,1)}, u32[]{:S(2)}, u32[]{:S(2)}) %collective-permute-start.7) | collective-permute-done | bytes 1179680 | tf_op jit(solution)/shard_map/ppermute | solution.py:990
  252.2 7.4 %collective-permute-start.10 = (bf16[8,128,384]{2,1,0:T(8,128)(2,1)}, bf16[8,128,384]{2,1,0:T(8,128)(2,1)S(1)}, u32[]{:S(2)}, u32[]{:S(2)}) collective-permute-start(bf16[8,128,384]{2,1,0:T(8,128)(2,1)} %bitcast.26), channel_id=1, source_target_pairs={{0,16},{2,18},{4,20},{6,22},{8,24},{10,26},{12,28},{14,30},{16,0},... | collective-permute-start | bytes 2359304 | tf_op jit(solution)/shard_map/ppermute | solution.py:1127
  261.7 30.9 %backward_local.1.packed_ref = bf16[8,2,128,640]{3,2,1,0:T(8,128)(2,1)} custom-call(s32[9]{0:T(128)} %pad_add_fusion.scalars_ref, s32[4,1,256]{2,1,0:T(1,128)} %bitcast.126, bf16[8,2,128,640]{3,2,1,0:T(8,128)(2,1)} %bitcast.98, bf16[8,2,128,192]{3,2,1,0:T(8,128)(2,1)} %bitcast.108, f32[8,3,1,256]{3,2,1,0:T(1,128)} %get-tuple-element.67.log_ref, ...), custom_call_target="tpu_custom_call" | custom-call | tf_op jit(solution)/shard_map/backward_local/pallas_call | solution.py:952
  296.1 10.6 %unproject.1 = (bf16[8,256,768]{2,1,0:T(8,128)(2,1)}, bf16[384,768]{1,0:T(8,128)(2,1)}, bf16[384,768]{1,0:T(8,128)(2,1)}, f32[1,640]{1,0:T(1,128)}, f32[768,1]{1,0:T(8,128)}, /*index=5*/f32[768,1]{1,0:T(8,128)}) custom-call(s32[1]{0:T(128)} %bitcast.at_ref, s32[1]{0:T(128)} %constant.120.clone.1.halo_ref, bf16[8,256,768]{2,1,0:T(8,128)(2,1)} %all-to-all-done.low_ref, ...), custom_call_target="tpu_custom_call" | custom-call | tf_op jit(solution)/shard_map/unproject/pallas_call | solution.py:177
  319.3 16.2 %collective-permute-start.15 = (f32[80,128]{1,0:T(8,128)S(1)}, f32[80,128]{1,0:T(8,128)S(1)}, u32[]{:S(2)}, u32[]{:S(2)}) collective-permute-start(f32[80,128]{1,0:T(8,128)S(1)} %add.215), channel_id=1, source_target_pairs={{0,8},{2,10},{4,12},{6,14},{8,0},{10,2},{12,4},{14,6},{16,24},{18,... | collective-permute-start | bytes 122888 | tf_op jit(solution)/shard_map/ppermute | solution.py:990
  343.7 3.9 all-to-all-start.3
  354.8 7.3 %collective-permute-start.25 = (bf16[120,768]{1,0:T(8,128)(2,1)S(1)}, bf16[120,768]{1,0:T(8,128)(2,1)S(1)}, u32[]{:S(2)}, u32[]{:S(2)}) collective-permute-start(bf16[120,768]{1,0:T(8,128)(2,1)S(1)} %constant_dynamic-slice_fusion.2), channel_id=1, source_target_pairs={{0,16},{2,18},{4,20},{6,22},{8,24},{10,26},{12,28},{14,30},{16,0},... | collective-permute-start | bytes 552968 | tf_op jit(solution)/shard_map/ppermute | solution.py:990
  362.1 26.2 %collective-permute-done.31 = bf16[96,768]{1,0:T(8,128)(2,1)S(1)} collective-permute-done((bf16[96,768]{1,0:T(8,128)(2,1)S(1)}, bf16[96,768]{1,0:T(8,128)(2,1)S(1)}, u32[]{:S(2)}, u32[]{:S(2)}) %collective-permute-start.31) | collective-permute-done | bytes 147488 | tf_op jit(solution)/shard_map/ppermute | solution.py:990
  388.3 3.4 collective-permute-start.32
  392.3 3.5 collective-permute-start.26
  397.2 16.3 %collective-permute-done.32 = bf16[96,768]{1,0:T(8,128)(2,1)S(1)} collective-permute-done((bf16[96,768]{1,0:T(8,128)(2,1)S(1)}, bf16[96,768]{1,0:T(8,128)(2,1)S(1)}, u32[]{:S(2)}, u32[]{:S(2)}) %collective-permute-start.32) | collective-permute-done | bytes 147488 | tf_op jit(solution)/shard_map/ppermute | solution.py:990
  413.7 8.6 %collective-permute-done.18 = bf16[192,768]{1,0:T(8,128)(2,1)S(1)} collective-permute-done((bf16[192,768]{1,0:T(8,128)(2,1)S(1)}, bf16[192,768]{1,0:T(8,128)(2,1)S(1)}, u32[]{:S(2)}, u32[]{:S(2)}) %collective-permute-start.18) | collective-permute-done | bytes 294944 | tf_op jit(solution)/shard_map/ppermute | solution.py:990
  422.4 3.8 collective-permute-start.19
  426.4 3.8 collective-permute-done.19
  432.6 5.0 collective-permute-done.20
  441.6 6.0 %collective-permute-done.21 = bf16[2,96,768]{2,1,0:T(8,128)(2,1)S(1)} collective-permute-done((bf16[2,96,768]{2,1,0:T(8,128)(2,1)S(1)}, bf16[2,96,768]{2,1,0:T(8,128)(2,1)S(1)}, u32[]{:S(2)}, u32[]{:S(2)}) %collective-permute-start.21) | collective-permute-done | bytes 294944 | tf_op jit(solution)/shard_map/ppermute | solution.py:990
  452.9 7.5 %collective-permute-done.22 = bf16[4,96,768]{2,1,0:T(8,128)(2,1)} collective-permute-done((bf16[4,96,768]{2,1,0:T(8,128)(2,1)}, bf16[4,96,768]{2,1,0:T(8,128)(2,1)}, u32[]{:S(2)}, u32[]{:S(2)}) %collective-permute-start.22) | collective-permute-done | bytes 589856 | tf_op jit(solution)/shard_map/ppermute | solution.py:990
  463.7 3.5 collective-permute-start.23
  482.1 4.7 collective-permute-done.35
  (331 shorter events, 147.6 us)
Async XLA Ops:
  7.3 149.1 %all-gather.4.cloned.1.call-start = ((), (), s32[]{:S(2)}) async-start(), calls=%async_computation.4 | async-start | bytes 1769472 | tf_op jit(solution)/shard_map/all_gather | solution.py:1073
  8.0 148.4 %all-gather.6.cloned.1.call-start = ((), (), s32[]{:S(2)}) async-start(), calls=%async_computation.5 | async-start | bytes 7077888 | tf_op jit(solution)/shard_map/all_gather | solution.py:1074
  13.1 44.0 %all-to-all-start = ((bf16[8,256,768]{2,1,0:T(8,128)(2,1)}), bf16[8,256,768]{2,1,0:T(8,128)(2,1)}, u32[]{:S(2)}, u32[]{:S(2)}) async-start(bf16[8,256,768]{2,1,0:T(8,128)(2,1)} %bitcast.103), calls=%async_computation | async-start | bytes 6291456 | tf_op jit(solution)/shard_map/all_to_all | solution.py:1082
  18.8 137.6 %all-gather.8.cloned.1.call-start = ((), (), s32[]{:S(2)}) async-start(), calls=%async_computation.6 | async-start | bytes 7077888 | tf_op jit(solution)/shard_map/all_gather | solution.py:1075
  64.5 53.8 %collective-permute-start.2 = (bf16[8,128,384]{2,1,0:T(8,128)(2,1)S(1)}, bf16[8,128,384]{2,1,0:T(8,128)(2,1)S(1)}, u32[]{:S(2)}, u32[]{:S(2)}) collective-permute-start(bf16[8,128,384]{2,1,0:T(8,128)(2,1)S(1)} %slice_bitcast_fusion), channel_id=1, source_target_pairs={{0,16},{2,18},{4,20},{6,22},{8,24},{10,26},{12,28},{14,30},{16,0},... | collective-permute-start | bytes 2359304 | tf_op jit(solution)/shard_map/ppermute | solution.py:1127
  68.4 49.9 %collective-permute-start.3 = (bf16[4,128,384]{2,1,0:T(8,128)(2,1)S(1)}, bf16[4,128,384]{2,1,0:T(8,128)(2,1)S(1)}, u32[]{:S(2)}, u32[]{:S(2)}) collective-permute-start(bf16[4,128,384]{2,1,0:T(8,128)(2,1)S(1)} %slice_bitcast_fusion.1), channel_id=1, source_target_pairs={{16,0},{18,2},{20,4},{22,6},{24,8},{26,10},{28,12},{30,14},{17,1},... | collective-permute-start | bytes 1179656 | tf_op jit(solution)/shard_map/ppermute | solution.py:1131
  137.0 18.1 %all-to-all-start.1 = ((bf16[8,256,192]{1,2,0:T(8,128)(2,1)}), bf16[8,256,192]{1,2,0:T(8,128)(2,1)S(1)}, u32[]{:S(2)}, u32[]{:S(2)}) async-start(bf16[8,256,192]{1,2,0:T(8,128)(2,1)} %copy.56), calls=%async_computation.1 | async-start | bytes 1572864 | tf_op jit(solution)/shard_map/all_to_all | solution.py:1082
  186.8 20.4 %collective-permute-start.5 = (bf16[1536,768]{1,0:T(8,128)(2,1)}, bf16[1536,768]{1,0:T(8,128)(2,1)}, u32[]{:S(2)}, u32[]{:S(2)}) collective-permute-start(bf16[1536,768]{1,0:T(8,128)(2,1)} %bitcast.140), channel_id=1, source_target_pairs={{0,1},{1,0},{2,3},{3,2},{4,5},{5,4},{6,7},{7,6},{8,9},{9,8},{10,11... | collective-permute-start | bytes 7077896 | tf_op jit(solution)/shard_map/ppermute | solution.py:982
  186.9 22.7 %collective-permute-start.4 = (bf16[5,384,768]{2,1,0:T(8,128)(2,1)}, bf16[5,384,768]{2,1,0:T(8,128)(2,1)}, u32[]{:S(2)}, u32[]{:S(2)}) collective-permute-start(bf16[5,384,768]{2,1,0:T(8,128)(2,1)} %get-tuple-element.60), channel_id=1, source_target_pairs={{0,1},{1,0},{2,3},{3,2},{4,5},{5,4},{6,7},{7,6},{8,9},{9,8},{10,11... | collective-permute-start | bytes 8847368 | tf_op jit(solution)/shard_map/ppermute | solution.py:982
  189.6 16.3 %all-to-all-start.2 = ((bf16[8,256,192]{1,2,0:T(8,128)(2,1)}), bf16[8,256,192]{1,2,0:T(8,128)(2,1)S(1)}, u32[]{:S(2)}, u32[]{:S(2)}) async-start(bf16[8,256,192]{1,2,0:T(8,128)(2,1)} %copy.58), calls=%async_computation.2 | async-start | bytes 1572864 | tf_op jit(solution)/shard_map/all_to_all | solution.py:1082
  214.4 33.3 %collective-permute-start.6 = (bf16[960,768]{1,0:T(8,128)(2,1)}, bf16[960,768]{1,0:T(8,128)(2,1)}, u32[]{:S(2)}, u32[]{:S(2)}) collective-permute-start(bf16[960,768]{1,0:T(8,128)(2,1)} %constant_dynamic-slice_fusion.9), channel_id=1, source_target_pairs={{0,2},{2,0},{4,6},{6,4},{8,10},{10,8},{12,14},{14,12},{16,18},{18,... | collective-permute-start | bytes 4423688 | tf_op jit(solution)/shard_map/ppermute | solution.py:990
  216.0 27.9 %collective-permute-start.7 = (bf16[768,768]{1,0:T(8,128)(2,1)}, bf16[768,768]{1,0:T(8,128)(2,1)}, u32[]{:S(2)}, u32[]{:S(2)}) collective-permute-start(bf16[768,768]{1,0:T(8,128)(2,1)} %constant_dynamic-slice_fusion.8), channel_id=1, source_target_pairs={{0,4},{2,6},{4,0},{6,2},{8,12},{10,14},{12,8},{14,10},{16,20},{18,... | collective-permute-start | bytes 3538952 | tf_op jit(solution)/shard_map/ppermute | solution.py:990
  249.5 43.1 %collective-permute-start.9 = (bf16[384,768]{1,0:T(8,128)(2,1)S(1)}, bf16[384,768]{1,0:T(8,128)(2,1)S(1)}, u32[]{:S(2)}, u32[]{:S(2)}) collective-permute-start(bf16[384,768]{1,0:T(8,128)(2,1)S(1)} %constant_dynamic-slice_fusion.6), channel_id=1, source_target_pairs={{0,2},{2,0},{4,6},{6,4},{8,10},{10,8},{12,14},{14,12},{16,18},{18,... | collective-permute-start | bytes 1769480 | tf_op jit(solution)/shard_map/ppermute | solution.py:990
  251.4 41.5 %collective-permute-start.8 = (bf16[480,768]{1,0:T(8,128)(2,1)S(1)}, bf16[480,768]{1,0:T(8,128)(2,1)S(1)}, u32[]{:S(2)}, u32[]{:S(2)}) collective-permute-start(bf16[480,768]{1,0:T(8,128)(2,1)S(1)} %constant_dynamic-slice_fusion.7), channel_id=1, source_target_pairs={{0,4},{2,6},{4,0},{6,2},{8,12},{10,14},{12,8},{14,10},{16,20},{18,... | collective-permute-start | bytes 2211848 | tf_op jit(solution)/shard_map/ppermute | solution.py:990
  252.2 42.3 %collective-permute-start.10 = (bf16[8,128,384]{2,1,0:T(8,128)(2,1)}, bf16[8,128,384]{2,1,0:T(8,128)(2,1)S(1)}, u32[]{:S(2)}, u32[]{:S(2)}) collective-permute-start(bf16[8,128,384]{2,1,0:T(8,128)(2,1)} %bitcast.26), channel_id=1, source_target_pairs={{0,16},{2,18},{4,20},{6,22},{8,24},{10,26},{12,28},{14,30},{16,0},... | collective-permute-start | bytes 2359304 | tf_op jit(solution)/shard_map/ppermute | solution.py:1127
  259.6 34.8 %collective-permute-start.11 = (bf16[4,128,384]{2,1,0:T(8,128)(2,1)}, bf16[4,128,384]{2,1,0:T(8,128)(2,1)S(1)}, u32[]{:S(2)}, u32[]{:S(2)}) collective-permute-start(bf16[4,128,384]{2,1,0:T(8,128)(2,1)} %get-tuple-element.78), channel_id=1, source_target_pairs={{0,16},{2,18},{4,20},{6,22},{8,24},{10,26},{12,28},{14,30},{1,17},... | collective-permute-start | bytes 1179656 | tf_op jit(solution)/shard_map/ppermute | solution.py:1135
  319.3 18.6 %collective-permute-start.15 = (f32[80,128]{1,0:T(8,128)S(1)}, f32[80,128]{1,0:T(8,128)S(1)}, u32[]{:S(2)}, u32[]{:S(2)}) collective-permute-start(f32[80,128]{1,0:T(8,128)S(1)} %add.215), channel_id=1, source_target_pairs={{0,8},{2,10},{4,12},{6,14},{8,0},{10,2},{12,4},{14,6},{16,24},{18,... | collective-permute-start | bytes 122888 | tf_op jit(solution)/shard_map/ppermute | solution.py:990
  336.2 12.9 %collective-permute-start.30 = (bf16[192,768]{1,0:T(8,128)(2,1)}, bf16[192,768]{1,0:T(8,128)(2,1)}, u32[]{:S(2)}, u32[]{:S(2)}) collective-permute-start(bf16[192,768]{1,0:T(8,128)(2,1)} %constant_dynamic-slice_fusion.1), channel_id=1, source_target_pairs={{0,8},{2,10},{4,12},{6,14},{8,0},{10,2},{12,4},{14,6},{16,24},{18,... | collective-permute-start | bytes 884744 | tf_op jit(solution)/shard_map/ppermute | solution.py:990
  343.7 52.1 %collective-permute-start.17 = (bf16[384,768]{1,0:T(8,128)(2,1)}, bf16[384,768]{1,0:T(8,128)(2,1)}, u32[]{:S(2)}, u32[]{:S(2)}) collective-permute-start(bf16[384,768]{1,0:T(8,128)(2,1)} %get-tuple-element.86), channel_id=1, source_target_pairs={{0,1},{1,0},{2,3},{3,2},{4,5},{5,4},{6,7},{7,6},{8,9},{9,8},{10,11... | collective-permute-start | bytes 1769480 | tf_op jit(solution)/shard_map/ppermute | solution.py:982
  343.7 177.0 %all-to-all-start.3 = ((bf16[8,256,768]{2,1,0:T(8,128)(2,1)}), bf16[8,256,768]{2,1,0:T(8,128)(2,1)S(1)}, u32[]{:S(2)}, u32[]{:S(2)}) async-start(bf16[8,256,768]{2,1,0:T(8,128)(2,1)} %get-tuple-element.79), calls=%async_computation.3 | async-start | bytes 6291456 | tf_op jit(solution)/shard_map/all_to_all | solution.py:1082
  350.2 38.1 %collective-permute-start.31 = (bf16[96,768]{1,0:T(8,128)(2,1)S(1)}, bf16[96,768]{1,0:T(8,128)(2,1)S(1)}, u32[]{:S(2)}, u32[]{:S(2)}) collective-permute-start(bf16[96,768]{1,0:T(8,128)(2,1)S(1)} %constant_dynamic-slice_fusion), channel_id=1, source_target_pairs={{0,16},{2,18},{4,20},{6,22},{8,24},{10,26},{12,28},{14,30},{16,0},... | collective-permute-start | bytes 442376 | tf_op jit(solution)/shard_map/ppermute | solution.py:990
  354.8 37.4 %collective-permute-start.25 = (bf16[120,768]{1,0:T(8,128)(2,1)S(1)}, bf16[120,768]{1,0:T(8,128)(2,1)S(1)}, u32[]{:S(2)}, u32[]{:S(2)}) collective-permute-start(bf16[120,768]{1,0:T(8,128)(2,1)S(1)} %constant_dynamic-slice_fusion.2), channel_id=1, source_target_pairs={{0,16},{2,18},{4,20},{6,22},{8,24},{10,26},{12,28},{14,30},{16,0},... | collective-permute-start | bytes 552968 | tf_op jit(solution)/shard_map/ppermute | solution.py:990
  388.3 25.2 %collective-permute-start.32 = (bf16[96,768]{1,0:T(8,128)(2,1)S(1)}, bf16[96,768]{1,0:T(8,128)(2,1)S(1)}, u32[]{:S(2)}, u32[]{:S(2)}) collective-permute-start(bf16[96,768]{1,0:T(8,128)(2,1)S(1)} %add_convert_fusion.10), channel_id=1, source_target_pairs={{0,16},{2,18},{4,20},{6,22},{8,24},{10,26},{12,28},{14,30},{16,0},... | collective-permute-start | bytes 442376 | tf_op jit(solution)/shard_map/ppermute | solution.py:990
  392.3 33.9 %collective-permute-start.26 = (bf16[120,768]{1,0:T(8,128)(2,1)S(1)}, bf16[120,768]{1,0:T(8,128)(2,1)S(1)}, u32[]{:S(2)}, u32[]{:S(2)}) collective-permute-start(bf16[120,768]{1,0:T(8,128)(2,1)S(1)} %add_convert_fusion.9), channel_id=1, source_target_pairs={{0,16},{2,18},{4,20},{6,22},{8,24},{10,26},{12,28},{14,30},{16,0},... | collective-permute-start | bytes 552968 | tf_op jit(solution)/shard_map/ppermute | solution.py:990
  397.1 25.2 %collective-permute-start.18 = (bf16[192,768]{1,0:T(8,128)(2,1)S(1)}, bf16[192,768]{1,0:T(8,128)(2,1)S(1)}, u32[]{:S(2)}, u32[]{:S(2)}) collective-permute-start(bf16[192,768]{1,0:T(8,128)(2,1)S(1)} %constant_dynamic-slice_fusion.5), channel_id=1, source_target_pairs={{0,16},{2,18},{4,20},{6,22},{8,24},{10,26},{12,28},{14,30},{16,0},... | collective-permute-start | bytes 884744 | tf_op jit(solution)/shard_map/ppermute | solution.py:990
  413.6 16.7 %collective-permute-start.33 = (bf16[192,768]{1,0:T(8,128)(2,1)S(1)}, bf16[192,768]{1,0:T(8,128)(2,1)S(1)}, u32[]{:S(2)}, u32[]{:S(2)}) collective-permute-start(bf16[192,768]{1,0:T(8,128)(2,1)S(1)} %pad_maximum_fusion.10), channel_id=1, source_target_pairs={{0,8},{2,10},{4,12},{6,14},{8,0},{10,2},{12,4},{14,6},{16,24},{18,... | collective-permute-start | bytes 884744 | tf_op jit(solution)/shard_map/ppermute | solution.py:990
  426.3 13.4 %collective-permute-start.27 = (bf16[240,768]{1,0:T(8,128)(2,1)S(1)}, bf16[240,768]{1,0:T(8,128)(2,1)S(1)}, u32[]{:S(2)}, u32[]{:S(2)}) collective-permute-start(bf16[240,768]{1,0:T(8,128)(2,1)S(1)} %pad_maximum_fusion.8), channel_id=1, source_target_pairs={{0,8},{2,10},{4,12},{6,14},{8,0},{10,2},{12,4},{14,6},{16,24},{18,... | collective-permute-start | bytes 1105928 | tf_op jit(solution)/shard_map/ppermute | solution.py:990
  430.5 19.7 %collective-permute-start.34 = (bf16[384,768]{1,0:T(8,128)(2,1)S(1)}, bf16[384,768]{1,0:T(8,128)(2,1)S(1)}, u32[]{:S(2)}, u32[]{:S(2)}) collective-permute-start(bf16[384,768]{1,0:T(8,128)(2,1)S(1)} %pad_maximum_fusion.7), channel_id=1, source_target_pairs={{0,2},{2,0},{4,6},{6,4},{8,10},{10,8},{12,14},{14,12},{16,18},{18,... | collective-permute-start | bytes 1769480 | tf_op jit(solution)/shard_map/ppermute | solution.py:990
  440.8 35.2 %collective-permute-start.28 = (bf16[480,768]{1,0:T(8,128)(2,1)}, bf16[480,768]{1,0:T(8,128)(2,1)}, u32[]{:S(2)}, u32[]{:S(2)}) collective-permute-start(bf16[480,768]{1,0:T(8,128)(2,1)} %pad_maximum_fusion.5), channel_id=1, source_target_pairs={{0,4},{2,6},{4,0},{6,2},{8,12},{10,14},{12,8},{14,10},{16,20},{18,... | collective-permute-start | bytes 2211848 | tf_op jit(solution)/shard_map/ppermute | solution.py:990
  452.3 34.5 %collective-permute-start.35 = (bf16[768,768]{1,0:T(8,128)(2,1)}, bf16[768,768]{1,0:T(8,128)(2,1)}, u32[]{:S(2)}, u32[]{:S(2)}) collective-permute-start(bf16[768,768]{1,0:T(8,128)(2,1)} %pad_maximum_fusion.4), channel_id=1, source_target_pairs={{0,4},{2,6},{4,0},{6,2},{8,12},{10,14},{12,8},{14,10},{16,20},{18,... | collective-permute-start | bytes 3538952 | tf_op jit(solution)/shard_map/ppermute | solution.py:990
  463.7 27.5 %collective-permute-start.23 = (bf16[8,96,768]{2,1,0:T(8,128)(2,1)}, bf16[8,96,768]{2,1,0:T(8,128)(2,1)}, u32[]{:S(2)}, u32[]{:S(2)}) collective-permute-start(bf16[8,96,768]{2,1,0:T(8,128)(2,1)} %pad_maximum_fusion.3), channel_id=1, source_target_pairs={{0,8},{2,10},{4,12},{6,14},{8,0},{10,2},{12,4},{14,6},{16,24},{18,... | collective-permute-start | bytes 3538952 | tf_op jit(solution)/shard_map/ppermute | solution.py:990
  481.2 30.9 %collective-permute-start.29 = (bf16[960,768]{1,0:T(8,128)(2,1)}, bf16[960,768]{1,0:T(8,128)(2,1)}, u32[]{:S(2)}, u32[]{:S(2)}) collective-permute-start(bf16[960,768]{1,0:T(8,128)(2,1)} %pad_maximum_fusion.2), channel_id=1, source_target_pairs={{0,2},{2,0},{4,6},{6,4},{8,10},{10,8},{12,14},{14,12},{16,18},{18,... | collective-permute-start | bytes 4423688 | tf_op jit(solution)/shard_map/ppermute | solution.py:990
  (68 other events, 865.5 us)
Sparse Core Ops, SparseCore 0:
  9.7 11.9 all-gather.3
  23.2 15.6 all-gather.5
  40.4 15.5 all-gather.7
